TPU v7x, 128 devices: a whole 4x4x4 slice. The times are simulated.
128 devices in a mesh: gx: 8 (over x_lo, y), gy: 16 (over z, x_hi, core).
Axes of the slice: x: 4 (x_hi: 2, x_lo: 2; x = x_hi * 2 + x_lo), y: 4, z: 4, core: 2. Of those that a mesh axis runs over, the one named last changes fastest.
Arguments:
- voxel_feats: bfloat16 [512, 64, 128], P(('gx', 'gy')), may hold values from -6 to 6
- w_first: bfloat16 [27, 128, 128], replicated, may hold values from -0.109375 to 0.109375
- w_second: bfloat16 [27, 128, 128], replicated, may hold values from -0.109375 to 0.109375
- norm_gain: float32 [2, 128], replicated, may hold values from 0.5 to 1.5
- norm_shift: float32 [2, 128], replicated, may hold values from -3 to 3
- grad_out: bfloat16 [512, 64, 128], P(('gx', 'gy')), may hold values from -6 to 6
- brick_count: int32 [128], P(('gx', 'gy')), may hold values from 1 to 4, as said below
- kernel_map: int32 [512, 27], P(('gx', 'gy')), may hold values from 0 to 12, as said below
- face_send: int32 [128, 4, 1], P(('gx', 'gy')), may hold values from 0 to 3, as said below
- corner_send: int32 [128, 4, 1], P(('gx', 'gy')), may hold values from 0 to 3, as said below
Outputs:
- out_feats: bfloat16 [512, 64, 128], P(('gx', 'gy'))
- grad_in: bfloat16 [512, 64, 128], P(('gx', 'gy'))
- weight_grads: float32 [2, 27, 128, 128], replicated
- norm_grads: float32 [4, 128], replicated
Inputs may be any that keep to these rules, and one draw needn't show every extreme that they name: `brick_count`: some tile is full in every draw. `kernel_map`: direction 13 names the brick itself; index 12 is the zero brick. `face_send`: list k names bricks of the tile below its brick_count, sent to its +x, -x, +y, -y neighbour for k = 0, 1, 2, 3. `corner_send`: list k names bricks of the tile below its brick_count, sent to its (+x, +y), (+x, -y), (-x, +y), (-x, -y) neighbour for k = 0, 1, 2, 3.
All inputs are finite; a program needn't handle non-finite values.
Results may differ from a plain program's by a relative error of at most 0.006.
Values may be sent and summed in bfloat16 or wider, within the bound.
No kernel may reach another device: no remote copies, remote signals or barrier semaphores. Data moves between devices by JAX's collectives and lax.ppermute only.
A program may use at most 128 MiB of HBM per device.

v0:
```python
import jax
import jax.numpy as jnp
from jax import lax
from jax.sharding import Mesh
from jax.sharding import PartitionSpec as P

GX = ("gx_0", "gx_1")
GY = ("gy_0", "gy_1", "gy_2")
GX_GY = ("gx_0", "gx_1", "gy_0", "gy_1", "gy_2")


TAP_LIST = [(a, b, c) for a in range(3) for b in range(3) for c in range(3)]
epsilon = 1e-05


def shifted(value, axis, by):
    length = lax.axis_size(axis)
    pairs = [(i, i + by) for i in range(length) if 0 <= i + by < length]
    return lax.ppermute(value, axis, pairs)


def by_axis(value, axes):
    for axis in axes:
        value = lax.psum(value, axis)
    return value


def in_one(arrays, axis):
    ravelled, at, gathered = (jnp.concatenate([a.reshape(-1) for a in arrays]), 0, [])
    subtotal = lax.psum(ravelled, axis)
    for a in arrays:
        gathered.append(subtotal[at : at + a.size].reshape(a.shape))
        at += a.size
    return tuple(gathered)


def silu_slope(values):
    sigma = jax.nn.sigmoid(values)
    return sigma * (1.0 + values * (1.0 - sigma))


def source_range(e):
    if e < 0:
        return (slice(3, 4), slice(0, 1))
    if e == 0:
        return (slice(0, 4), slice(1, 5))
    return (slice(0, 1), slice(5, 6))


def assemble(extended, tile_table):
    planes = []
    for a in (-1, 0, 1):
        layers = []
        for b in (-1, 0, 1):
            pieces = []
            for c in (-1, 0, 1):
                d = 9 * (a + 1) + 3 * (b + 1) + (c + 1)
                region = extended[:, source_range(a)[0], source_range(b)[0], source_range(c)[0]]
                pieces.append(jnp.take(region, tile_table[:, d], axis=0))
            layers.append(jnp.concatenate(pieces, axis=3))
        planes.append(jnp.concatenate(layers, axis=2))
    return jnp.concatenate(planes, axis=1)


def patches(padded):
    bricks = padded.shape[0]
    channels = padded.shape[-1]
    return jnp.concatenate(
        [
            padded[:, a : a + 4, b : b + 4, c : c + 4].reshape(bricks * 64, channels)
            for a, b, c in TAP_LIST
        ],
        axis=1,
    )


def spread(columns, bricks, channels):
    padded = jnp.zeros((bricks, 6, 6, 6, channels), jnp.float32)
    for k, (a, b, c) in enumerate(TAP_LIST):
        piece = columns[:, k * channels : (k + 1) * channels].reshape(bricks, 4, 4, 4, channels)
        padded = padded.at[:, a : a + 4, b : b + 4, c : c + 4].add(piece)
    return padded


def scatter_bricks(padded, tile_table, total):
    result = jnp.zeros((total, 4, 4, 4, padded.shape[-1]), jnp.float32)
    for a in (-1, 0, 1):
        for b in (-1, 0, 1):
            for c in (-1, 0, 1):
                d = 9 * (a + 1) + 3 * (b + 1) + (c + 1)
                range_a = source_range(a)
                range_b = source_range(b)
                range_c = source_range(c)
                result = result.at[tile_table[:, d], range_a[0], range_b[0], range_c[0]].add(
                    padded[:, range_a[1], range_b[1], range_c[1]]
                )
    return result


def section_x(values, steps):
    return shifted(values, GX, steps)


def section_y(values, steps):
    return shifted(values, GY, steps)


def return_x(values, steps):
    return shifted(values.astype(jnp.bfloat16), GX, steps).astype(values.dtype)


def return_y(values, steps):
    return shifted(values.astype(jnp.bfloat16), GY, steps).astype(values.dtype)


def extend(field, face_list, corner_list):
    side = face_list.shape[1]
    small = corner_list.shape[1]
    faces = [jnp.take(field, face_list[k], axis=0) for k in range(4)]
    corners = [jnp.take(field, corner_list[k], axis=0) for k in range(4)]
    upper_x = section_x(jnp.concatenate([faces[0], corners[0], corners[1]], axis=0), 1)
    lower_x = section_x(jnp.concatenate([faces[1], corners[2], corners[3]], axis=0), -1)
    upper_y = section_y(
        jnp.concatenate(
            [faces[2], upper_x[side : side + small], lower_x[side : side + small]], axis=0
        ),
        1,
    )
    lower_y = section_y(
        jnp.concatenate([faces[3], upper_x[side + small :], lower_x[side + small :]], axis=0), -1
    )
    got_faces = [upper_x[:side], lower_x[:side], upper_y[:side], lower_y[:side]]
    got_corners = [
        upper_y[side : side + small],
        lower_y[side : side + small],
        upper_y[side + small :],
        lower_y[side + small :],
    ]
    zero_brick = jnp.zeros((1,) + field.shape[1:], field.dtype)
    return jnp.concatenate([field] + got_faces + got_corners + [zero_brick], axis=0)


def return_home(ext_grads, face_list, corner_list, bricks):
    side = face_list.shape[1]
    small = corner_list.shape[1]
    start = bricks + 4 * side
    grad_faces = [ext_grads[bricks + k * side : bricks + (k + 1) * side] for k in range(4)]
    grad_corners = [ext_grads[start + k * small : start + (k + 1) * small] for k in range(4)]
    lower_y = return_y(
        jnp.concatenate([grad_faces[2], grad_corners[0], grad_corners[2]], axis=0), -1
    )
    upper_y = return_y(
        jnp.concatenate([grad_faces[3], grad_corners[1], grad_corners[3]], axis=0), 1
    )
    lower_x = return_x(
        jnp.concatenate(
            [grad_faces[0], lower_y[side : side + small], upper_y[side : side + small]], axis=0
        ),
        -1,
    )
    upper_x = return_x(
        jnp.concatenate([grad_faces[1], lower_y[side + small :], upper_y[side + small :]], axis=0),
        1,
    )
    home_faces = [lower_x[:side], upper_x[:side], lower_y[:side], upper_y[:side]]
    home_corners = [
        lower_x[side : side + small],
        lower_x[side + small :],
        upper_x[side : side + small],
        upper_x[side + small :],
    ]
    result = ext_grads[:bricks]
    for k in range(4):
        result = result.at[face_list[k]].add(home_faces[k])
        result = result.at[corner_list[k]].add(home_corners[k])
    return result


def moments(values, occupied, weighted):
    return (
        by_axis(weighted, GX_GY),
        by_axis(jnp.sum(values * occupied, axis=0), GX_GY),
        by_axis(jnp.sum(values * values * occupied, axis=0), GX_GY),
    )


def normalize(values, totals):
    center = totals[1] / totals[0]
    spread_sq = totals[2] / totals[0] - center * center
    recip = lax.rsqrt(spread_sq + epsilon)
    return ((values - center) * recip, recip)


def conv_back(columns, grads, flat, kernel_map, face_list, corner_list, bricks, channels, total):
    partial_w = lax.dot_general(
        columns, grads, (((0,), (0,)), ((), ())), preferred_element_type=jnp.float32
    )
    spread_cols = lax.dot_general(
        grads, flat, (((1,), (1,)), ((), ())), preferred_element_type=jnp.float32
    )
    ext_grads = scatter_bricks(spread(spread_cols, bricks, channels), kernel_map, total)
    homed = return_home(ext_grads, face_list, corner_list, bricks)
    return (partial_w, homed.reshape(bricks * 64, channels))


def body(
    voxel_feats,
    w_first,
    w_second,
    norm_gain,
    norm_shift,
    grad_out,
    brick_count,
    kernel_map,
    face_send,
    corner_send,
):
    bricks = voxel_feats.shape[0]
    channels = voxel_feats.shape[2]
    face_list = face_send[0]
    corner_list = corner_send[0]
    total = bricks + 4 * face_list.shape[1] + 4 * corner_list.shape[1] + 1
    shape_five = (bricks, 4, 4, 4, channels)
    occupied = (lax.broadcasted_iota(jnp.int32, (bricks * 64, 1), 0) // 64 < brick_count[0]).astype(
        jnp.float32
    )
    feats = voxel_feats.reshape(bricks * 64, channels) * occupied.astype(jnp.bfloat16)
    flat_one = w_first.reshape(27 * channels, channels)
    flat_two = w_second.reshape(27 * channels, channels)
    cols_one = patches(
        assemble(extend(feats.reshape(shape_five), face_list, corner_list), kernel_map)
    )
    z_one = jnp.dot(cols_one, flat_one, preferred_element_type=jnp.float32)
    weighted = 64.0 * brick_count[0].astype(jnp.float32)
    totals_one = moments(z_one, occupied, weighted)
    voxels = totals_one[0]
    xh_one, recip_one = normalize(z_one, totals_one)
    u_one = norm_gain[0] * xh_one + norm_shift[0]
    a_one = (jax.nn.silu(u_one) * occupied).astype(jnp.bfloat16)
    cols_two = patches(
        assemble(extend(a_one.reshape(shape_five), face_list, corner_list), kernel_map)
    )
    z_two = jnp.dot(cols_two, flat_two, preferred_element_type=jnp.float32)
    xh_two, recip_two = normalize(z_two, moments(z_two, occupied, weighted))
    pre = norm_gain[1] * xh_two + norm_shift[1] + feats.astype(jnp.float32)
    out_feats = (jax.nn.silu(pre) * occupied).astype(jnp.bfloat16)
    d_val = grad_out.reshape(bricks * 64, channels).astype(jnp.float32) * occupied * silu_slope(pre)
    sum_two, cross_two = (
        by_axis(jnp.sum(d_val, axis=0), GX_GY),
        by_axis(jnp.sum(d_val * xh_two, axis=0), GX_GY),
    )
    dz_two = (
        occupied
        * norm_gain[1]
        * recip_two
        * (d_val - sum_two / voxels - xh_two * cross_two / voxels)
    ).astype(jnp.bfloat16)
    dw_two, da_one = conv_back(
        cols_two, dz_two, flat_two, kernel_map, face_list, corner_list, bricks, channels, total
    )
    du_one = da_one * occupied * silu_slope(u_one)
    sum_one, cross_one = (
        by_axis(jnp.sum(du_one, axis=0), GX_GY),
        by_axis(jnp.sum(du_one * xh_one, axis=0), GX_GY),
    )
    dz_one = (
        occupied
        * norm_gain[0]
        * recip_one
        * (du_one - sum_one / voxels - xh_one * cross_one / voxels)
    ).astype(jnp.bfloat16)
    dw_one, back_in = conv_back(
        cols_one, dz_one, flat_one, kernel_map, face_list, corner_list, bricks, channels, total
    )
    grad_in = ((d_val + back_in) * occupied).astype(jnp.bfloat16)
    dw_one, dw_two = in_one((dw_one, dw_two), GX_GY)
    root = jnp.sqrt(voxels)
    weight_grads = jnp.stack([dw_one, dw_two]).reshape(2, 27, channels, channels) / root
    norm_grads = jnp.stack([cross_one, sum_one, cross_two, sum_two]) / root
    return (
        out_feats.reshape(bricks, 64, channels),
        grad_in.reshape(bricks, 64, channels),
        weight_grads,
        norm_grads,
    )


def solution(mesh):
    split = Mesh(mesh.devices.reshape(2, 4, 4, 2, 2), ("gx_0", "gx_1", "gy_0", "gy_1", "gy_2"))
    in_specs = (
        P(GX_GY, None, None),
        P(),
        P(),
        P(),
        P(),
        P(GX_GY, None, None),
        P(GX_GY),
        P(GX_GY, None),
        P(GX_GY, None, None),
        P(GX_GY, None, None),
    )
    out_specs = (P(GX_GY, None, None), P(GX_GY, None, None), P(), P())
    return jax.shard_map(body, mesh=split, in_specs=in_specs, out_specs=out_specs, check_vma=False)
```

profile of v0, /device:TPU:34, one launch (start us, length us, event | category | flops | bytes accessed | tf_op | source)
XLA Modules:
  0.0 2363.0 jit_solution(18110427342837406985)
XLA Ops:
  410.0 40.7 %while.123 = (s32[]{:T(128)}, f32[13,4,4,4,128]{4,3,2,1,0:T(4,128)S(1)}, s32[4,4]{1,0:T(4,128)S(1)}, f32[4,1,1,1,128]{4,3,2,1,0:T(1,128)}, s32[]{:T(128)}, /*index=5*/s32[5]{0:T(128)S(1)}, s32[1]{0:T(128)}, s32[]{:T(128)}) while((s32[]{:T(128)}, f32[13,4,4,4,128]{4,3,2,1,0:T(4,128)S(1)}, s32[4,4]{1,0:T(4,128)S(1)}, ...), condition=%wide.while_cond.71, body=%wide.while_body.71.sunk | while | flops 277 | bytes 2819 | solution.py:94
  476.6 41.5 %while.125 = (s32[]{:T(128)}, f32[13,4,4,4,128]{4,3,2,1,0:T(4,128)S(1)}, s32[4,4]{1,0:T(4,128)S(1)}, f32[4,1,1,1,128]{4,3,2,1,0:T(1,128)}, s32[]{:T(128)}, /*index=5*/s32[5]{0:T(128)S(1)}, s32[1]{0:T(128)}, s32[]{:T(128)}) while((s32[]{:T(128)}, f32[13,4,4,4,128]{4,3,2,1,0:T(4,128)S(1)}, s32[4,4]{1,0:T(4,128)S(1)}, ...), condition=%wide.while_cond.73, body=%wide.while_body.73.sunk | while | flops 277 | bytes 2819 | solution.py:94
  576.3 38.8 %while.128 = (s32[]{:T(128)}, f32[13,4,4,4,128]{4,3,2,1,0:T(4,128)S(1)}, s32[4,3]{1,0:T(4,128)}, f32[4,1,4,1,128]{4,3,2,1,0:T(1,128)}, s32[]{:T(128)}, /*index=5*/s32[5]{0:T(128)}, s32[1]{0:T(128)}, s32[]{:T(128)}) while((s32[]{:T(128)}, f32[13,4,4,4,128]{4,3,2,1,0:T(4,128)S(1)}, s32[4,3]{1,0:T(4,128)}, f32[4,1,4,1,128]{4,3,2,1,0:T(1,128)}, ...), condition=%wide.while_cond.76, body=%wide.while_body.76.sunk | while | flops 1045 | bytes 10479 | solution.py:94
  615.2 45.4 %while.129 = (s32[]{:T(128)}, f32[13,4,4,4,128]{4,3,2,1,0:T(4,128)S(1)}, s32[4,4]{1,0:T(4,128)}, f32[4,1,1,1,128]{4,3,2,1,0:T(1,128)}, s32[]{:T(128)}, /*index=5*/s32[5]{0:T(128)}, s32[1]{0:T(128)}, s32[]{:T(128)}) while((s32[]{:T(128)}, f32[13,4,4,4,128]{4,3,2,1,0:T(4,128)S(1)}, s32[4,4]{1,0:T(4,128)}, f32[4,1,1,1,128]{4,3,2,1,0:T(1,128)}, ...), condition=%wide.while_cond.77, body=%wide.while_body.77.sunk | while | flops 277 | bytes 2819 | solution.py:94
  691.5 42.8 %while.131 = (s32[]{:T(128)}, f32[13,4,4,4,128]{4,3,2,1,0:T(4,128)S(1)}, s32[4,4]{1,0:T(4,128)S(1)}, f32[4,1,1,1,128]{4,3,2,1,0:T(1,128)}, s32[]{:T(128)}, /*index=5*/s32[5]{0:T(128)}, s32[1]{0:T(128)}, s32[]{:T(128)}) while((s32[]{:T(128)}, f32[13,4,4,4,128]{4,3,2,1,0:T(4,128)S(1)}, s32[4,4]{1,0:T(4,128)S(1)}, f32[4,1,1,1,128]{4,3,2,1,0:T(1,128)}, ...), condition=%wide.while_cond.79, body=%wide.while_body.79.sunk | while | flops 277 | bytes 2819 | solution.py:94
  794.2 37.1 %while.134 = (s32[]{:T(128)}, f32[13,4,4,4,128]{4,3,2,1,0:T(4,128)S(1)}, s32[4,3]{1,0:T(4,128)S(1)}, f32[4,4,1,1,128]{4,3,2,1,0:T(1,128)}, s32[]{:T(128)}, /*index=5*/s32[5]{0:T(128)}, s32[1]{0:T(128)}, s32[]{:T(128)}) while((s32[]{:T(128)}, f32[13,4,4,4,128]{4,3,2,1,0:T(4,128)S(1)}, s32[4,3]{1,0:T(4,128)S(1)}, f32[4,4,1,1,128]{4,3,2,1,0:T(1,128)}, ...), condition=%wide.while_cond.82, body=%wide.while_body.82.sunk | while | flops 1045 | bytes 10479 | solution.py:94
  890.9 38.8 %while.137 = (s32[]{:T(128)}, f32[13,4,4,4,128]{4,3,2,1,0:T(4,128)S(1)}, s32[4,3]{1,0:T(4,128)}, f32[4,4,1,1,128]{4,3,2,1,0:T(1,128)}, s32[]{:T(128)}, /*index=5*/s32[5]{0:T(128)}, s32[1]{0:T(128)}, s32[]{:T(128)}) while((s32[]{:T(128)}, f32[13,4,4,4,128]{4,3,2,1,0:T(4,128)S(1)}, s32[4,3]{1,0:T(4,128)}, f32[4,4,1,1,128]{4,3,2,1,0:T(1,128)}, ...), condition=%wide.while_cond.85, body=%wide.while_body.85.sunk | while | flops 1045 | bytes 10479 | solution.py:94
  953.5 38.9 %while.139 = (s32[]{:T(128)}, f32[13,4,4,4,128]{4,3,2,1,0:T(4,128)S(1)}, s32[4,3]{1,0:T(4,128)}, f32[4,4,1,1,128]{4,3,2,1,0:T(1,128)}, s32[]{:T(128)}, /*index=5*/s32[5]{0:T(128)}, s32[1]{0:T(128)}, s32[]{:T(128)}) while((s32[]{:T(128)}, f32[13,4,4,4,128]{4,3,2,1,0:T(4,128)S(1)}, s32[4,3]{1,0:T(4,128)}, f32[4,4,1,1,128]{4,3,2,1,0:T(1,128)}, ...), condition=%wide.while_cond.87, body=%wide.while_body.87.sunk | while | flops 1045 | bytes 10479 | solution.py:94
  992.4 43.1 %while.140 = (s32[]{:T(128)}, f32[13,4,4,4,128]{4,3,2,1,0:T(4,128)S(1)}, s32[4,4]{1,0:T(4,128)S(1)}, f32[4,1,1,1,128]{4,3,2,1,0:T(1,128)}, s32[]{:T(128)}, /*index=5*/s32[5]{0:T(128)}, s32[1]{0:T(128)}, s32[]{:T(128)}) while((s32[]{:T(128)}, f32[13,4,4,4,128]{4,3,2,1,0:T(4,128)S(1)}, s32[4,4]{1,0:T(4,128)S(1)}, f32[4,1,1,1,128]{4,3,2,1,0:T(1,128)}, ...), condition=%wide.while_cond.88, body=%wide.while_body.88.sunk | while | flops 277 | bytes 2819 | solution.py:94
  1066.3 46.9 %while.142 = (s32[]{:T(128)}, f32[13,4,4,4,128]{4,3,2,1,0:T(4,128)S(1)}, s32[4,4]{1,0:T(4,128)}, f32[4,1,1,1,128]{4,3,2,1,0:T(1,128)}, s32[]{:T(128)}, /*index=5*/s32[5]{0:T(128)}, s32[1]{0:T(128)}, s32[]{:T(128)}) while((s32[]{:T(128)}, f32[13,4,4,4,128]{4,3,2,1,0:T(4,128)S(1)}, s32[4,4]{1,0:T(4,128)}, f32[4,1,1,1,128]{4,3,2,1,0:T(1,128)}, ...), condition=%wide.while_cond.90, body=%wide.while_body.90.sunk | while | flops 277 | bytes 2819 | solution.py:94
  1113.2 38.8 %while.143 = (s32[]{:T(128)}, f32[13,4,4,4,128]{4,3,2,1,0:T(4,128)S(1)}, s32[4,3]{1,0:T(4,128)}, f32[4,1,4,1,128]{4,3,2,1,0:T(1,128)}, s32[]{:T(128)}, /*index=5*/s32[5]{0:T(128)}, s32[1]{0:T(128)}, s32[]{:T(128)}) while((s32[]{:T(128)}, f32[13,4,4,4,128]{4,3,2,1,0:T(4,128)S(1)}, s32[4,3]{1,0:T(4,128)}, f32[4,1,4,1,128]{4,3,2,1,0:T(1,128)}, ...), condition=%wide.while_cond.91, body=%wide.while_body.91.sunk | while | flops 1045 | bytes 10479 | solution.py:94
  1173.4 37.5 %while.145 = (s32[]{:T(128)}, f32[13,4,4,4,128]{4,3,2,1,0:T(4,128)S(1)}, s32[4,3]{1,0:T(4,128)S(1)}, f32[4,1,4,1,128]{4,3,2,1,0:T(1,128)}, s32[]{:T(128)}, /*index=5*/s32[5]{0:T(128)}, s32[1]{0:T(128)}, s32[]{:T(128)}) while((s32[]{:T(128)}, f32[13,4,4,4,128]{4,3,2,1,0:T(4,128)S(1)}, s32[4,3]{1,0:T(4,128)S(1)}, f32[4,1,4,1,128]{4,3,2,1,0:T(1,128)}, ...), condition=%wide.while_cond.93, body=%wide.while_body.93.sunk | while | flops 1045 | bytes 10479 | solution.py:94
  1210.8 44.2 %while.146 = (s32[]{:T(128)}, f32[13,4,4,4,128]{4,3,2,1,0:T(4,128)S(1)}, s32[4,4]{1,0:T(4,128)S(1)}, f32[4,1,1,1,128]{4,3,2,1,0:T(1,128)}, s32[]{:T(128)}, /*index=5*/s32[5]{0:T(128)}, s32[1]{0:T(128)}, s32[]{:T(128)}) while((s32[]{:T(128)}, f32[13,4,4,4,128]{4,3,2,1,0:T(4,128)S(1)}, s32[4,4]{1,0:T(4,128)S(1)}, f32[4,1,1,1,128]{4,3,2,1,0:T(1,128)}, ...), condition=%wide.while_cond.94, body=%wide.while_body.94.sunk | while | flops 277 | bytes 2819 | solution.py:94
  1281.7 42.1 %while.148 = (s32[]{:T(128)}, f32[13,4,4,4,128]{4,3,2,1,0:T(4,128)S(1)}, s32[4,4]{1,0:T(4,128)S(1)}, f32[4,1,1,1,128]{4,3,2,1,0:T(1,128)S(1)}, s32[]{:T(128)}, /*index=5*/s32[5]{0:T(128)}, s32[1]{0:T(128)}, s32[]{:T(128)}) while((s32[]{:T(128)}, f32[13,4,4,4,128]{4,3,2,1,0:T(4,128)S(1)}, s32[4,4]{1,0:T(4,128)S(1)}, ...), condition=%wide.while_cond.96, body=%wide.while_body.96.sunk | while | flops 277 | bytes 2819 | solution.py:94
  1431.9 43.3 %while.149 = (s32[]{:T(128)}, f32[13,4,4,4,128]{4,3,2,1,0:T(4,128)S(1)}, s32[4,4]{1,0:T(4,128)}, f32[4,1,1,1,128]{4,3,2,1,0:T(1,128)}, s32[]{:T(128)}, /*index=5*/s32[5]{0:T(128)S(1)}, s32[1]{0:T(128)}, s32[]{:T(128)}) while((s32[]{:T(128)}, f32[13,4,4,4,128]{4,3,2,1,0:T(4,128)S(1)}, s32[4,4]{1,0:T(4,128)}, f32[4,1,1,1,128]{4,3,2,1,0:T(1,128)}, ...), condition=%wide.while_cond.97, body=%wide.while_body.97.sunk | while | flops 277 | bytes 2819 | solution.py:94
  1504.3 43.5 %while.151 = (s32[]{:T(128)}, f32[13,4,4,4,128]{4,3,2,1,0:T(4,128)S(1)}, s32[4,4]{1,0:T(4,128)}, f32[4,1,1,1,128]{4,3,2,1,0:T(1,128)}, s32[]{:T(128)}, /*index=5*/s32[5]{0:T(128)S(1)}, s32[1]{0:T(128)}, s32[]{:T(128)}) while((s32[]{:T(128)}, f32[13,4,4,4,128]{4,3,2,1,0:T(4,128)S(1)}, s32[4,4]{1,0:T(4,128)}, f32[4,1,1,1,128]{4,3,2,1,0:T(1,128)}, ...), condition=%wide.while_cond.99, body=%wide.while_body.99.sunk | while | flops 277 | bytes 2819 | solution.py:94
  1640.6 43.9 %while.155 = (s32[]{:T(128)}, f32[13,4,4,4,128]{4,3,2,1,0:T(4,128)S(1)}, s32[4,4]{1,0:T(4,128)}, f32[4,1,1,1,128]{4,3,2,1,0:T(1,128)}, s32[]{:T(128)}, /*index=5*/s32[5]{0:T(128)S(1)}, s32[1]{0:T(128)}, s32[]{:T(128)}) while((s32[]{:T(128)}, f32[13,4,4,4,128]{4,3,2,1,0:T(4,128)S(1)}, s32[4,4]{1,0:T(4,128)}, f32[4,1,1,1,128]{4,3,2,1,0:T(1,128)}, ...), condition=%wide.while_cond.103, body=%wide.while_body.103.sunk | while | flops 277 | bytes 2819 | solution.py:94
  1713.2 43.9 %while.157 = (s32[]{:T(128)}, f32[13,4,4,4,128]{4,3,2,1,0:T(4,128)S(1)}, s32[4,4]{1,0:T(4,128)}, f32[4,1,1,1,128]{4,3,2,1,0:T(1,128)}, s32[]{:T(128)}, /*index=5*/s32[5]{0:T(128)S(1)}, s32[1]{0:T(128)}, s32[]{:T(128)}) while((s32[]{:T(128)}, f32[13,4,4,4,128]{4,3,2,1,0:T(4,128)S(1)}, s32[4,4]{1,0:T(4,128)}, f32[4,1,1,1,128]{4,3,2,1,0:T(1,128)}, ...), condition=%wide.while_cond.105, body=%wide.while_body.105.sunk | while | flops 277 | bytes 2819 | solution.py:94
  1757.1 37.2 %while.158 = (s32[]{:T(128)}, f32[13,4,4,4,128]{4,3,2,1,0:T(4,128)S(1)}, s32[4,3]{1,0:T(4,128)}, f32[4,4,1,1,128]{4,3,2,1,0:T(1,128)}, s32[]{:T(128)}, /*index=5*/s32[5]{0:T(128)S(1)}, s32[1]{0:T(128)}, s32[]{:T(128)}) while((s32[]{:T(128)}, f32[13,4,4,4,128]{4,3,2,1,0:T(4,128)S(1)}, s32[4,3]{1,0:T(4,128)}, f32[4,4,1,1,128]{4,3,2,1,0:T(1,128)}, ...), condition=%wide.while_cond.106, body=%wide.while_body.106.sunk | while | flops 1045 | bytes 10479 | solution.py:94
  2001.1 43.8 %while.166 = (s32[]{:T(128)}, f32[13,4,4,4,128]{4,3,2,1,0:T(4,128)S(1)}, s32[4,4]{1,0:T(4,128)}, f32[4,1,1,1,128]{4,3,2,1,0:T(1,128)}, s32[]{:T(128)}, /*index=5*/s32[5]{0:T(128)S(1)}, s32[1]{0:T(128)}, s32[]{:T(128)}) while((s32[]{:T(128)}, f32[13,4,4,4,128]{4,3,2,1,0:T(4,128)S(1)}, s32[4,4]{1,0:T(4,128)}, f32[4,1,1,1,128]{4,3,2,1,0:T(1,128)}, ...), condition=%wide.while_cond.114, body=%wide.while_body.114.sunk | while | flops 277 | bytes 2819 | solution.py:94
  2073.7 44.0 %while.168 = (s32[]{:T(128)}, f32[13,4,4,4,128]{4,3,2,1,0:T(4,128)S(1)}, s32[4,4]{1,0:T(4,128)}, f32[4,1,1,1,128]{4,3,2,1,0:T(1,128)}, s32[]{:T(128)}, /*index=5*/s32[5]{0:T(128)S(1)}, s32[1]{0:T(128)}, s32[]{:T(128)}) while((s32[]{:T(128)}, f32[13,4,4,4,128]{4,3,2,1,0:T(4,128)S(1)}, s32[4,4]{1,0:T(4,128)}, f32[4,1,1,1,128]{4,3,2,1,0:T(1,128)}, ...), condition=%wide.while_cond.116, body=%wide.while_body.116.sunk | while | flops 277 | bytes 2819 | solution.py:94
  2172.3 36.9 %while.171 = (s32[]{:T(128)}, f32[13,4,4,4,128]{4,3,2,1,0:T(4,128)S(1)}, s32[4,3]{1,0:T(4,128)}, f32[4,1,4,1,128]{4,3,2,1,0:T(1,128)}, s32[]{:T(128)}, /*index=5*/s32[5]{0:T(128)S(1)}, s32[1]{0:T(128)}, s32[]{:T(128)}) while((s32[]{:T(128)}, f32[13,4,4,4,128]{4,3,2,1,0:T(4,128)S(1)}, s32[4,3]{1,0:T(4,128)}, f32[4,1,4,1,128]{4,3,2,1,0:T(1,128)}, ...), condition=%wide.while_cond.119, body=%wide.while_body.119.sunk | while | flops 1045 | bytes 10479 | solution.py:94
  2209.3 43.4 %while.172 = (s32[]{:T(128)}, f32[13,4,4,4,128]{4,3,2,1,0:T(4,128)S(1)}, s32[4,4]{1,0:T(4,128)}, f32[4,1,1,1,128]{4,3,2,1,0:T(1,128)}, s32[]{:T(128)}, /*index=5*/s32[5]{0:T(128)S(1)}, s32[1]{0:T(128)}, s32[]{:T(128)}) while((s32[]{:T(128)}, f32[13,4,4,4,128]{4,3,2,1,0:T(4,128)S(1)}, s32[4,4]{1,0:T(4,128)}, f32[4,1,1,1,128]{4,3,2,1,0:T(1,128)}, ...), condition=%wide.while_cond.120, body=%wide.while_body.120.sunk | while | flops 277 | bytes 2819 | solution.py:94
  2280.8 41.0 %while.174 = (s32[]{:T(128)}, f32[13,4,4,4,128]{4,3,2,1,0:T(4,128)S(1)}, s32[4,4]{1,0:T(4,128)}, f32[4,1,1,1,128]{4,3,2,1,0:T(1,128)S(1)}, s32[]{:T(128)}, /*index=5*/s32[5]{0:T(128)S(1)}, s32[1]{0:T(128)}, s32[]{:T(128)}) while((s32[]{:T(128)}, f32[13,4,4,4,128]{4,3,2,1,0:T(4,128)S(1)}, s32[4,4]{1,0:T(4,128)}, ...), condition=%wide.while_cond.122, body=%wide.while_body.122.sunk | while | flops 277 | bytes 2819 | solution.py:94
  (2055 shorter events, 3129.0 us)
Async XLA Ops:
  7.2 2344.3 %all-reduce.36.cloned.1.call-start = ((), (), s32[]{:S(2)}) async-start(), calls=%async_computation | async-start | bytes 7077888 | tf_op jit(solution)/shard_map/psum | solution.py:30
  27.7 34.0 %collective-permute-start.1 = (bf16[3,4,4,4,128]{4,0,3,2,1:T(4,128)(2,1)S(1)}, bf16[3,4,4,4,128]{4,0,3,2,1:T(4,128)(2,1)S(1)}, u32[]{:S(2)}, u32[]{:S(2)}) collective-permute-start(bf16[3,4,4,4,128]{4,0,3,2,1:T(4,128)(2,1)S(1)} %pad_maximum_fusion.6), channel_id=1, source_target_pairs={{16,0},{32,16},{48,32},{64,48},{80,64},{96,80},{112,96},{17,1},{33... | collective-permute-start | bytes 147464 | tf_op jit(solution)/shard_map/ppermute | solution.py:19
  32.7 29.0 %collective-permute-start = (bf16[3,4,4,4,128]{4,0,3,2,1:T(4,128)(2,1)S(1)}, bf16[3,4,4,4,128]{4,0,3,2,1:T(4,128)(2,1)S(1)}, u32[]{:S(2)}, u32[]{:S(2)}) collective-permute-start(bf16[3,4,4,4,128]{4,0,3,2,1:T(4,128)(2,1)S(1)} %pad_maximum_fusion.5), channel_id=1, source_target_pairs={{0,16},{16,32},{32,48},{48,64},{64,80},{80,96},{96,112},{1,17},{17... | collective-permute-start | bytes 147464 | tf_op jit(solution)/shard_map/ppermute | solution.py:19
  61.9 5.1 collective-permute-start.3
  65.1 8.0 collective-permute-start.2
  164.8 6.7 collective-permute-start.5
  168.8 8.3 collective-permute-start.4
  177.3 5.1 collective-permute-start.7
  180.0 8.0 collective-permute-start.6
  410.0 360.5 %copy-start.24 = (s32[4,2]{0,1:T(2,128)S(1)}, s32[4,2]{0,1:T(2,128)}, u32[]{:S(2)}) copy-start(s32[4,2]{0,1:T(2,128)} %concatenate.586.clone) | copy-start | bytes 100
  861.7 349.1 %copy-start.89 = (s32[4,4]{1,0:T(4,128)S(1)}, s32[4,4]{1,0:T(4,128)}, u32[]{:S(2)}) copy-start(s32[4,4]{1,0:T(4,128)} %get-tuple-element.5248) | copy-start | bytes 196
  890.9 364.2 %copy-start.95 = (s32[4,3]{1,0:T(4,128)S(1)}, s32[4,3]{1,0:T(4,128)}, u32[]{:S(2)}) copy-start(s32[4,3]{1,0:T(4,128)} %concatenate.600) | copy-start | bytes 148
  929.8 351.9 %copy-start.88 = (s32[4,4]{1,0:T(4,128)S(1)}, s32[4,4]{1,0:T(4,128)}, u32[]{:S(2)}) copy-start(s32[4,4]{1,0:T(4,128)} %get-tuple-element.5293) | copy-start | bytes 196
  1324.0 6.4 collective-permute-start.8
  1328.4 7.8 collective-permute-start.9
  1336.3 6.0 collective-permute-start.10
  1338.4 8.1 collective-permute-start.11
  1431.9 362.4 %copy-start.25 = (s32[4,2]{0,1:T(2,128)S(1)}, s32[4,2]{0,1:T(2,128)}, u32[]{:S(2)}) copy-start(s32[4,2]{0,1:T(2,128)} %concatenate.586.clone) | copy-start | bytes 100
  1431.9 362.4 %copy-start.121 = (s32[5]{0:T(128)S(1)}, s32[5]{0:T(128)}, u32[]{:S(2)}) copy-start(s32[5]{0:T(128)} %get-tuple-element.5417) | copy-start | bytes 64
  1504.3 347.3 %copy-start.122 = (s32[5]{0:T(128)S(1)}, s32[5]{0:T(128)}, u32[]{:S(2)}) copy-start(s32[5]{0:T(128)} %get-tuple-element.5420) | copy-start | bytes 64
  2322.0 6.4 collective-permute-start.12
  2326.5 7.8 collective-permute-start.13
  2334.3 6.0 collective-permute-start.14
  2338.1 8.1 collective-permute-start.15
  (116 other events, 8048.5 us)
Sparse Core Ops, SparseCore 0:
  1431.4 149.5 all-reduce.35
where the time goes:
time: 2400 us; the launch traced here: 2360 us
  local copies, waits for them, and re-layouts  1100 us (46%)
  other arithmetic  1000 us (42%)
  blocking collectives  128 us (5%)
  starting transfers between devices  46.3 us (2%)
  waiting for transfers between devices  36.9 us (2%)
  between operations  34.8 us (1%)
    scatter-add x768, local copies, waits for them, and re-layouts  941 us
    scatter-add x416, other arithmetic  858 us
    psum x20, blocking collectives, by_axis(): value = lax.psum(value, axis)  128 us
    gather x54, local copies, waits for them, and re-layouts, assemble(): pieces.append(jnp.take(region, tile_table[:, d], axis=0))  61 us
  transfers between devices with their start and end apart: 17, of which 9 were waited for; matrix products, arithmetic and copies ran while one was open for 39% of the time, Pallas kernels for 0%

commit v1 on v0

v1 whole, which is shorter than its diff:
```python
import functools

import jax
import jax.numpy as jnp
import numpy as np
from jax import lax
from jax.experimental import pallas as pl
from jax.experimental.pallas import tpu as pltpu
from jax.sharding import Mesh
from jax.sharding import PartitionSpec as P

GX = ("gx_0", "gx_1")
GY = ("gy_0", "gy_1", "gy_2")
GX_GY = ("gx_0", "gx_1", "gy_0", "gy_1", "gy_2")
CORE = ("gy_2",)
CHIPS = ("gx_0", "gx_1", "gy_0", "gy_1")
C = 128
NB = 4
ROWS = NB * 64
TAPS = 27
EXT = 13
EPSILON = 1e-05
F32 = jnp.float32
BF16 = jnp.bfloat16
COUNT, FACE, CORNER, VALID = 108, 109, 113, 117
NEIGHBOURS = ((-1, 0), (1, 0), (0, -1), (0, 1), (-1, -1), (-1, 1), (1, -1), (1, 1))
CHUNK = 56
PADDED = 64 * CHUNK


def shift_matrix():
    shift = np.zeros((9, 4, 4, 9, 4, 4), np.float32)
    for b in range(3):
        for c in range(3):
            for q in range(4):
                for r in range(4):
                    y, x = q + b - 1, r + c - 1
                    ob = 0 if y < 0 else 1 if y < 4 else 2
                    oc = 0 if x < 0 else 1 if x < 4 else 2
                    shift[3 * b + c, q, r, 3 * ob + oc, y % 4, x % 4] = 1.0
    return shift.reshape(144, 144)


def sources():
    return [(0, 0, 3), (1, 1, 0), (2, 1, 1), (3, 1, 2), (4, 1, 3), (5, 2, 0)]


def sigmoid(v):
    return 1.0 / (1.0 + jnp.exp(-v))


def slope(v):
    s = sigmoid(v)
    return s * (1.0 + v * (1.0 - s))


def occupied_rows(meta):
    brick = lax.broadcasted_iota(jnp.int32, (ROWS, C), 0) // 64
    return (brick < meta[COUNT]).astype(F32)


def gather_columns(meta, ext, gathered, shift, columns):
    for b in range(NB):
        for plane, oa, source in sources():
            for d in range(9):
                entry = meta[27 * b + 9 * oa + d]
                gathered[16 * d : 16 * d + 16, (6 * b + plane) * C : (6 * b + plane + 1) * C] = ext[
                    entry, 16 * source : 16 * source + 16, :
                ]
    for b in range(NB):
        moved = jnp.dot(
            shift[...], gathered[:, 6 * b * C : 6 * (b + 1) * C], preferred_element_type=F32
        ).astype(BF16)
        for a in range(3):
            for p in range(4):
                for d in range(9):
                    k = 9 * a + d
                    columns[64 * b + 16 * p : 64 * b + 16 * p + 16, k * C : (k + 1) * C] = moved[
                        16 * d : 16 * d + 16, (p + a) * C : (p + a + 1) * C
                    ]


def convolve(columns, weight):
    return jnp.dot(columns[...], weight[...], preferred_element_type=F32)


def convolve_back(meta, dz, weight, shift_back, spread, moved, acc):
    for a in range(3):
        spread[a] = lax.dot_general(
            dz,
            weight[9 * a * C : 9 * (a + 1) * C, :],
            (((1,), (1,)), ((), ())),
            preferred_element_type=F32,
        )
    acc[...] = jnp.zeros_like(acc)
    for b in range(NB):
        for plane in range(6):
            taps = [a for a in range(3) if 0 <= plane - a < 4]
            for d in range(9):
                total = None
                for a in taps:
                    row = 64 * b + 16 * (plane - a)
                    piece = spread[a, row : row + 16, d * C : (d + 1) * C]
                    total = piece if total is None else total + piece
                moved[16 * d : 16 * d + 16, (6 * b + plane) * C : (6 * b + plane + 1) * C] = (
                    total.astype(BF16)
                )
    for b in range(NB):
        home = jnp.dot(
            shift_back[...], moved[:, 6 * b * C : 6 * (b + 1) * C], preferred_element_type=F32
        )
        for plane, oa, source in sources():
            for d in range(9):
                entry = meta[27 * b + 9 * oa + d]
                acc[entry, 16 * source : 16 * source + 16, :] += home[
                    16 * d : 16 * d + 16, plane * C : (plane + 1) * C
                ]


def write_sums(out, first, second):
    odd = lax.broadcasted_iota(jnp.int32, (8, C), 0) % 2
    both = jnp.where(odd == 0, jnp.broadcast_to(first, (8, C)), jnp.broadcast_to(second, (8, C)))
    out[...] = jnp.broadcast_to(both[None], (out.shape[0] // 8, 8, C)).reshape(out.shape)


def read_sums(got):
    total = jnp.sum(got[...].reshape(got.shape[0] // 8, 8, C), axis=0)
    odd = lax.broadcasted_iota(jnp.int32, (8, C), 0) % 2
    first = jnp.sum(jnp.where(odd == 0, total, 0.0), axis=0, keepdims=True)
    second = jnp.sum(jnp.where(odd == 1, total, 0.0), axis=0, keepdims=True)
    return first, second


def rows_sum(v):
    return jnp.sum(v, axis=0, keepdims=True)


def statistics(total, squares, voxels):
    center = total / voxels
    spread_sq = squares / voxels - center * center
    return center, lax.rsqrt(spread_sq + EPSILON)


def place_received(ext, ux, lx, uy, ly):
    for e, (ref, k) in enumerate(
        ((ux, 0), (lx, 0), (uy, 0), (ly, 0), (uy, 1), (ly, 1), (uy, 2), (ly, 2))
    ):
        ext[NB + e] = ref[k]


def send_kernel(meta, field, x_up, x_low, y_faces):
    x_up[0] = field[meta[FACE]]
    x_up[1] = field[meta[CORNER]]
    x_up[2] = field[meta[CORNER + 1]]
    x_low[0] = field[meta[FACE + 1]]
    x_low[1] = field[meta[CORNER + 2]]
    x_low[2] = field[meta[CORNER + 3]]
    y_faces[0] = field[meta[FACE + 2]]
    y_faces[1] = field[meta[FACE + 3]]


def first_kernel(
    meta, voxel_feats, ux, lx, uy, ly, weight, shift,
    z_out, columns, sums, x_up, x_low, y_faces, ext, gathered,
):
    ext[NB + 8] = jnp.zeros((64, C), BF16)
    for b in range(NB):
        keep = (meta[COUNT] > b).astype(F32)
        ext[b] = (voxel_feats[b].astype(F32) * keep).astype(BF16)
    place_received(ext, ux, lx, uy, ly)
    gather_columns(meta, ext, gathered, shift, columns)
    z = convolve(columns, weight)
    z_out[...] = z.reshape(NB, 64, C)
    masked = z * occupied_rows(meta)
    write_sums(sums, rows_sum(masked), rows_sum(z * masked))
    send_kernel(meta, z_out, x_up, x_low, y_faces)


def second_kernel(
    meta, got, voxels, z_one, ux, lx, uy, ly, norm, weight, shift,
    z_out, columns, sums, xh_out, recip_out, field, ext, gathered,
):
    total, squares = read_sums(got)
    center, recip = statistics(total, squares, voxels[0])
    recip_out[...] = jnp.broadcast_to(recip, (8, C))
    field[0:NB] = z_one[...]
    place_received(field, ux, lx, uy, ly)
    for e in range(EXT - 1):
        keep = meta[COUNT] > e if e < NB else meta[VALID + e - NB] > 0
        xh = (field[e] - center) * recip
        xh_out[e] = xh
        u = norm[0:1] * xh + norm[2:3]
        ext[e] = (u * sigmoid(u) * keep.astype(F32)).astype(BF16)
    ext[EXT - 1] = jnp.zeros((64, C), BF16)
    gather_columns(meta, ext, gathered, shift, columns)
    z = convolve(columns, weight)
    z_out[...] = z
    masked = z * occupied_rows(meta)
    write_sums(sums, rows_sum(masked), rows_sum(z * masked))


def third_kernel(
    meta, got, voxels, z_two, voxel_feats, grad_out, norm, out_feats, dv_out, xh_out, recip_out, sums
):
    total, squares = read_sums(got)
    center, recip = statistics(total, squares, voxels[0])
    recip_out[...] = jnp.broadcast_to(recip, (8, C))
    occupied = occupied_rows(meta)
    xh = (z_two[...] - center) * recip
    xh_out[...] = xh
    feats = voxel_feats[...].astype(F32) * occupied
    pre = norm[1:2] * xh + norm[3:4] + feats
    s = sigmoid(pre)
    out_feats[...] = (pre * s * occupied).astype(BF16)
    dv = grad_out[...].astype(F32) * occupied * (s * (1.0 + pre * (1.0 - s)))
    dv_out[...] = dv
    write_sums(sums, rows_sum(dv), rows_sum(dv * xh))


def norm_back(dv, xh, gain, recip, total, cross, voxels, occupied):
    return (occupied * gain * recip * (dv - total / voxels - xh * cross / voxels)).astype(BF16)


def send_gradients(acc, own, y_low, y_up, x_faces):
    own[...] = acc[0:NB].reshape(ROWS, C)
    y_low[0] = acc[NB + 2].astype(BF16)
    y_low[1] = acc[NB + 4].astype(BF16)
    y_low[2] = acc[NB + 6].astype(BF16)
    y_up[0] = acc[NB + 3].astype(BF16)
    y_up[1] = acc[NB + 5].astype(BF16)
    y_up[2] = acc[NB + 7].astype(BF16)
    x_faces[0] = acc[NB].astype(BF16)
    x_faces[1] = acc[NB + 1].astype(BF16)


def fourth_kernel(
    meta, got, voxels, dv, xh_two, recip, xh_one, norm, weight, shift_back,
    dz_out, own, y_low, y_up, x_faces, sums, grads, spread, moved, acc,
):
    total, cross = read_sums(got)
    grads[0:1] = cross
    grads[1:2] = total
    dz = norm_back(
        dv[...], xh_two[...], norm[1:2], recip[0:1], total, cross, voxels[0], occupied_rows(meta)
    )
    dz_out[...] = dz
    convolve_back(meta, dz, weight, shift_back, spread, moved, acc)
    send_gradients(acc, own, y_low, y_up, x_faces)
    first = jnp.zeros((64, C), F32)
    second = jnp.zeros((64, C), F32)
    for e in range(EXT - 1):
        keep = meta[COUNT] > e if e < NB else meta[VALID + e - NB] > 0
        xh = xh_one[e]
        du = acc[e] * slope(norm[0:1] * xh + norm[2:3]) * keep.astype(F32)
        first += du
        second += du * xh
    write_sums(sums, rows_sum(first), rows_sum(second))


def add_returned(meta, field, lx, ux, ly, uy):
    for e, (ref, k, at) in enumerate(
        (
            (lx, 0, FACE), (ux, 0, FACE + 1), (ly, 0, FACE + 2), (uy, 0, FACE + 3),
            (lx, 1, CORNER), (lx, 2, CORNER + 1), (ux, 1, CORNER + 2), (ux, 2, CORNER + 3),
        )
    ):
        field[meta[at]] += ref[k].astype(F32)


def fifth_kernel(
    meta, got, voxels, own_in, lx, ux, ly, uy, xh_one, recip, norm, weight, shift_back,
    dz_out, own, y_low, y_up, x_faces, grads, field, spread, moved, acc,
):
    total, cross = read_sums(got)
    grads[0:1] = cross
    grads[1:2] = total
    field[...] = own_in[...].reshape(NB, 64, C)
    add_returned(meta, field, lx, ux, ly, uy)
    occupied = occupied_rows(meta)
    xh = xh_one[0:NB].reshape(ROWS, C)
    du = field[...].reshape(ROWS, C) * occupied * slope(norm[0:1] * xh + norm[2:3])
    dz = norm_back(du, xh, norm[0:1], recip[0:1], total, cross, voxels[0], occupied)
    dz_out[...] = dz
    convolve_back(meta, dz, weight, shift_back, spread, moved, acc)
    send_gradients(acc, own, y_low, y_up, x_faces)


def taps_kernel(columns, dz, out):
    for k in range(TAPS):
        out[k * C : (k + 1) * C, :] = lax.dot_general(
            columns[:, k * C : (k + 1) * C],
            dz[...],
            (((0,), (0,)), ((), ())),
            preferred_element_type=F32,
        )


def last_kernel(meta, own, lx, ux, ly, uy, dv, grad_in, field):
    field[...] = own[...].reshape(NB, 64, C)
    add_returned(meta, field, lx, ux, ly, uy)
    total = (dv[...] + field[...].reshape(ROWS, C)) * occupied_rows(meta)
    grad_in[...] = total.astype(BF16)


def local(kernel, outs, ins, scratch=()):
    vmem = pl.BlockSpec(memory_space=pltpu.VMEM)
    smem = pl.BlockSpec(memory_space=pltpu.SMEM)
    specs = [smem if a.ndim == 1 else vmem for a in ins]
    return pl.pallas_call(
        kernel,
        out_shape=[jax.ShapeDtypeStruct(s, d) for s, d in outs],
        in_specs=specs,
        out_specs=[vmem] * len(outs),
        scratch_shapes=[pltpu.VMEM(s, d) for s, d in scratch],
        compiler_params=pltpu.CompilerParams(vmem_limit_bytes=48 << 20),
        name=kernel.__name__,
    )(*ins)


def shifted(value, axis, by):
    length = lax.axis_size(axis)
    pairs = [(i, i + by) for i in range(length) if 0 <= i + by < length]
    return lax.ppermute(value, axis, pairs)


def exchange(value, axes):
    return lax.all_to_all(value, axes, 0, 0, tiled=True)


def swap(value):
    return lax.ppermute(value, CORE, [(0, 1), (1, 0)])


def outward(x_up, x_low, y_faces):
    ux = shifted(x_up, GX, 1)
    lx = shifted(x_low, GX, -1)
    uy = shifted(jnp.concatenate([y_faces[0:1], ux[1:2], lx[1:2]], axis=0), GY, 1)
    ly = shifted(jnp.concatenate([y_faces[1:2], ux[2:3], lx[2:3]], axis=0), GY, -1)
    return ux, lx, uy, ly


def homeward(y_low, y_up, x_faces):
    ly = shifted(y_low, GY, -1)
    uy = shifted(y_up, GY, 1)
    lx = shifted(jnp.concatenate([x_faces[0:1], ly[1:2], uy[1:2]], axis=0), GX, -1)
    ux = shifted(jnp.concatenate([x_faces[1:2], ly[2:3], uy[2:3]], axis=0), GX, 1)
    return lx, ux, ly, uy


def body(
    voxel_feats,
    w_first,
    w_second,
    norm_gain,
    norm_shift,
    grad_out,
    brick_count,
    kernel_map,
    face_send,
    corner_send,
):
    i = lax.axis_index(GX)
    j = lax.axis_index(GY)
    dx = np.array([d[0] for d in NEIGHBOURS], np.int32)
    dy = np.array([d[1] for d in NEIGHBOURS], np.int32)
    inside = (i + dx >= 0) & (i + dx < 8) & (j + dy >= 0) & (j + dy < 16)
    meta = jnp.concatenate(
        [
            kernel_map.reshape(-1),
            brick_count,
            face_send.reshape(-1),
            corner_send.reshape(-1),
            inside.astype(jnp.int32),
        ]
    )
    norm = jnp.concatenate([norm_gain, norm_shift], axis=0)
    shift = jnp.asarray(shift_matrix(), BF16)
    shift_back = jnp.asarray(shift_matrix().T, BF16)
    flat_one = w_first.reshape(TAPS * C, C)
    flat_two = w_second.reshape(TAPS * C, C)
    brick = (64, C)
    three, two = (3,) + brick, (2,) + brick
    wide = (ROWS, TAPS * C)
    rows = (ROWS, C)
    sums = ((2 * 128, C), F32)
    ext = ((EXT,) + brick, BF16)
    gathered = ((144, 6 * NB * C), BF16)

    sends = local(send_kernel, [(three, BF16), (three, BF16), (two, BF16)], [meta, voxel_feats])
    received = outward(*sends)
    counts = exchange(jnp.broadcast_to(brick_count.astype(F32).reshape(1, 1), (128, C)), GX_GY)
    voxels = (64.0 * jnp.sum(counts[:, 0])).reshape(1)
    z_one, columns_one, part, *sends = local(
        first_kernel,
        [((NB,) + brick, F32), (wide, BF16), sums, (three, F32), (three, F32), (two, F32)],
        [meta, voxel_feats, *received, flat_one, shift],
        [ext, gathered],
    )
    received = outward(*sends)
    part = exchange(part, GX_GY)
    z_two, columns_two, part, xh_one, recip_one = local(
        second_kernel,
        [(rows, F32), (wide, BF16), sums, ((EXT - 1,) + brick, F32), ((8, C), F32)],
        [meta, part, voxels, z_one, *received, norm, flat_two, shift],
        [((EXT - 1,) + brick, F32), ext, gathered],
    )
    part = exchange(part, GX_GY)
    out_feats, dv, xh_two, recip_two, part = local(
        third_kernel,
        [(rows, BF16), (rows, F32), (rows, F32), ((8, C), F32), sums],
        [meta, part, voxels, z_two, voxel_feats.reshape(rows), grad_out.reshape(rows), norm],
    )
    part = exchange(part, GX_GY)
    back = [
        ((3, ROWS, 9 * C), F32),
        gathered,
        ((EXT,) + brick, F32),
    ]
    dz_two, own, y_low, y_up, x_faces, part, grads_two = local(
        fourth_kernel,
        [(rows, BF16), (rows, F32), (three, BF16), (three, BF16), (two, BF16), sums, ((2, C), F32)],
        [meta, part, voxels, dv, xh_two, recip_two, xh_one, norm, flat_two, shift_back],
        back,
    )
    returned = homeward(y_low, y_up, x_faces)
    (dw_two,) = local(taps_kernel, [((TAPS * C, C), F32)], [columns_two, dz_two])
    part = exchange(part, GX_GY)
    dz_one, own, y_low, y_up, x_faces, grads_one = local(
        fifth_kernel,
        [(rows, BF16), (rows, F32), (three, BF16), (three, BF16), (two, BF16), ((2, C), F32)],
        [meta, part, voxels, own, *returned, xh_one, recip_one, norm, flat_one, shift_back],
        [((NB,) + brick, F32)] + back,
    )
    returned = homeward(y_low, y_up, x_faces)
    (dw_one,) = local(taps_kernel, [((TAPS * C, C), F32)], [columns_one, dz_one])
    (grad_in,) = local(
        last_kernel, [(rows, BF16)], [meta, own, *returned, dv], [((NB,) + brick, F32)]
    )
    root = jnp.sqrt(voxels[0])
    core = lax.axis_index(CORE)
    mine = jnp.where(core == 0, dw_one, dw_two)
    other = jnp.where(core == 0, dw_two, dw_one).astype(BF16)
    mine = (mine + swap(other).astype(F32)).astype(BF16)
    mine = jnp.pad(mine, ((0, PADDED - TAPS * C), (0, 0)))
    pieces = exchange(mine, CHIPS).reshape(64, CHUNK, C)
    piece = (jnp.sum(pieces.astype(F32), axis=0) / root).astype(BF16)
    whole = exchange(jnp.broadcast_to(piece[None], (64, CHUNK, C)).reshape(PADDED, C), CHIPS)
    partner = swap(whole)
    first = jnp.where(core == 0, whole, partner)[: TAPS * C]
    second = jnp.where(core == 0, partner, whole)[: TAPS * C]
    weight_grads = jnp.stack([first, second]).reshape(2, TAPS, C, C).astype(F32)
    norm_grads = jnp.concatenate([grads_one, grads_two], axis=0) / root
    return (
        out_feats.reshape(NB, 64, C),
        grad_in.reshape(NB, 64, C),
        weight_grads,
        norm_grads,
    )


def solution(mesh):
    split = Mesh(mesh.devices.reshape(2, 4, 4, 2, 2), GX_GY)
    in_specs = (
        P(GX_GY, None, None),
        P(),
        P(),
        P(),
        P(),
        P(GX_GY, None, None),
        P(GX_GY),
        P(GX_GY, None),
        P(GX_GY, None, None),
        P(GX_GY, None, None),
    )
    out_specs = (P(GX_GY, None, None), P(GX_GY, None, None), P(), P())
    return jax.shard_map(body, mesh=split, in_specs=in_specs, out_specs=out_specs, check_vma=False)
```

time: 2400 us -> 217 us (0.09); the launches traced: 2360 us -> 214 us
  local copies, waits for them, and re-layouts: 1100 us -> 16.2 us
  other arithmetic: 1000 us -> 6.61 us
  blocking collectives: 128 us -> 31.8 us
  starting transfers between devices: 46.3 us -> 99.9 us
  between operations: 34.8 us -> 2.57 us
    scatter-add x806 -> x0, local copies, waits for them, and re-layouts: 979 us -> none
    scatter-add x450 -> x0, other arithmetic: 881 us -> none
    psum x20 -> x0, blocking collectives: 128 us -> none  [by_axis(): value = lax.psum(value, axis)]
    gather x54 -> x0, local copies, waits for them, and re-layouts: 61 us -> none  [assemble(): pieces.append(jnp.take(region, tile_table[:, d], axis=0))]
    add x36 -> x0, other arithmetic: 45.6 us -> none  [spread(): padded = padded.at[:, a:a + 4, b:b + 4, c:c + 4].add(piece)]
    select_n x73 -> x1, other arithmetic: 42.5 us -> 0.12 us  [body(): first = jnp.where(core == 0, whole, partner)[:TAPS * C]]
    all_to_all x0 -> x5, starting transfers between devices: none -> 40.9 us  [exchange(): return lax.all_to_all(value, axes, 0, 0, tiled=True)]
    all_to_all x0 -> x2, blocking collectives: none -> 31.8 us  [exchange(): return lax.all_to_all(value, axes, 0, 0, tiled=True)]
  transfers between devices with their start and end apart: 17 -> 23, of which waited for: 9 -> 9; matrix products, arithmetic and copies ran while one was open for 39% -> 2% of each run, Pallas kernels for 0% -> 2%
where the time goes in v1:
time: 217 us; the launch traced here: 214 us
  starting transfers between devices  99.9 us (46%)
  waiting for transfers between devices  43.3 us (20%)
  blocking collectives  31.8 us (15%)
  local copies, waits for them, and re-layouts  16.2 us (7%)
  Pallas kernels  14 us (6%)
  other arithmetic  6.61 us (3%)
  between operations  2.57 us (1%)
    ppermute x16, starting transfers between devices, shifted(): return lax.ppermute(value, axis, pairs)  58.2 us
    all_to_all x5, starting transfers between devices, exchange(): return lax.all_to_all(value, axes, 0, 0, tiled=True)  40.9 us
    all_to_all x2, blocking collectives, exchange(): return lax.all_to_all(value, axes, 0, 0, tiled=True)  31.8 us
    all_to_all x5, waiting for transfers between devices, exchange(): return lax.all_to_all(value, axes, 0, 0, tiled=True)  25.9 us
    ppermute x16, waiting for transfers between devices, shifted(): return lax.ppermute(value, axis, pairs)  15.4 us
    pallas_call x9, Pallas kernels, local(): pl.pallas_call(kernel, out_shape=[jax.ShapeDtypeStruct(s, d) for s, d in...  14 us
    unnamed x52, local copies, waits for them, and re-layouts  11.8 us
  transfers between devices with their start and end apart: 23, of which 9 were waited for; matrix products, arithmetic and copies ran while one was open for 2% of the time, Pallas kernels for 2%

profile of v1, /device:TPU:34, one launch (start us, length us, event | category | flops | bytes accessed | tf_op | source)
XLA Modules:
  0.0 214.4 jit_solution(12632556904802186613)
XLA Ops:
  5.0 3.5 %collective-permute-start = (bf16[3,64,128]{2,1,0:T(8,128)(2,1)S(1)}, bf16[3,64,128]{2,1,0:T(8,128)(2,1)S(1)}, u32[]{:S(2)}, u32[]{:S(2)}) collective-permute-start(bf16[3,64,128]{2,1,0:T(8,128)(2,1)S(1)} %get-tuple-element.36), channel_id=1, source_target_pairs={{0,16},{16,32},{32,48},{48,64},{64,80},{80,96},{96,112},{1,17},{17... | collective-permute-start | bytes 147464 | tf_op jit(solution)/shard_map/ppermute | solution.py:323
  8.5 4.5 %collective-permute-start.1 = (bf16[3,64,128]{2,1,0:T(8,128)(2,1)S(1)}, bf16[3,64,128]{2,1,0:T(8,128)(2,1)S(1)}, u32[]{:S(2)}, u32[]{:S(2)}) collective-permute-start(bf16[3,64,128]{2,1,0:T(8,128)(2,1)S(1)} %get-tuple-element.37), channel_id=1, source_target_pairs={{16,0},{32,16},{48,32},{64,48},{80,64},{96,80},{112,96},{17,1},{33... | collective-permute-start | bytes 147464 | tf_op jit(solution)/shard_map/ppermute | solution.py:323
  13.6 8.1 %all-to-all-start.1 = ((f32[128,1,128]{2,1,0:T(1,128)}), f32[128,1,128]{2,1,0:T(1,128)S(1)}, u32[]{:S(2)}, u32[]{:S(2)}) async-start(f32[128,1,128]{2,1,0:T(1,128)} %broadcast_in_dim.14), calls=%async_computation.1 | async-start | bytes 131072 | tf_op jit(solution)/shard_map/all_to_all | solution.py:327
  23.9 5.9 %collective-permute-start.3 = (bf16[3,64,128]{2,1,0:T(8,128)(2,1)S(1)}, bf16[3,64,128]{2,1,0:T(8,128)(2,1)S(1)}, u32[]{:S(2)}, u32[]{:S(2)}) collective-permute-start(bf16[3,64,128]{2,1,0:T(8,128)(2,1)S(1)} %pad_maximum_fusion.3), channel_id=1, source_target_pairs={{1,0},{2,1},{3,2},{4,3},{5,4},{6,5},{7,6},{8,7},{9,8},{10,9},{11,1... | collective-permute-start | bytes 147464 | tf_op jit(solution)/shard_map/ppermute | solution.py:323
  38.0 3.5 %collective-permute-start.4 = (f32[3,64,128]{2,1,0:T(8,128)S(1)}, f32[3,64,128]{2,1,0:T(8,128)S(1)}, u32[]{:S(2)}, u32[]{:S(2)}) collective-permute-start(f32[3,64,128]{2,1,0:T(8,128)S(1)} %get-tuple-element.41), channel_id=1, source_target_pairs={{0,16},{16,32},{32,48},{48,64},{64,80},{80,96},{96,112},{1,17},{17... | collective-permute-start | bytes 294920 | tf_op jit(solution)/shard_map/ppermute | solution.py:323
  41.5 4.5 %collective-permute-start.5 = (f32[3,64,128]{2,1,0:T(8,128)S(1)}, f32[3,64,128]{2,1,0:T(8,128)S(1)}, u32[]{:S(2)}, u32[]{:S(2)}) collective-permute-start(f32[3,64,128]{2,1,0:T(8,128)S(1)} %get-tuple-element.42), channel_id=1, source_target_pairs={{16,0},{32,16},{48,32},{64,48},{80,64},{96,80},{112,96},{17,1},{33... | collective-permute-start | bytes 294920 | tf_op jit(solution)/shard_map/ppermute | solution.py:323
  46.1 3.1 %collective-permute-done.5.lx = f32[3,64,128]{2,1,0:T(8,128)S(1)} collective-permute-done((f32[3,64,128]{2,1,0:T(8,128)S(1)}, f32[3,64,128]{2,1,0:T(8,128)S(1)}, u32[]{:S(2)}, u32[]{:S(2)}) %collective-permute-start.5) | collective-permute-done | bytes 98336 | tf_op jit(solution)/shard_map/ppermute | solution.py:323
  51.4 12.1 %all-to-all-start = ((f32[128,2,128]{2,1,0:T(2,128)}), f32[128,2,128]{2,1,0:T(2,128)S(1)}, u32[]{:S(2)}, u32[]{:S(2)}) async-start(f32[128,2,128]{2,1,0:T(2,128)} %bitcast.3), calls=%async_computation | async-start | bytes 262144 | tf_op jit(solution)/shard_map/all_to_all | solution.py:327
  63.5 3.6 %collective-permute-start.7 = (f32[3,64,128]{2,1,0:T(8,128)S(1)}, f32[3,64,128]{2,1,0:T(8,128)S(1)}, u32[]{:S(2)}, u32[]{:S(2)}) collective-permute-start(f32[3,64,128]{2,1,0:T(8,128)S(1)} %pad_maximum_fusion.1), channel_id=1, source_target_pairs={{1,0},{2,1},{3,2},{4,3},{5,4},{6,5},{7,6},{8,7},{9,8},{10,9},{11,1... | collective-permute-start | bytes 294920 | tf_op jit(solution)/shard_map/ppermute | solution.py:323
  68.3 3.2 %all-to-all-done = f32[128,2,128]{2,1,0:T(2,128)S(1)} async-done(((f32[128,2,128]{2,1,0:T(2,128)}), f32[128,2,128]{2,1,0:T(2,128)S(1)}, u32[]{:S(2)}, u32[]{:S(2)}) %all-to-all-start) | async-done | bytes 131104 | tf_op jit(solution)/shard_map/all_to_all | solution.py:327
  74.6 17.7 %all_to_all.71 = f32[128,2,128]{2,1,0:T(2,128)S(1)} all-to-all(f32[128,2,128]{2,1,0:T(2,128)S(1)} %bitcast.32), channel_id=1, replica_groups=mesh['gx_0'=2,'gx_1'=4,'gy_0'=4,'gy_1'=2,'gy_2'=2] {'gx_0','gx_1','gy_0'..., dimensions={0} | all-to-all | bytes 262144 | tf_op jit(solution)/shard_map/all_to_all | solution.py:327
  93.6 14.2 %all_to_all.72 = f32[128,2,128]{2,1,0:T(2,128)S(1)} all-to-all(f32[128,2,128]{2,1,0:T(2,128)S(1)} %bitcast.33), channel_id=1, replica_groups=mesh['gx_0'=2,'gx_1'=4,'gy_0'=4,'gy_1'=2,'gy_2'=2] {'gx_0','gx_1','gy_0'..., dimensions={0} | all-to-all | bytes 262144 | tf_op jit(solution)/shard_map/all_to_all | solution.py:327
  107.7 3.0 %fourth_kernel.1 = (bf16[256,128]{1,0:T(8,128)(2,1)S(1)}, f32[256,128]{1,0:T(8,128)S(1)}, bf16[3,64,128]{2,1,0:T(8,128)(2,1)S(1)}, bf16[3,64,128]{2,1,0:T(8,128)...) custom-call(s32[125]{0:T(128)S(1)} %concatenate.34.meta, ...), custom_call_target="tpu_custom_call" | custom-call | tf_op jit(solution)/shard_map/fourth_kernel/pallas_call | solution.py:309
  111.9 6.2 %all-to-all-start.4 = ((f32[128,2,128]{2,1,0:T(2,128)}), f32[128,2,128]{2,1,0:T(2,128)S(1)}, u32[]{:S(2)}, u32[]{:S(2)}) async-start(f32[128,2,128]{2,1,0:T(2,128)} %bitcast.16), calls=%async_computation.4 | async-start | bytes 262144 | tf_op jit(solution)/shard_map/all_to_all | solution.py:327
  120.1 5.9 %collective-permute-start.8 = (bf16[3,64,128]{2,1,0:T(8,128)(2,1)S(1)}, bf16[3,64,128]{2,1,0:T(8,128)(2,1)S(1)}, u32[]{:S(2)}, u32[]{:S(2)}) collective-permute-start(bf16[3,64,128]{2,1,0:T(8,128)(2,1)S(1)} %get-tuple-element.55), channel_id=1, source_target_pairs={{1,0},{2,1},{3,2},{4,3},{5,4},{6,5},{7,6},{8,7},{9,8},{10,9},{11,1... | collective-permute-start | bytes 147464 | tf_op jit(solution)/shard_map/ppermute | solution.py:323
  128.4 4.8 %collective-permute-start.10 = (bf16[3,64,128]{2,1,0:T(8,128)(2,1)}, bf16[3,64,128]{2,1,0:T(8,128)(2,1)}, u32[]{:S(2)}, u32[]{:S(2)}) collective-permute-start(bf16[3,64,128]{2,1,0:T(8,128)(2,1)} %pad_maximum_fusion.4), channel_id=1, source_target_pairs={{16,0},{32,16},{48,32},{64,48},{80,64},{96,80},{112,96},{17,1},{33... | collective-permute-start | bytes 147464 | tf_op jit(solution)/shard_map/ppermute | solution.py:323
  137.9 4.3 %collective-permute-done.11.ux = bf16[3,64,128]{2,1,0:T(8,128)(2,1)} collective-permute-done((bf16[3,64,128]{2,1,0:T(8,128)(2,1)}, bf16[3,64,128]{2,1,0:T(8,128)(2,1)}, u32[]{:S(2)}, u32[]{:S(2)}) %collective-permute-start.11) | collective-permute-done | bytes 49184 | tf_op jit(solution)/shard_map/ppermute | solution.py:323
  152.7 8.1 %all-to-all-start.5 = ((bf16[64,56,128]{2,1,0:T(8,128)(2,1)}), bf16[64,56,128]{2,1,0:T(8,128)(2,1)S(1)}, u32[]{:S(2)}, u32[]{:S(2)}) async-start(bf16[64,56,128]{2,1,0:T(8,128)(2,1)} %bitcast.19), calls=%async_computation.5 | async-start | bytes 1835008 | tf_op jit(solution)/shard_map/all_to_all | solution.py:327
  160.8 15.9 %all-to-all-done.5 = bf16[64,56,128]{2,1,0:T(8,128)(2,1)S(1)} async-done(((bf16[64,56,128]{2,1,0:T(8,128)(2,1)}), bf16[64,56,128]{2,1,0:T(8,128)(2,1)S(1)}, u32[]{:S(2)}, u32[]{:S(2)}) %all-to-all-start.5) | async-done | bytes 917536 | tf_op jit(solution)/shard_map/all_to_all | solution.py:327
  178.0 6.4 %all-to-all-start.6 = ((bf16[64,56,128]{2,1,0:T(8,128)(2,1)}), bf16[64,56,128]{2,1,0:T(8,128)(2,1)S(1)}, u32[]{:S(2)}, u32[]{:S(2)}) async-start(bf16[64,56,128]{2,1,0:T(8,128)(2,1)} %broadcast_in_dim.15), calls=%async_computation.6 | async-start | bytes 1835008 | tf_op jit(solution)/shard_map/all_to_all | solution.py:327
  186.4 6.0 %collective-permute-start.12 = (bf16[3,64,128]{2,1,0:T(8,128)(2,1)S(1)}, bf16[3,64,128]{2,1,0:T(8,128)(2,1)S(1)}, u32[]{:S(2)}, u32[]{:S(2)}) collective-permute-start(bf16[3,64,128]{2,1,0:T(8,128)(2,1)S(1)} %copy-done.23), channel_id=1, source_target_pairs={{1,0},{2,1},{3,2},{4,3},{5,4},{6,5},{7,6},{8,7},{9,8},{10,9},{11,1... | collective-permute-start | bytes 147464 | tf_op jit(solution)/shard_map/ppermute | solution.py:323
  192.4 6.8 %all-to-all-done.6 = bf16[64,56,128]{2,1,0:T(8,128)(2,1)S(1)} async-done(((bf16[64,56,128]{2,1,0:T(8,128)(2,1)}), bf16[64,56,128]{2,1,0:T(8,128)(2,1)S(1)}, u32[]{:S(2)}, u32[]{:S(2)}) %all-to-all-start.6) | async-done | bytes 917536 | tf_op jit(solution)/shard_map/all_to_all | solution.py:327
  199.2 3.6 %collective-permute-start.14 = (bf16[3,64,128]{2,1,0:T(8,128)(2,1)S(1)}, bf16[3,64,128]{2,1,0:T(8,128)(2,1)S(1)}, u32[]{:S(2)}, u32[]{:S(2)}) collective-permute-start(bf16[3,64,128]{2,1,0:T(8,128)(2,1)S(1)} %pad_maximum_fusion.6), channel_id=1, source_target_pairs={{16,0},{32,16},{48,32},{64,48},{80,64},{96,80},{112,96},{17,1},{33... | collective-permute-start | bytes 147464 | tf_op jit(solution)/shard_map/ppermute | solution.py:323
  205.7 5.3 %collective-permute-done.15.ux = bf16[3,64,128]{2,1,0:T(8,128)(2,1)S(1)} collective-permute-done((bf16[3,64,128]{2,1,0:T(8,128)(2,1)S(1)}, bf16[3,64,128]{2,1,0:T(8,128)(2,1)S(1)}, u32[]{:S(2)}, u32[]{:S(2)}) %collective-permute-start.15) | collective-permute-done | bytes 49184 | tf_op jit(solution)/shard_map/ppermute | solution.py:323
  (120 shorter events, 51.7 us)
Async XLA Ops:
  0.6 70.9 %copy-start = (bf16[27,128,128]{2,1,0:T(8,128)(2,1)S(1)}, bf16[27,128,128]{2,1,0:T(8,128)(2,1)}, u32[]{:S(2)}) copy-start(bf16[27,128,128]{2,1,0:T(8,128)(2,1)} %param.16) | copy-start | bytes 2654212
  5.0 16.8 %collective-permute-start = (bf16[3,64,128]{2,1,0:T(8,128)(2,1)S(1)}, bf16[3,64,128]{2,1,0:T(8,128)(2,1)S(1)}, u32[]{:S(2)}, u32[]{:S(2)}) collective-permute-start(bf16[3,64,128]{2,1,0:T(8,128)(2,1)S(1)} %get-tuple-element.36), channel_id=1, source_target_pairs={{0,16},{16,32},{32,48},{48,64},{64,80},{80,96},{96,112},{1,17},{17... | collective-permute-start | bytes 147464 | tf_op jit(solution)/shard_map/ppermute | solution.py:323
  8.5 13.3 %collective-permute-start.1 = (bf16[3,64,128]{2,1,0:T(8,128)(2,1)S(1)}, bf16[3,64,128]{2,1,0:T(8,128)(2,1)S(1)}, u32[]{:S(2)}, u32[]{:S(2)}) collective-permute-start(bf16[3,64,128]{2,1,0:T(8,128)(2,1)S(1)} %get-tuple-element.37), channel_id=1, source_target_pairs={{16,0},{32,16},{48,32},{64,48},{80,64},{96,80},{112,96},{17,1},{33... | collective-permute-start | bytes 147464 | tf_op jit(solution)/shard_map/ppermute | solution.py:323
  13.6 37.7 %all-to-all-start.1 = ((f32[128,1,128]{2,1,0:T(1,128)}), f32[128,1,128]{2,1,0:T(1,128)S(1)}, u32[]{:S(2)}, u32[]{:S(2)}) async-start(f32[128,1,128]{2,1,0:T(1,128)} %broadcast_in_dim.14), calls=%async_computation.1 | async-start | bytes 131072 | tf_op jit(solution)/shard_map/all_to_all | solution.py:327
  21.8 8.7 %collective-permute-start.2 = (bf16[3,64,128]{2,1,0:T(8,128)(2,1)S(1)}, bf16[3,64,128]{2,1,0:T(8,128)(2,1)S(1)}, u32[]{:S(2)}, u32[]{:S(2)}) collective-permute-start(bf16[3,64,128]{2,1,0:T(8,128)(2,1)S(1)} %pad_maximum_fusion.2), channel_id=1, source_target_pairs={{0,1},{1,2},{2,3},{3,4},{4,5},{5,6},{6,7},{7,8},{8,9},{9,10},{10,1... | collective-permute-start | bytes 147464 | tf_op jit(solution)/shard_map/ppermute | solution.py:323
  23.9 7.7 %collective-permute-start.3 = (bf16[3,64,128]{2,1,0:T(8,128)(2,1)S(1)}, bf16[3,64,128]{2,1,0:T(8,128)(2,1)S(1)}, u32[]{:S(2)}, u32[]{:S(2)}) collective-permute-start(bf16[3,64,128]{2,1,0:T(8,128)(2,1)S(1)} %pad_maximum_fusion.3), channel_id=1, source_target_pairs={{1,0},{2,1},{3,2},{4,3},{5,4},{6,5},{7,6},{8,7},{9,8},{10,9},{11,1... | collective-permute-start | bytes 147464 | tf_op jit(solution)/shard_map/ppermute | solution.py:323
  38.0 11.2 %collective-permute-start.4 = (f32[3,64,128]{2,1,0:T(8,128)S(1)}, f32[3,64,128]{2,1,0:T(8,128)S(1)}, u32[]{:S(2)}, u32[]{:S(2)}) collective-permute-start(f32[3,64,128]{2,1,0:T(8,128)S(1)} %get-tuple-element.41), channel_id=1, source_target_pairs={{0,16},{16,32},{32,48},{48,64},{64,80},{80,96},{96,112},{1,17},{17... | collective-permute-start | bytes 294920 | tf_op jit(solution)/shard_map/ppermute | solution.py:323
  41.5 7.6 %collective-permute-start.5 = (f32[3,64,128]{2,1,0:T(8,128)S(1)}, f32[3,64,128]{2,1,0:T(8,128)S(1)}, u32[]{:S(2)}, u32[]{:S(2)}) collective-permute-start(f32[3,64,128]{2,1,0:T(8,128)S(1)} %get-tuple-element.42), channel_id=1, source_target_pairs={{16,0},{32,16},{48,32},{64,48},{80,64},{96,80},{112,96},{17,1},{33... | collective-permute-start | bytes 294920 | tf_op jit(solution)/shard_map/ppermute | solution.py:323
  49.2 22.4 %collective-permute-start.6 = (f32[3,64,128]{2,1,0:T(8,128)S(1)}, f32[3,64,128]{2,1,0:T(8,128)S(1)}, u32[]{:S(2)}, u32[]{:S(2)}) collective-permute-start(f32[3,64,128]{2,1,0:T(8,128)S(1)} %pad_maximum_fusion), channel_id=1, source_target_pairs={{0,1},{1,2},{2,3},{3,4},{4,5},{5,6},{6,7},{7,8},{8,9},{9,10},{10,1... | collective-permute-start | bytes 294920 | tf_op jit(solution)/shard_map/ppermute | solution.py:323
  51.4 20.2 %all-to-all-start = ((f32[128,2,128]{2,1,0:T(2,128)}), f32[128,2,128]{2,1,0:T(2,128)S(1)}, u32[]{:S(2)}, u32[]{:S(2)}) async-start(f32[128,2,128]{2,1,0:T(2,128)} %bitcast.3), calls=%async_computation | async-start | bytes 262144 | tf_op jit(solution)/shard_map/all_to_all | solution.py:327
  63.5 8.1 %collective-permute-start.7 = (f32[3,64,128]{2,1,0:T(8,128)S(1)}, f32[3,64,128]{2,1,0:T(8,128)S(1)}, u32[]{:S(2)}, u32[]{:S(2)}) collective-permute-start(f32[3,64,128]{2,1,0:T(8,128)S(1)} %pad_maximum_fusion.1), channel_id=1, source_target_pairs={{1,0},{2,1},{3,2},{4,3},{5,4},{6,5},{7,6},{8,7},{9,8},{10,9},{11,1... | collective-permute-start | bytes 294920 | tf_op jit(solution)/shard_map/ppermute | solution.py:323
  111.9 30.3 %all-to-all-start.4 = ((f32[128,2,128]{2,1,0:T(2,128)}), f32[128,2,128]{2,1,0:T(2,128)S(1)}, u32[]{:S(2)}, u32[]{:S(2)}) async-start(f32[128,2,128]{2,1,0:T(2,128)} %bitcast.16), calls=%async_computation.4 | async-start | bytes 262144 | tf_op jit(solution)/shard_map/all_to_all | solution.py:327
  118.1 8.0 %collective-permute-start.9 = (bf16[3,64,128]{2,1,0:T(8,128)(2,1)S(1)}, bf16[3,64,128]{2,1,0:T(8,128)(2,1)S(1)}, u32[]{:S(2)}, u32[]{:S(2)}) collective-permute-start(bf16[3,64,128]{2,1,0:T(8,128)(2,1)S(1)} %get-tuple-element.56), channel_id=1, source_target_pairs={{0,1},{1,2},{2,3},{3,4},{4,5},{5,6},{6,7},{7,8},{8,9},{9,10},{10,1... | collective-permute-start | bytes 147464 | tf_op jit(solution)/shard_map/ppermute | solution.py:323
  120.1 7.7 %collective-permute-start.8 = (bf16[3,64,128]{2,1,0:T(8,128)(2,1)S(1)}, bf16[3,64,128]{2,1,0:T(8,128)(2,1)S(1)}, u32[]{:S(2)}, u32[]{:S(2)}) collective-permute-start(bf16[3,64,128]{2,1,0:T(8,128)(2,1)S(1)} %get-tuple-element.55), channel_id=1, source_target_pairs={{1,0},{2,1},{3,2},{4,3},{5,4},{6,5},{7,6},{8,7},{9,8},{10,9},{11,1... | collective-permute-start | bytes 147464 | tf_op jit(solution)/shard_map/ppermute | solution.py:323
  128.4 9.5 %collective-permute-start.10 = (bf16[3,64,128]{2,1,0:T(8,128)(2,1)}, bf16[3,64,128]{2,1,0:T(8,128)(2,1)}, u32[]{:S(2)}, u32[]{:S(2)}) collective-permute-start(bf16[3,64,128]{2,1,0:T(8,128)(2,1)} %pad_maximum_fusion.4), channel_id=1, source_target_pairs={{16,0},{32,16},{48,32},{64,48},{80,64},{96,80},{112,96},{17,1},{33... | collective-permute-start | bytes 147464 | tf_op jit(solution)/shard_map/ppermute | solution.py:323
  133.8 8.4 %collective-permute-start.11 = (bf16[3,64,128]{2,1,0:T(8,128)(2,1)}, bf16[3,64,128]{2,1,0:T(8,128)(2,1)}, u32[]{:S(2)}, u32[]{:S(2)}) collective-permute-start(bf16[3,64,128]{2,1,0:T(8,128)(2,1)} %pad_maximum_fusion.5), channel_id=1, source_target_pairs={{0,16},{16,32},{32,48},{48,64},{64,80},{80,96},{96,112},{1,17},{17... | collective-permute-start | bytes 147464 | tf_op jit(solution)/shard_map/ppermute | solution.py:323
  148.6 2.9 %collective-permute-start.16 = (bf16[3456,128]{1,0:T(8,128)(2,1)S(1)}, bf16[3456,128]{1,0:T(8,128)(2,1)S(1)}, u32[]{:S(2)}, u32[]{:S(2)}) collective-permute-start(bf16[3456,128]{1,0:T(8,128)(2,1)S(1)} %select_convert_fusion), channel_id=1, source_target_pairs={{0,1},{1,0},{2,3},{3,2},{4,5},{5,4},{6,7},{7,6},{8,9},{9,8},{10,11... | collective-permute-start | bytes 2654216 | tf_op jit(solution)/shard_map/ppermute | solution.py:331
  152.7 24.1 %all-to-all-start.5 = ((bf16[64,56,128]{2,1,0:T(8,128)(2,1)}), bf16[64,56,128]{2,1,0:T(8,128)(2,1)S(1)}, u32[]{:S(2)}, u32[]{:S(2)}) async-start(bf16[64,56,128]{2,1,0:T(8,128)(2,1)} %bitcast.19), calls=%async_computation.5 | async-start | bytes 1835008 | tf_op jit(solution)/shard_map/all_to_all | solution.py:327
  178.0 21.2 %all-to-all-start.6 = ((bf16[64,56,128]{2,1,0:T(8,128)(2,1)}), bf16[64,56,128]{2,1,0:T(8,128)(2,1)S(1)}, u32[]{:S(2)}, u32[]{:S(2)}) async-start(bf16[64,56,128]{2,1,0:T(8,128)(2,1)} %broadcast_in_dim.15), calls=%async_computation.6 | async-start | bytes 1835008 | tf_op jit(solution)/shard_map/all_to_all | solution.py:327
  184.4 14.8 %collective-permute-start.13 = (bf16[3,64,128]{2,1,0:T(8,128)(2,1)S(1)}, bf16[3,64,128]{2,1,0:T(8,128)(2,1)S(1)}, u32[]{:S(2)}, u32[]{:S(2)}) collective-permute-start(bf16[3,64,128]{2,1,0:T(8,128)(2,1)S(1)} %copy-done.25), channel_id=1, source_target_pairs={{0,1},{1,2},{2,3},{3,4},{4,5},{5,6},{6,7},{7,8},{8,9},{9,10},{10,1... | collective-permute-start | bytes 147464 | tf_op jit(solution)/shard_map/ppermute | solution.py:323
  186.4 12.8 %collective-permute-start.12 = (bf16[3,64,128]{2,1,0:T(8,128)(2,1)S(1)}, bf16[3,64,128]{2,1,0:T(8,128)(2,1)S(1)}, u32[]{:S(2)}, u32[]{:S(2)}) collective-permute-start(bf16[3,64,128]{2,1,0:T(8,128)(2,1)S(1)} %copy-done.23), channel_id=1, source_target_pairs={{1,0},{2,1},{3,2},{4,3},{5,4},{6,5},{7,6},{8,7},{9,8},{10,9},{11,1... | collective-permute-start | bytes 147464 | tf_op jit(solution)/shard_map/ppermute | solution.py:323
  199.2 13.1 %collective-permute-start.17 = (bf16[3584,128]{1,0:T(8,128)(2,1)S(1)}, bf16[3584,128]{1,0:T(8,128)(2,1)S(1)}, u32[]{:S(2)}, u32[]{:S(2)}) collective-permute-start(bf16[3584,128]{1,0:T(8,128)(2,1)S(1)} %bitcast.35), channel_id=1, source_target_pairs={{0,1},{1,0},{2,3},{3,2},{4,5},{5,4},{6,7},{7,6},{8,9},{9,8},{10,11... | collective-permute-start | bytes 2752520 | tf_op jit(solution)/shard_map/ppermute | solution.py:331
  199.2 6.5 %collective-permute-start.14 = (bf16[3,64,128]{2,1,0:T(8,128)(2,1)S(1)}, bf16[3,64,128]{2,1,0:T(8,128)(2,1)S(1)}, u32[]{:S(2)}, u32[]{:S(2)}) collective-permute-start(bf16[3,64,128]{2,1,0:T(8,128)(2,1)S(1)} %pad_maximum_fusion.6), channel_id=1, source_target_pairs={{16,0},{32,16},{48,32},{64,48},{80,64},{96,80},{112,96},{17,1},{33... | collective-permute-start | bytes 147464 | tf_op jit(solution)/shard_map/ppermute | solution.py:323
  202.9 8.1 %collective-permute-start.15 = (bf16[3,64,128]{2,1,0:T(8,128)(2,1)S(1)}, bf16[3,64,128]{2,1,0:T(8,128)(2,1)S(1)}, u32[]{:S(2)}, u32[]{:S(2)}) collective-permute-start(bf16[3,64,128]{2,1,0:T(8,128)(2,1)S(1)} %pad_maximum_fusion.7), channel_id=1, source_target_pairs={{0,16},{16,32},{32,48},{48,64},{64,80},{80,96},{96,112},{1,17},{17... | collective-permute-start | bytes 147464 | tf_op jit(solution)/shard_map/ppermute | solution.py:323
  (25 other events, 378.0 us)

commit v2 on v1

--- a/solution.py
+++ b/solution.py
@@ -22,10 +22,11 @@
 EPSILON = 1e-05
 F32 = jnp.float32
 BF16 = jnp.bfloat16
-COUNT, FACE, CORNER, VALID = 108, 109, 113, 117
+COUNT, FACE, CORNER, VALID, CORE_AT = 108, 109, 113, 117, 125
 NEIGHBOURS = ((-1, 0), (1, 0), (0, -1), (0, 1), (-1, -1), (-1, 1), (1, -1), (1, 1))
 CHUNK = 56
-PADDED = 64 * CHUNK
+HALF = TAPS * C // 2
+VMEM_BYTES = 16 << 20
 
 
 def shift_matrix():
@@ -141,58 +142,106 @@
     return center, lax.rsqrt(spread_sq + EPSILON)
 
 
-def place_received(ext, ux, lx, uy, ly):
-    for e, (ref, k) in enumerate(
-        ((ux, 0), (lx, 0), (uy, 0), (ly, 0), (uy, 1), (ly, 1), (uy, 2), (ly, 2))
+def received_bricks(ux, lx, uy, ly):
+    return (
+        ux.at[0], lx.at[0], uy.at[0], ly.at[0], uy.at[1], ly.at[1], uy.at[2], ly.at[2]
+    )
+
+
+def sends_of(face, corner, x_up, x_low, y_faces):
+    return (
+        (face(0), x_up.at[0]), (corner(0), x_up.at[1]), (corner(1), x_up.at[2]),
+        (face(1), x_low.at[0]), (corner(2), x_low.at[1]), (corner(3), x_low.at[2]),
+        (face(2), y_faces.at[0]), (face(3), y_faces.at[1]),
+    )
+
+
+def select_sends(meta, field, x_up, x_low, y_faces):
+    for entry, out in sends_of(
+        lambda k: meta[FACE + k], lambda k: meta[CORNER + k], x_up, x_low, y_faces
     ):
-        ext[NB + e] = ref[k]
-
-
-def send_kernel(meta, field, x_up, x_low, y_faces):
-    x_up[0] = field[meta[FACE]]
-    x_up[1] = field[meta[CORNER]]
-    x_up[2] = field[meta[CORNER + 1]]
-    x_low[0] = field[meta[FACE + 1]]
-    x_low[1] = field[meta[CORNER + 2]]
-    x_low[2] = field[meta[CORNER + 3]]
-    y_faces[0] = field[meta[FACE + 2]]
-    y_faces[1] = field[meta[FACE + 3]]
+        out[...] = field[entry]
+
+
+def send_kernel(face_far, corner_far, field, x_up, x_low, y_faces, face, corner, sems):
+    lists = [
+        pltpu.make_async_copy(face_far, face, sems.at[8]),
+        pltpu.make_async_copy(corner_far, corner, sems.at[9]),
+    ]
+    for copy in lists:
+        copy.start()
+    for copy in lists:
+        copy.wait()
+    copies = []
+    for n, (entry, out) in enumerate(
+        sends_of(lambda k: face[0, k, 0], lambda k: corner[0, k, 0], x_up, x_low, y_faces)
+    ):
+        copies.append(pltpu.make_async_copy(field.at[entry], out, sems.at[n]))
+        copies[-1].start()
+    for copy in copies:
+        copy.wait()
+
+
+def join_kernel(faces, first, second, up, low):
+    up[0] = faces[0]
+    up[1] = first[1]
+    up[2] = second[1]
+    low[0] = faces[1]
+    low[1] = first[2]
+    low[2] = second[2]
 
 
 def first_kernel(
-    meta, voxel_feats, ux, lx, uy, ly, weight, shift,
-    z_out, columns, sums, x_up, x_low, y_faces, ext, gathered,
+    meta, voxel_feats, ux, lx, uy, ly, weight_far, shift,
+    z_out, ext, sums, x_up, x_low, y_faces, weight, gathered, columns, sem,
 ):
+    fetch = pltpu.make_async_copy(weight_far, weight, sem)
+    fetch.start()
     ext[NB + 8] = jnp.zeros((64, C), BF16)
     for b in range(NB):
         keep = (meta[COUNT] > b).astype(F32)
         ext[b] = (voxel_feats[b].astype(F32) * keep).astype(BF16)
-    place_received(ext, ux, lx, uy, ly)
+    for e, brick in enumerate(received_bricks(ux, lx, uy, ly)):
+        keep = meta[VALID + e].astype(F32)
+        ext[NB + e] = (brick[...].astype(F32) * keep).astype(BF16)
     gather_columns(meta, ext, gathered, shift, columns)
+    fetch.wait()
     z = convolve(columns, weight)
     z_out[...] = z.reshape(NB, 64, C)
+    select_sends(meta, z_out, x_up, x_low, y_faces)
     masked = z * occupied_rows(meta)
-    write_sums(sums, rows_sum(masked), rows_sum(z * masked))
-    send_kernel(meta, z_out, x_up, x_low, y_faces)
+    row = lax.broadcasted_iota(jnp.int32, (8, C), 0) % 4
+    count = (64 * meta[COUNT]).astype(F32)
+    part = jnp.where(
+        row == 0, rows_sum(masked), jnp.where(row == 1, rows_sum(z * masked), count)
+    )
+    sums[...] = jnp.broadcast_to(part[None], (64, 8, C)).reshape(512, C)
 
 
 def second_kernel(
-    meta, got, voxels, z_one, ux, lx, uy, ly, norm, weight, shift,
-    z_out, columns, sums, xh_out, recip_out, field, ext, gathered,
+    meta, got, z_one, ux, lx, uy, ly, norm, weight_far, shift,
+    z_out, ext, sums, xh_out, recip_out, voxels_out, weight, gathered, columns, sem,
 ):
-    total, squares = read_sums(got)
-    center, recip = statistics(total, squares, voxels[0])
+    fetch = pltpu.make_async_copy(weight_far, weight, sem)
+    fetch.start()
+    row = lax.broadcasted_iota(jnp.int32, (8, C), 0) % 4
+    both = jnp.sum(got[...].reshape(64, 8, C), axis=0)
+    total = rows_sum(jnp.where(row == 0, both, 0.0))
+    squares = rows_sum(jnp.where(row == 1, both, 0.0))
+    voxels = rows_sum(jnp.where(row == 2, both, 0.0))
+    center, recip = statistics(total, squares, voxels)
     recip_out[...] = jnp.broadcast_to(recip, (8, C))
-    field[0:NB] = z_one[...]
-    place_received(field, ux, lx, uy, ly)
+    voxels_out[...] = jnp.broadcast_to(voxels, (8, C))
     for e in range(EXT - 1):
         keep = meta[COUNT] > e if e < NB else meta[VALID + e - NB] > 0
-        xh = (field[e] - center) * recip
+        field = z_one[e] if e < NB else received_bricks(ux, lx, uy, ly)[e - NB][...]
+        xh = (field - center) * recip
         xh_out[e] = xh
         u = norm[0:1] * xh + norm[2:3]
         ext[e] = (u * sigmoid(u) * keep.astype(F32)).astype(BF16)
     ext[EXT - 1] = jnp.zeros((64, C), BF16)
     gather_columns(meta, ext, gathered, shift, columns)
+    fetch.wait()
     z = convolve(columns, weight)
     z_out[...] = z
     masked = z * occupied_rows(meta)
@@ -203,7 +252,7 @@
     meta, got, voxels, z_two, voxel_feats, grad_out, norm, out_feats, dv_out, xh_out, recip_out, sums
 ):
     total, squares = read_sums(got)
-    center, recip = statistics(total, squares, voxels[0])
+    center, recip = statistics(total, squares, voxels[0:1])
     recip_out[...] = jnp.broadcast_to(recip, (8, C))
     occupied = occupied_rows(meta)
     xh = (z_two[...] - center) * recip
@@ -234,16 +283,19 @@
 
 
 def fourth_kernel(
-    meta, got, voxels, dv, xh_two, recip, xh_one, norm, weight, shift_back,
-    dz_out, own, y_low, y_up, x_faces, sums, grads, spread, moved, acc,
+    meta, got, voxels, dv, xh_two, recip, xh_one, norm, weight_far, shift_back,
+    dz_out, own, y_low, y_up, x_faces, sums, grads, weight, spread, moved, acc, sem,
 ):
+    fetch = pltpu.make_async_copy(weight_far, weight, sem)
+    fetch.start()
     total, cross = read_sums(got)
     grads[0:1] = cross
     grads[1:2] = total
     dz = norm_back(
-        dv[...], xh_two[...], norm[1:2], recip[0:1], total, cross, voxels[0], occupied_rows(meta)
+        dv[...], xh_two[...], norm[1:2], recip[0:1], total, cross, voxels[0:1], occupied_rows(meta)
     )
     dz_out[...] = dz
+    fetch.wait()
     convolve_back(meta, dz, weight, shift_back, spread, moved, acc)
     send_gradients(acc, own, y_low, y_up, x_faces)
     first = jnp.zeros((64, C), F32)
@@ -258,19 +310,20 @@
 
 
 def add_returned(meta, field, lx, ux, ly, uy):
-    for e, (ref, k, at) in enumerate(
-        (
-            (lx, 0, FACE), (ux, 0, FACE + 1), (ly, 0, FACE + 2), (uy, 0, FACE + 3),
-            (lx, 1, CORNER), (lx, 2, CORNER + 1), (ux, 1, CORNER + 2), (ux, 2, CORNER + 3),
-        )
+    for ref, k, at, neighbour in (
+        (lx, 0, FACE, 1), (ux, 0, FACE + 1, 0), (ly, 0, FACE + 2, 3), (uy, 0, FACE + 3, 2),
+        (lx, 1, CORNER, 7), (lx, 2, CORNER + 1, 6),
+        (ux, 1, CORNER + 2, 5), (ux, 2, CORNER + 3, 4),
     ):
-        field[meta[at]] += ref[k].astype(F32)
+        field[meta[at]] += ref[k].astype(F32) * meta[VALID + neighbour].astype(F32)
 
 
 def fifth_kernel(
-    meta, got, voxels, own_in, lx, ux, ly, uy, xh_one, recip, norm, weight, shift_back,
-    dz_out, own, y_low, y_up, x_faces, grads, field, spread, moved, acc,
+    meta, got, voxels, own_in, lx, ux, ly, uy, xh_one, recip, norm, weight_far, shift_back,
+    dz_out, own, y_low, y_up, x_faces, grads, weight, field, spread, moved, acc, sem,
 ):
+    fetch = pltpu.make_async_copy(weight_far, weight, sem)
+    fetch.start()
     total, cross = read_sums(got)
     grads[0:1] = cross
     grads[1:2] = total
@@ -279,20 +332,54 @@
     occupied = occupied_rows(meta)
     xh = xh_one[0:NB].reshape(ROWS, C)
     du = field[...].reshape(ROWS, C) * occupied * slope(norm[0:1] * xh + norm[2:3])
-    dz = norm_back(du, xh, norm[0:1], recip[0:1], total, cross, voxels[0], occupied)
+    dz = norm_back(du, xh, norm[0:1], recip[0:1], total, cross, voxels[0:1], occupied)
     dz_out[...] = dz
+    fetch.wait()
     convolve_back(meta, dz, weight, shift_back, spread, moved, acc)
     send_gradients(acc, own, y_low, y_up, x_faces)
 
 
-def taps_kernel(columns, dz, out):
+def taps_kernel(meta, ext, dz, shift, mine, other, gathered, columns, taps):
+    gather_columns(meta, ext, gathered, shift, columns)
     for k in range(TAPS):
-        out[k * C : (k + 1) * C, :] = lax.dot_general(
+        taps[k * C : (k + 1) * C, :] = lax.dot_general(
             columns[:, k * C : (k + 1) * C],
             dz[...],
             (((0,), (0,)), ((), ())),
             preferred_element_type=F32,
         )
+    here = meta[CORE_AT] == 0
+    mine[30:32] = jnp.zeros((2, CHUNK, C), F32)
+    other[30:32] = jnp.zeros((2, CHUNK, C), BF16)
+    for c in range(31):
+        full = min(CHUNK, HALF - CHUNK * c)
+        at = CHUNK * c
+        low = taps[at : at + full, :]
+        high = taps[HALF + at : HALF + at + full, :]
+        mine[c, 0:full, :] = jnp.where(here, low, high)
+        other[c, 0:full, :] = jnp.where(here, high, low).astype(BF16)
+
+
+def second_sum_kernel(mine, received, out):
+    out[...] = (mine[...] + received[...].astype(F32)).astype(BF16)
+
+
+def first_sum_kernel(mine, received, second, out):
+    out[0:32] = (mine[...] + received[...].astype(F32)).astype(BF16)
+    out[32:64] = second[...]
+
+
+def total_kernel(voxels, pieces, out):
+    total = jnp.sum(pieces[...].astype(F32), axis=0) / jnp.sqrt(voxels[0:1])
+    out[...] = jnp.broadcast_to(total.astype(BF16)[None], (64, CHUNK, C))
+
+
+def widen_kernel(meta, whole, partner, out):
+    same = meta[CORE_AT] == pl.program_id(1)
+    for c in range(31):
+        full = min(CHUNK, HALF - CHUNK * c)
+        half = jnp.where(same, whole[c].astype(F32), partner[c].astype(F32))
+        out[0, 0, CHUNK * c : CHUNK * c + full, :] = half[0:full]
 
 
 def last_kernel(meta, own, lx, ux, ly, uy, dv, grad_in, field):
@@ -302,25 +389,38 @@
     grad_in[...] = total.astype(BF16)
 
 
-def local(kernel, outs, ins, scratch=()):
+def local(kernel, outs, ins, scratch=(), far=()):
     vmem = pl.BlockSpec(memory_space=pltpu.VMEM)
     smem = pl.BlockSpec(memory_space=pltpu.SMEM)
-    specs = [smem if a.ndim == 1 else vmem for a in ins]
+    hbm = pl.BlockSpec(memory_space=pltpu.HBM)
+    specs = [hbm if n in far else smem if a.ndim == 1 else vmem for n, a in enumerate(ins)]
     return pl.pallas_call(
         kernel,
         out_shape=[jax.ShapeDtypeStruct(s, d) for s, d in outs],
         in_specs=specs,
         out_specs=[vmem] * len(outs),
-        scratch_shapes=[pltpu.VMEM(s, d) for s, d in scratch],
-        compiler_params=pltpu.CompilerParams(vmem_limit_bytes=48 << 20),
+        scratch_shapes=[pltpu.VMEM(*s) if isinstance(s, tuple) else s for s in scratch],
+        compiler_params=pltpu.CompilerParams(vmem_limit_bytes=VMEM_BYTES),
         name=kernel.__name__,
     )(*ins)
 
 
+def widen(meta, whole, partner):
+    block = pl.BlockSpec((32, CHUNK, C), lambda conv, half: (conv, 0, 0))
+    return pl.pallas_call(
+        widen_kernel,
+        grid=(2, 2),
+        out_shape=jax.ShapeDtypeStruct((2, 2, HALF, C), F32),
+        in_specs=[pl.BlockSpec(memory_space=pltpu.SMEM), block, block],
+        out_specs=pl.BlockSpec((1, 1, HALF, C), lambda conv, half: (conv, half, 0, 0)),
+        compiler_params=pltpu.CompilerParams(vmem_limit_bytes=VMEM_BYTES),
+        name="widen_kernel",
+    )(meta, whole, partner)
+
+
 def shifted(value, axis, by):
     length = lax.axis_size(axis)
-    pairs = [(i, i + by) for i in range(length) if 0 <= i + by < length]
-    return lax.ppermute(value, axis, pairs)
+    return lax.ppermute(value, axis, [(i, (i + by) % length) for i in range(length)])
 
 
 def exchange(value, axes):
@@ -329,21 +429,28 @@
 
 def swap(value):
     return lax.ppermute(value, CORE, [(0, 1), (1, 0)])
+
+
+def join(faces, first, second):
+    outs = [(first.shape, first.dtype)] * 2
+    return local(join_kernel, outs, [faces, first, second])
 
 
 def outward(x_up, x_low, y_faces):
     ux = shifted(x_up, GX, 1)
     lx = shifted(x_low, GX, -1)
-    uy = shifted(jnp.concatenate([y_faces[0:1], ux[1:2], lx[1:2]], axis=0), GY, 1)
-    ly = shifted(jnp.concatenate([y_faces[1:2], ux[2:3], lx[2:3]], axis=0), GY, -1)
+    up, low = join(y_faces, ux, lx)
+    uy = shifted(up, GY, 1)
+    ly = shifted(low, GY, -1)
     return ux, lx, uy, ly
 
 
 def homeward(y_low, y_up, x_faces):
     ly = shifted(y_low, GY, -1)
     uy = shifted(y_up, GY, 1)
-    lx = shifted(jnp.concatenate([x_faces[0:1], ly[1:2], uy[1:2]], axis=0), GX, -1)
-    ux = shifted(jnp.concatenate([x_faces[1:2], ly[2:3], uy[2:3]], axis=0), GX, 1)
+    low, up = join(x_faces, ly, uy)
+    lx = shifted(low, GX, -1)
+    ux = shifted(up, GX, 1)
     return lx, ux, ly, uy
 
 
@@ -371,6 +478,7 @@
             face_send.reshape(-1),
             corner_send.reshape(-1),
             inside.astype(jnp.int32),
+            lax.axis_index(CORE).reshape(1),
         ]
     )
     norm = jnp.concatenate([norm_gain, norm_shift], axis=0)
@@ -380,75 +488,82 @@
     flat_two = w_second.reshape(TAPS * C, C)
     brick = (64, C)
     three, two = (3,) + brick, (2,) + brick
-    wide = (ROWS, TAPS * C)
     rows = (ROWS, C)
     sums = ((2 * 128, C), F32)
     ext = ((EXT,) + brick, BF16)
+    list_xh = ((EXT - 1,) + brick, F32)
+    row8 = ((8, C), F32)
+    sem = pltpu.SemaphoreType.DMA
+    weight = ((TAPS * C, C), BF16)
     gathered = ((144, 6 * NB * C), BF16)
-
-    sends = local(send_kernel, [(three, BF16), (three, BF16), (two, BF16)], [meta, voxel_feats])
+    columns = ((ROWS, TAPS * C), BF16)
+    forward = [weight, gathered, columns, sem(())]
+    lists = [pltpu.SMEM((1, 4, 1), jnp.int32)] * 2
+
+    sends = local(
+        send_kernel,
+        [(three, BF16), (three, BF16), (two, BF16)],
+        [face_send, corner_send, voxel_feats],
+        lists + [sem((10,))],
+        far=(0, 1, 2),
+    )
     received = outward(*sends)
-    counts = exchange(jnp.broadcast_to(brick_count.astype(F32).reshape(1, 1), (128, C)), GX_GY)
-    voxels = (64.0 * jnp.sum(counts[:, 0])).reshape(1)
-    z_one, columns_one, part, *sends = local(
+    z_one, ext_one, part, *sends = local(
         first_kernel,
-        [((NB,) + brick, F32), (wide, BF16), sums, (three, F32), (three, F32), (two, F32)],
+        [((NB,) + brick, F32), ext, ((512, C), F32), (three, F32), (three, F32), (two, F32)],
         [meta, voxel_feats, *received, flat_one, shift],
-        [ext, gathered],
+        forward,
+        far=(6,),
     )
     received = outward(*sends)
     part = exchange(part, GX_GY)
-    z_two, columns_two, part, xh_one, recip_one = local(
+    z_two, ext_two, part, xh_one, recip_one, voxels = local(
         second_kernel,
-        [(rows, F32), (wide, BF16), sums, ((EXT - 1,) + brick, F32), ((8, C), F32)],
-        [meta, part, voxels, z_one, *received, norm, flat_two, shift],
-        [((EXT - 1,) + brick, F32), ext, gathered],
+        [(rows, F32), ext, sums, list_xh, row8, row8],
+        [meta, part, z_one, *received, norm, flat_two, shift],
+        forward,
+        far=(8,),
     )
     part = exchange(part, GX_GY)
     out_feats, dv, xh_two, recip_two, part = local(
         third_kernel,
-        [(rows, BF16), (rows, F32), (rows, F32), ((8, C), F32), sums],
+        [(rows, BF16), (rows, F32), (rows, F32), row8, sums],
         [meta, part, voxels, z_two, voxel_feats.reshape(rows), grad_out.reshape(rows), norm],
     )
     part = exchange(part, GX_GY)
-    back = [
-        ((3, ROWS, 9 * C), F32),
-        gathered,
-        ((EXT,) + brick, F32),
-    ]
+    back = [((3, ROWS, 9 * C), F32), gathered, ((EXT,) + brick, F32), sem(())]
     dz_two, own, y_low, y_up, x_faces, part, grads_two = local(
         fourth_kernel,
         [(rows, BF16), (rows, F32), (three, BF16), (three, BF16), (two, BF16), sums, ((2, C), F32)],
         [meta, part, voxels, dv, xh_two, recip_two, xh_one, norm, flat_two, shift_back],
-        back,
+        [weight] + back,
+        far=(8,),
     )
     returned = homeward(y_low, y_up, x_faces)
-    (dw_two,) = local(taps_kernel, [((TAPS * C, C), F32)], [columns_two, dz_two])
+    chunks = (32, CHUNK, C)
+    halves = [(chunks, F32), (chunks, BF16)]
+    products = [gathered, columns, ((TAPS * C, C), F32)]
+    mine, other = local(taps_kernel, halves, [meta, ext_two, dz_two, shift], products)
+    (second,) = local(second_sum_kernel, [(chunks, BF16)], [mine, swap(other)])
     part = exchange(part, GX_GY)
     dz_one, own, y_low, y_up, x_faces, grads_one = local(
         fifth_kernel,
         [(rows, BF16), (rows, F32), (three, BF16), (three, BF16), (two, BF16), ((2, C), F32)],
         [meta, part, voxels, own, *returned, xh_one, recip_one, norm, flat_one, shift_back],
-        [((NB,) + brick, F32)] + back,
+        [weight, ((NB,) + brick, F32)] + back,
+        far=(11,),
     )
     returned = homeward(y_low, y_up, x_faces)
-    (dw_one,) = local(taps_kernel, [((TAPS * C, C), F32)], [columns_one, dz_one])
+    mine, other = local(taps_kernel, halves, [meta, ext_one, dz_one, shift], products)
     (grad_in,) = local(
         last_kernel, [(rows, BF16)], [meta, own, *returned, dv], [((NB,) + brick, F32)]
     )
-    root = jnp.sqrt(voxels[0])
-    core = lax.axis_index(CORE)
-    mine = jnp.where(core == 0, dw_one, dw_two)
-    other = jnp.where(core == 0, dw_two, dw_one).astype(BF16)
-    mine = (mine + swap(other).astype(F32)).astype(BF16)
-    mine = jnp.pad(mine, ((0, PADDED - TAPS * C), (0, 0)))
-    pieces = exchange(mine, CHIPS).reshape(64, CHUNK, C)
-    piece = (jnp.sum(pieces.astype(F32), axis=0) / root).astype(BF16)
-    whole = exchange(jnp.broadcast_to(piece[None], (64, CHUNK, C)).reshape(PADDED, C), CHIPS)
-    partner = swap(whole)
-    first = jnp.where(core == 0, whole, partner)[: TAPS * C]
-    second = jnp.where(core == 0, partner, whole)[: TAPS * C]
-    weight_grads = jnp.stack([first, second]).reshape(2, TAPS, C, C).astype(F32)
+    both = ((64, CHUNK, C), BF16)
+    (part,) = local(first_sum_kernel, [both], [mine, swap(other), second])
+    (whole,) = local(total_kernel, [both], [voxels, exchange(part, CHIPS)])
+    whole = exchange(whole, CHIPS)
+    weight_grads = widen(meta, whole, swap(whole)).reshape(2, TAPS, C, C)
+    root = jnp.sqrt(voxels[0, 0])
     norm_grads = jnp.concatenate([grads_one, grads_two], axis=0) / root
     return (
         out_feats.reshape(NB, 64, C),

time: 217 us -> 194 us (0.89)
  starting transfers between devices: 99.9 us -> 44.2 us
  blocking collectives: 31.8 us -> 77.9 us
  waiting for transfers between devices: 43.3 us -> 28 us
  Pallas kernels: 14 us -> 21.1 us
  other arithmetic: 6.61 us -> 1.97 us
    all_to_all x2 -> x4, blocking collectives: 31.8 us -> 77.9 us  [exchange(): return lax.all_to_all(value, axes, 0, 0, tiled=True)]
    ppermute x16, starting transfers between devices: 58.2 us -> 26.7 us  [shifted(): lax.ppermute(value, axis, [(i, (i + by) % length) for i in range(length)])]
    all_to_all x5 -> x2, waiting for transfers between devices: 25.9 us -> 0.01 us  [exchange(): return lax.all_to_all(value, axes, 0, 0, tiled=True)]
    all_to_all x5 -> x2, starting transfers between devices: 40.9 us -> 17.4 us  [exchange(): return lax.all_to_all(value, axes, 0, 0, tiled=True)]
    ppermute x16, waiting for transfers between devices: 15.4 us -> 26.3 us  [shifted(): lax.ppermute(value, axis, [(i, (i + by) % length) for i in range(length)])]
    pallas_call x9 -> x16, Pallas kernels: 14 us -> 18.3 us  [local(): pl.pallas_call(kernel, out_shape=[jax.ShapeDtypeStruct(s, d) for s, d in...]
    pallas_call x0 -> x1, Pallas kernels: none -> 2.84 us  [widen(): pl.pallas_call(widen_kernel, grid=(2, 2), out_shape=jax.ShapeDtypeStruct(...]
    convert_element_type x4 -> x0, other arithmetic: 2.45 us -> none  [the longest x1 2.02 us: body(): weight_grads = jnp.stack([first, second]).reshape(2, TAPS, C, C).astype(F32)]
  transfers between devices with their start and end apart: 23 -> 21, of which waited for: 9 -> 11; matrix products, arithmetic and copies ran while one was open for 2% -> 2% of each run, Pallas kernels for 2% -> 4%
where the time goes in v2:
time: 194 us; the launch traced here: 191 us
  blocking collectives  77.9 us (40%)
  starting transfers between devices  44.2 us (23%)
  waiting for transfers between devices  28 us (14%)
  Pallas kernels  21.1 us (11%)
  local copies, waits for them, and re-layouts  15.4 us (8%)
  between operations  2.21 us (1%)
  other arithmetic  1.97 us (1%)
    all_to_all x4, blocking collectives, exchange(): return lax.all_to_all(value, axes, 0, 0, tiled=True)  77.9 us
    ppermute x16, starting transfers between devices, shifted(): lax.ppermute(value, axis, [(i, (i + by) % length) for i in range(length)])  26.7 us
    ppermute x16, waiting for transfers between devices, shifted(): lax.ppermute(value, axis, [(i, (i + by) % length) for i in range(length)])  26.3 us
    pallas_call x16, Pallas kernels, local(): pl.pallas_call(kernel, out_shape=[jax.ShapeDtypeStruct(s, d) for s, d in...  18.3 us
    all_to_all x2, starting transfers between devices, exchange(): return lax.all_to_all(value, axes, 0, 0, tiled=True)  17.4 us
    unnamed x46, local copies, waits for them, and re-layouts  13.4 us
  transfers between devices with their start and end apart: 21, of which 11 were waited for; matrix products, arithmetic and copies ran while one was open for 2% of the time, Pallas kernels for 4%

profile of v2, /device:TPU:34, one launch (start us, length us, event | category | flops | bytes accessed | tf_op | source)
XLA Modules:
  0.0 190.8 jit_solution(4907730605427965432)
XLA Ops:
  5.6 2.6 %collective-permute-start.1 = (bf16[3,64,128]{2,1,0:T(8,128)(2,1)S(1)}, bf16[3,64,128]{2,1,0:T(8,128)(2,1)S(1)}, u32[]{:S(2)}, u32[]{:S(2)}) collective-permute-start(bf16[3,64,128]{2,1,0:T(8,128)(2,1)S(1)} %get-tuple-element.50), channel_id=1, source_target_pairs={{0,112},{16,0},{32,16},{48,32},{64,48},{80,64},{96,80},{112,96},{1... | collective-permute-start | bytes 147464 | tf_op jit(solution)/shard_map/ppermute | solution.py:423
  8.1 2.1 %collective-permute-done.first.ux = bf16[3,64,128]{2,1,0:T(8,128)(2,1)S(1)} collective-permute-done((bf16[3,64,128]{2,1,0:T(8,128)(2,1)S(1)}, bf16[3,64,128]{2,1,0:T(8,128)(2,1)S(1)}, u32[]{:S(2)}, u32[]{:S(2)}) %collective-permute-start) | collective-permute-done | bytes 49184 | tf_op jit(solution)/shard_map/ppermute | solution.py:423
  10.3 4.1 %collective-permute-start.3 = (bf16[3,64,128]{2,1,0:T(8,128)(2,1)S(1)}, bf16[3,64,128]{2,1,0:T(8,128)(2,1)S(1)}, u32[]{:S(2)}, u32[]{:S(2)}) collective-permute-start(bf16[3,64,128]{2,1,0:T(8,128)(2,1)S(1)} %get-tuple-element.53), channel_id=1, source_target_pairs={{0,15},{1,0},{2,1},{3,2},{4,3},{5,4},{6,5},{7,6},{8,7},{9,8},{10,9... | collective-permute-start | bytes 147464 | tf_op jit(solution)/shard_map/ppermute | solution.py:423
  20.2 2.6 %first_kernel.1 = (f32[4,64,128]{2,1,0:T(8,128)S(1)}, bf16[13,64,128]{2,1,0:T(8,128)(2,1)S(1)}, f32[512,128]{1,0:T(8,128)}, f32[3,64,128]{2,1,0:T(8,128)S(1)}, f...) custom-call(s32[126]{0:T(128)S(1)} %concatenate.9.meta, bf16[4,64,128]{2,1,0:T(8,128)(2,1)S(1)} %copy-done.8, ...), custom_call_target="tpu_custom_call" | custom-call | tf_op jit(solution)/shard_map/first_kernel/pallas_call | solution.py:397
  23.5 11.2 %all-to-all-start = ((f32[128,4,128]{2,1,0:T(4,128)}), f32[128,4,128]{2,1,0:T(4,128)S(1)}, u32[]{:S(2)}, u32[]{:S(2)}) async-start(f32[128,4,128]{2,1,0:T(4,128)} %bitcast.4), calls=%async_computation | async-start | bytes 524288 | tf_op jit(solution)/shard_map/all_to_all | solution.py:427
  36.3 2.6 %collective-permute-start.5 = (f32[3,64,128]{2,1,0:T(8,128)S(1)}, f32[3,64,128]{2,1,0:T(8,128)S(1)}, u32[]{:S(2)}, u32[]{:S(2)}) collective-permute-start(f32[3,64,128]{2,1,0:T(8,128)S(1)} %get-tuple-element.57), channel_id=1, source_target_pairs={{0,112},{16,0},{32,16},{48,32},{64,48},{80,64},{96,80},{112,96},{1... | collective-permute-start | bytes 294920 | tf_op jit(solution)/shard_map/ppermute | solution.py:423
  38.9 4.4 %collective-permute-done.4.first.ux = f32[3,64,128]{2,1,0:T(8,128)S(1)} collective-permute-done((f32[3,64,128]{2,1,0:T(8,128)S(1)}, f32[3,64,128]{2,1,0:T(8,128)S(1)}, u32[]{:S(2)}, u32[]{:S(2)}) %collective-permute-start.4) | collective-permute-done | bytes 98336 | tf_op jit(solution)/shard_map/ppermute | solution.py:423
  43.4 4.1 %collective-permute-start.7 = (f32[3,64,128]{2,1,0:T(8,128)S(1)}, f32[3,64,128]{2,1,0:T(8,128)S(1)}, u32[]{:S(2)}, u32[]{:S(2)}) collective-permute-start(f32[3,64,128]{2,1,0:T(8,128)S(1)} %get-tuple-element.60), channel_id=1, source_target_pairs={{0,15},{1,0},{2,1},{3,2},{4,3},{5,4},{6,5},{7,6},{8,7},{9,8},{10,9... | collective-permute-start | bytes 294920 | tf_op jit(solution)/shard_map/ppermute | solution.py:423
  51.9 2.1 %second_kernel.1 = (f32[256,128]{1,0:T(8,128)S(1)}, bf16[13,64,128]{2,1,0:T(8,128)(2,1)S(1)}, f32[256,128]{1,0:T(8,128)S(1)}, f32[12,64,128]{2,1,0:T(8,128)S(1)}...) custom-call(s32[126]{0:T(128)S(1)} %concatenate.9.meta, f32[512,128]{1,0:T(8,128)S(1)} %bitcast.23, ...), custom_call_target="tpu_custom_call" | custom-call | tf_op jit(solution)/shard_map/second_kernel/pallas_call | solution.py:397
  54.0 18.1 %all_to_all.54 = f32[128,2,128]{2,1,0:T(2,128)S(1)} all-to-all(f32[128,2,128]{2,1,0:T(2,128)S(1)} %bitcast.28), channel_id=1, replica_groups=mesh['gx_0'=2,'gx_1'=4,'gy_0'=4,'gy_1'=2,'gy_2'=2] {'gx_0','gx_1','gy_0'..., dimensions={0} | all-to-all | bytes 262144 | tf_op jit(solution)/shard_map/all_to_all | solution.py:427
  73.5 14.2 %all_to_all.55 = f32[128,2,128]{2,1,0:T(2,128)S(1)} all-to-all(f32[128,2,128]{2,1,0:T(2,128)S(1)} %bitcast.29), channel_id=1, replica_groups=mesh['gx_0'=2,'gx_1'=4,'gy_0'=4,'gy_1'=2,'gy_2'=2] {'gx_0','gx_1','gy_0'..., dimensions={0} | all-to-all | bytes 262144 | tf_op jit(solution)/shard_map/all_to_all | solution.py:427
  87.6 3.2 %fourth_kernel.1 = (bf16[256,128]{1,0:T(8,128)(2,1)S(1)}, f32[256,128]{1,0:T(8,128)S(1)}, bf16[3,64,128]{2,1,0:T(8,128)(2,1)S(1)}, bf16[3,64,128]{2,1,0:T(8,128)...) custom-call(s32[126]{0:T(128)S(1)} %concatenate.9.meta, ...), custom_call_target="tpu_custom_call" | custom-call | tf_op jit(solution)/shard_map/fourth_kernel/pallas_call | solution.py:397
  92.0 6.2 %all-to-all-start.3 = ((f32[128,2,128]{2,1,0:T(2,128)}), f32[128,2,128]{2,1,0:T(2,128)S(1)}, u32[]{:S(2)}, u32[]{:S(2)}) async-start(f32[128,2,128]{2,1,0:T(2,128)} %bitcast.14), calls=%async_computation.3 | async-start | bytes 262144 | tf_op jit(solution)/shard_map/all_to_all | solution.py:427
  101.7 4.2 %collective-permute-done.9.second.uy = bf16[3,64,128]{2,1,0:T(8,128)(2,1)S(1)} collective-permute-done((bf16[3,64,128]{2,1,0:T(8,128)(2,1)S(1)}, bf16[3,64,128]{2,1,0:T(8,128)(2,1)S(1)}, u32[]{:S(2)}, u32[]{:S(2)}) %collective-permute-start.9) | collective-permute-done | bytes 49184 | tf_op jit(solution)/shard_map/ppermute | solution.py:423
  105.9 3.7 %collective-permute-start.10 = (bf16[3,64,128]{2,1,0:T(8,128)(2,1)S(1)}, bf16[3,64,128]{2,1,0:T(8,128)(2,1)S(1)}, u32[]{:S(2)}, u32[]{:S(2)}) collective-permute-start(bf16[3,64,128]{2,1,0:T(8,128)(2,1)S(1)} %get-tuple-element.75), channel_id=1, source_target_pairs={{0,112},{16,0},{32,16},{48,32},{64,48},{80,64},{96,80},{112,96},{1... | collective-permute-start | bytes 147464 | tf_op jit(solution)/shard_map/ppermute | solution.py:423
  111.4 2.4 %taps_kernel.3 = (f32[32,56,128]{2,1,0:T(8,128)S(1)}, bf16[32,56,128]{2,1,0:T(8,128)(2,1)}) custom-call(s32[126]{0:T(128)S(1)} %concatenate.9.meta, bf16[13,64,128]{2,1,0:T(8,128)(2,1)S(1)} %copy-done.14, bf16[256,128]{1,0:T(8,128)(2,1)S(1)} %copy-done.17, bf16[144,144]{1,0:T(8,128)(2,1)S(1)} %copy-done.6), custom_call_target="tpu_custom_call" | custom-call | tf_op jit(solution)/shard_map/taps_kernel/pallas_call | solution.py:397
  117.3 2.5 %fifth_kernel.1 = (bf16[256,128]{1,0:T(8,128)(2,1)S(1)}, f32[256,128]{1,0:T(8,128)S(1)}, bf16[3,64,128]{2,1,0:T(8,128)(2,1)S(1)}, bf16[3,64,128]{2,1,0:T(8,128)(...) custom-call(s32[126]{0:T(128)S(1)} %concatenate.9.meta, f32[256,128]{1,0:T(8,128)S(1)} %bitcast.25, ...), custom_call_target="tpu_custom_call" | custom-call | tf_op jit(solution)/shard_map/fifth_kernel/pallas_call | solution.py:397
  124.3 24.7 %all_to_all.56.pieces = bf16[64,56,128]{2,1,0:T(8,128)(2,1)S(1)} all-to-all(bf16[64,56,128]{2,1,0:T(8,128)(2,1)S(1)} %first_sum_kernel.1), channel_id=1, replica_groups=mesh['gx_0'=2,'gx_1'=4,'gy_0'=4,'gy_1'=2,'gy_2'=2] {'gx_0','gx_1','gy_0'..., dimensions={0} | all-to-all | bytes 1835008 | tf_op jit(solution)/shard_map/all_to_all | solution.py:427
  149.2 20.9 %all_to_all.57.whole = bf16[64,56,128]{2,1,0:T(8,128)(2,1)S(1)} all-to-all(bf16[64,56,128]{2,1,0:T(8,128)(2,1)S(1)} %total_kernel.1), channel_id=1, replica_groups=mesh['gx_0'=2,'gx_1'=4,'gy_0'=4,'gy_1'=2,'gy_2'=2] {'gx_0','gx_1','gy_0'..., dimensions={0} | all-to-all | bytes 1835008 | tf_op jit(solution)/shard_map/all_to_all | solution.py:427
  170.2 2.2 %collective-permute-start.12 = (bf16[3,64,128]{2,1,0:T(8,128)(2,1)S(1)}, bf16[3,64,128]{2,1,0:T(8,128)(2,1)S(1)}, u32[]{:S(2)}, u32[]{:S(2)}) collective-permute-start(bf16[3,64,128]{2,1,0:T(8,128)(2,1)S(1)} %get-tuple-element.80), channel_id=1, source_target_pairs={{0,15},{1,0},{2,1},{3,2},{4,3},{5,4},{6,5},{7,6},{8,7},{9,8},{10,9... | collective-permute-start | bytes 147464 | tf_op jit(solution)/shard_map/ppermute | solution.py:423
  174.1 4.2 %collective-permute-done.13.second.uy = bf16[3,64,128]{2,1,0:T(8,128)(2,1)S(1)} collective-permute-done((bf16[3,64,128]{2,1,0:T(8,128)(2,1)S(1)}, bf16[3,64,128]{2,1,0:T(8,128)(2,1)S(1)}, u32[]{:S(2)}, u32[]{:S(2)}) %collective-permute-start.13) | collective-permute-done | bytes 49184 | tf_op jit(solution)/shard_map/ppermute | solution.py:423
  178.3 2.2 %collective-permute-start.14 = (bf16[3,64,128]{2,1,0:T(8,128)(2,1)S(1)}, bf16[3,64,128]{2,1,0:T(8,128)(2,1)S(1)}, u32[]{:S(2)}, u32[]{:S(2)}) collective-permute-start(bf16[3,64,128]{2,1,0:T(8,128)(2,1)S(1)} %get-tuple-element.82), channel_id=1, source_target_pairs={{0,112},{16,0},{32,16},{48,32},{64,48},{80,64},{96,80},{112,96},{1... | collective-permute-start | bytes 147464 | tf_op jit(solution)/shard_map/ppermute | solution.py:423
  182.4 4.3 %collective-permute-done.15.ux = bf16[3,64,128]{2,1,0:T(8,128)(2,1)S(1)} collective-permute-done((bf16[3,64,128]{2,1,0:T(8,128)(2,1)S(1)}, bf16[3,64,128]{2,1,0:T(8,128)(2,1)S(1)}, u32[]{:S(2)}, u32[]{:S(2)}) %collective-permute-start.15) | collective-permute-done | bytes 49184 | tf_op jit(solution)/shard_map/ppermute | solution.py:423
  188.0 2.8 %widen_kernel.1 = f32[2,2,1728,128]{3,2,1,0:T(8,128)} custom-call(s32[126]{0:T(128)S(1)} %concatenate.9.meta, bf16[64,56,128]{2,1,0:T(8,128)(2,1)S(1)} %all_to_all.57.whole, bf16[64,56,128]{2,1,0:T(8,128)(2,1)S(1)} %collective-permute-done.18.partner), custom_call_target="tpu_custom_call" | custom-call | tf_op jit(solution)/shard_map/widen_kernel/pallas_call | solution.py:410
  (91 shorter events, 37.0 us)
Async XLA Ops:
  0.6 87.0 %copy-start.1 = (bf16[27,128,128]{2,1,0:T(8,128)(2,1)S(1)}, bf16[27,128,128]{2,1,0:T(8,128)(2,1)}, u32[]{:S(2)}) copy-start(bf16[27,128,128]{2,1,0:T(8,128)(2,1)} %param.16) | copy-start | bytes 2654212
  3.9 6.3 %collective-permute-start = (bf16[3,64,128]{2,1,0:T(8,128)(2,1)S(1)}, bf16[3,64,128]{2,1,0:T(8,128)(2,1)S(1)}, u32[]{:S(2)}, u32[]{:S(2)}) collective-permute-start(bf16[3,64,128]{2,1,0:T(8,128)(2,1)S(1)} %get-tuple-element.49), channel_id=1, source_target_pairs={{0,16},{16,32},{32,48},{48,64},{64,80},{80,96},{96,112},{112,0},{1... | collective-permute-start | bytes 147464 | tf_op jit(solution)/shard_map/ppermute | solution.py:423
  5.6 4.6 %collective-permute-start.1 = (bf16[3,64,128]{2,1,0:T(8,128)(2,1)S(1)}, bf16[3,64,128]{2,1,0:T(8,128)(2,1)S(1)}, u32[]{:S(2)}, u32[]{:S(2)}) collective-permute-start(bf16[3,64,128]{2,1,0:T(8,128)(2,1)S(1)} %get-tuple-element.50), channel_id=1, source_target_pairs={{0,112},{16,0},{32,16},{48,32},{64,48},{80,64},{96,80},{112,96},{1... | collective-permute-start | bytes 147464 | tf_op jit(solution)/shard_map/ppermute | solution.py:423
  10.2 7.1 %collective-permute-start.2 = (bf16[3,64,128]{2,1,0:T(8,128)(2,1)S(1)}, bf16[3,64,128]{2,1,0:T(8,128)(2,1)S(1)}, u32[]{:S(2)}, u32[]{:S(2)}) collective-permute-start(bf16[3,64,128]{2,1,0:T(8,128)(2,1)S(1)} %get-tuple-element.52), channel_id=1, source_target_pairs={{0,1},{1,2},{2,3},{3,4},{4,5},{5,6},{6,7},{7,8},{8,9},{9,10},{10,1... | collective-permute-start | bytes 147464 | tf_op jit(solution)/shard_map/ppermute | solution.py:423
  10.3 7.0 %collective-permute-start.3 = (bf16[3,64,128]{2,1,0:T(8,128)(2,1)S(1)}, bf16[3,64,128]{2,1,0:T(8,128)(2,1)S(1)}, u32[]{:S(2)}, u32[]{:S(2)}) collective-permute-start(bf16[3,64,128]{2,1,0:T(8,128)(2,1)S(1)} %get-tuple-element.53), channel_id=1, source_target_pairs={{0,15},{1,0},{2,1},{3,2},{4,3},{5,4},{6,5},{7,6},{8,7},{9,8},{10,9... | collective-permute-start | bytes 147464 | tf_op jit(solution)/shard_map/ppermute | solution.py:423
  20.2 89.5 %copy-start.6 = (bf16[144,144]{1,0:T(8,128)(2,1)S(1)}, bf16[144,144]{1,0:T(8,128)(2,1)}, u32[]{:S(2)}) copy-start(bf16[144,144]{1,0:T(8,128)(2,1)} %constant.39.clone.shift) | copy-start | bytes 124420
  20.2 96.3 %copy-start.3 = (bf16[27,128,128]{2,1,0:T(8,128)(2,1)S(1)}, bf16[27,128,128]{2,1,0:T(8,128)(2,1)}, u32[]{:S(2)}) copy-start(bf16[27,128,128]{2,1,0:T(8,128)(2,1)} %param.15) | copy-start | bytes 2654212
  23.5 26.4 %all-to-all-start = ((f32[128,4,128]{2,1,0:T(4,128)}), f32[128,4,128]{2,1,0:T(4,128)S(1)}, u32[]{:S(2)}, u32[]{:S(2)}) async-start(f32[128,4,128]{2,1,0:T(4,128)} %bitcast.4), calls=%async_computation | async-start | bytes 524288 | tf_op jit(solution)/shard_map/all_to_all | solution.py:427
  34.7 8.6 %collective-permute-start.4 = (f32[3,64,128]{2,1,0:T(8,128)S(1)}, f32[3,64,128]{2,1,0:T(8,128)S(1)}, u32[]{:S(2)}, u32[]{:S(2)}) collective-permute-start(f32[3,64,128]{2,1,0:T(8,128)S(1)} %get-tuple-element.56), channel_id=1, source_target_pairs={{0,16},{16,32},{32,48},{48,64},{64,80},{80,96},{96,112},{112,0},{1... | collective-permute-start | bytes 294920 | tf_op jit(solution)/shard_map/ppermute | solution.py:423
  36.3 7.0 %collective-permute-start.5 = (f32[3,64,128]{2,1,0:T(8,128)S(1)}, f32[3,64,128]{2,1,0:T(8,128)S(1)}, u32[]{:S(2)}, u32[]{:S(2)}) collective-permute-start(f32[3,64,128]{2,1,0:T(8,128)S(1)} %get-tuple-element.57), channel_id=1, source_target_pairs={{0,112},{16,0},{32,16},{48,32},{64,48},{80,64},{96,80},{112,96},{1... | collective-permute-start | bytes 294920 | tf_op jit(solution)/shard_map/ppermute | solution.py:423
  43.4 6.5 %collective-permute-start.6 = (f32[3,64,128]{2,1,0:T(8,128)S(1)}, f32[3,64,128]{2,1,0:T(8,128)S(1)}, u32[]{:S(2)}, u32[]{:S(2)}) collective-permute-start(f32[3,64,128]{2,1,0:T(8,128)S(1)} %get-tuple-element.59), channel_id=1, source_target_pairs={{0,1},{1,2},{2,3},{3,4},{4,5},{5,6},{6,7},{7,8},{8,9},{9,10},{10,1... | collective-permute-start | bytes 294920 | tf_op jit(solution)/shard_map/ppermute | solution.py:423
  43.4 6.4 %collective-permute-start.7 = (f32[3,64,128]{2,1,0:T(8,128)S(1)}, f32[3,64,128]{2,1,0:T(8,128)S(1)}, u32[]{:S(2)}, u32[]{:S(2)}) collective-permute-start(f32[3,64,128]{2,1,0:T(8,128)S(1)} %get-tuple-element.60), channel_id=1, source_target_pairs={{0,15},{1,0},{2,1},{3,2},{4,3},{5,4},{6,5},{7,6},{8,7},{9,8},{10,9... | collective-permute-start | bytes 294920 | tf_op jit(solution)/shard_map/ppermute | solution.py:423
  92.0 24.4 %all-to-all-start.3 = ((f32[128,2,128]{2,1,0:T(2,128)}), f32[128,2,128]{2,1,0:T(2,128)S(1)}, u32[]{:S(2)}, u32[]{:S(2)}) async-start(f32[128,2,128]{2,1,0:T(2,128)} %bitcast.14), calls=%async_computation.3 | async-start | bytes 262144 | tf_op jit(solution)/shard_map/all_to_all | solution.py:427
  98.2 3.5 %collective-permute-start.8 = (bf16[3,64,128]{2,1,0:T(8,128)(2,1)S(1)}, bf16[3,64,128]{2,1,0:T(8,128)(2,1)S(1)}, u32[]{:S(2)}, u32[]{:S(2)}) collective-permute-start(bf16[3,64,128]{2,1,0:T(8,128)(2,1)S(1)} %get-tuple-element.73), channel_id=1, source_target_pairs={{0,15},{1,0},{2,1},{3,2},{4,3},{5,4},{6,5},{7,6},{8,7},{9,8},{10,9... | collective-permute-start | bytes 147464 | tf_op jit(solution)/shard_map/ppermute | solution.py:423
  100.0 5.9 %collective-permute-start.9 = (bf16[3,64,128]{2,1,0:T(8,128)(2,1)S(1)}, bf16[3,64,128]{2,1,0:T(8,128)(2,1)S(1)}, u32[]{:S(2)}, u32[]{:S(2)}) collective-permute-start(bf16[3,64,128]{2,1,0:T(8,128)(2,1)S(1)} %get-tuple-element.74), channel_id=1, source_target_pairs={{0,1},{1,2},{2,3},{3,4},{4,5},{5,6},{6,7},{7,8},{8,9},{9,10},{10,1... | collective-permute-start | bytes 147464 | tf_op jit(solution)/shard_map/ppermute | solution.py:423
  105.9 7.9 %collective-permute-start.10 = (bf16[3,64,128]{2,1,0:T(8,128)(2,1)S(1)}, bf16[3,64,128]{2,1,0:T(8,128)(2,1)S(1)}, u32[]{:S(2)}, u32[]{:S(2)}) collective-permute-start(bf16[3,64,128]{2,1,0:T(8,128)(2,1)S(1)} %get-tuple-element.75), channel_id=1, source_target_pairs={{0,112},{16,0},{32,16},{48,32},{64,48},{80,64},{96,80},{112,96},{1... | collective-permute-start | bytes 147464 | tf_op jit(solution)/shard_map/ppermute | solution.py:423
  109.6 6.2 %collective-permute-start.11 = (bf16[3,64,128]{2,1,0:T(8,128)(2,1)S(1)}, bf16[3,64,128]{2,1,0:T(8,128)(2,1)S(1)}, u32[]{:S(2)}, u32[]{:S(2)}) collective-permute-start(bf16[3,64,128]{2,1,0:T(8,128)(2,1)S(1)} %get-tuple-element.76), channel_id=1, source_target_pairs={{0,16},{16,32},{32,48},{48,64},{64,80},{80,96},{96,112},{112,0},{1... | collective-permute-start | bytes 147464 | tf_op jit(solution)/shard_map/ppermute | solution.py:423
  113.8 8.6 %collective-permute-start.17 = (bf16[32,56,128]{2,1,0:T(8,128)(2,1)}, bf16[32,56,128]{2,1,0:T(8,128)(2,1)S(1)}, u32[]{:S(2)}, u32[]{:S(2)}) collective-permute-start(bf16[32,56,128]{2,1,0:T(8,128)(2,1)} %get-tuple-element.91), channel_id=1, source_target_pairs={{0,1},{1,0},{2,3},{3,2},{4,5},{5,4},{6,7},{7,6},{8,9},{9,8},{10,11... | collective-permute-start | bytes 1376264 | tf_op jit(solution)/shard_map/ppermute | solution.py:431
  122.3 1.9 collective-permute-start.16
  170.2 17.8 %collective-permute-start.18 = (bf16[64,56,128]{2,1,0:T(8,128)(2,1)S(1)}, bf16[64,56,128]{2,1,0:T(8,128)(2,1)S(1)}, u32[]{:S(2)}, u32[]{:S(2)}) collective-permute-start(bf16[64,56,128]{2,1,0:T(8,128)(2,1)S(1)} %all_to_all.57.whole), channel_id=1, source_target_pairs={{0,1},{1,0},{2,3},{3,2},{4,5},{5,4},{6,7},{7,6},{8,9},{9,8},{10,11... | collective-permute-start | bytes 2752520 | tf_op jit(solution)/shard_map/ppermute | solution.py:431
  170.2 3.9 %collective-permute-start.12 = (bf16[3,64,128]{2,1,0:T(8,128)(2,1)S(1)}, bf16[3,64,128]{2,1,0:T(8,128)(2,1)S(1)}, u32[]{:S(2)}, u32[]{:S(2)}) collective-permute-start(bf16[3,64,128]{2,1,0:T(8,128)(2,1)S(1)} %get-tuple-element.80), channel_id=1, source_target_pairs={{0,15},{1,0},{2,1},{3,2},{4,3},{5,4},{6,5},{7,6},{8,7},{9,8},{10,9... | collective-permute-start | bytes 147464 | tf_op jit(solution)/shard_map/ppermute | solution.py:423
  172.3 5.9 %collective-permute-start.13 = (bf16[3,64,128]{2,1,0:T(8,128)(2,1)S(1)}, bf16[3,64,128]{2,1,0:T(8,128)(2,1)S(1)}, u32[]{:S(2)}, u32[]{:S(2)}) collective-permute-start(bf16[3,64,128]{2,1,0:T(8,128)(2,1)S(1)} %get-tuple-element.81), channel_id=1, source_target_pairs={{0,1},{1,2},{2,3},{3,4},{4,5},{5,6},{6,7},{7,8},{8,9},{9,10},{10,1... | collective-permute-start | bytes 147464 | tf_op jit(solution)/shard_map/ppermute | solution.py:423
  178.3 4.2 %collective-permute-start.14 = (bf16[3,64,128]{2,1,0:T(8,128)(2,1)S(1)}, bf16[3,64,128]{2,1,0:T(8,128)(2,1)S(1)}, u32[]{:S(2)}, u32[]{:S(2)}) collective-permute-start(bf16[3,64,128]{2,1,0:T(8,128)(2,1)S(1)} %get-tuple-element.82), channel_id=1, source_target_pairs={{0,112},{16,0},{32,16},{48,32},{64,48},{80,64},{96,80},{112,96},{1... | collective-permute-start | bytes 147464 | tf_op jit(solution)/shard_map/ppermute | solution.py:423
  180.5 6.2 %collective-permute-start.15 = (bf16[3,64,128]{2,1,0:T(8,128)(2,1)S(1)}, bf16[3,64,128]{2,1,0:T(8,128)(2,1)S(1)}, u32[]{:S(2)}, u32[]{:S(2)}) collective-permute-start(bf16[3,64,128]{2,1,0:T(8,128)(2,1)S(1)} %get-tuple-element.83), channel_id=1, source_target_pairs={{0,16},{16,32},{32,48},{48,64},{64,80},{80,96},{96,112},{112,0},{1... | collective-permute-start | bytes 147464 | tf_op jit(solution)/shard_map/ppermute | solution.py:423
  (19 other events, 259.0 us)

commit v3 on v2

--- a/solution.py
+++ b/solution.py
@@ -1,5 +1,3 @@
-import functools
-
 import jax
 import jax.numpy as jnp
 import numpy as np
@@ -26,20 +24,21 @@
 NEIGHBOURS = ((-1, 0), (1, 0), (0, -1), (0, 1), (-1, -1), (-1, 1), (1, -1), (1, 1))
 CHUNK = 56
 HALF = TAPS * C // 2
-VMEM_BYTES = 16 << 20
-
-
-def shift_matrix():
-    shift = np.zeros((9, 4, 4, 9, 4, 4), np.float32)
-    for b in range(3):
-        for c in range(3):
-            for q in range(4):
-                for r in range(4):
-                    y, x = q + b - 1, r + c - 1
-                    ob = 0 if y < 0 else 1 if y < 4 else 2
-                    oc = 0 if x < 0 else 1 if x < 4 else 2
-                    shift[3 * b + c, q, r, 3 * ob + oc, y % 4, x % 4] = 1.0
-    return shift.reshape(144, 144)
+VMEM_BYTES = 64 << 20
+SPARE = 48 << 20
+
+
+def shift_matrix(flipped):
+    def places(axis):
+        at = lax.broadcasted_iota(jnp.int32, (144, 144), axis)
+        major = (at >= 48).astype(jnp.int32) + (at >= 96).astype(jnp.int32)
+        minor = (at >> 4) - 3 * major
+        return major, minor, (at >> 2) & 3, at & 3
+
+    b, c, q, r = places(1 if flipped else 0)
+    ob, oc, qs, rs = places(0 if flipped else 1)
+    hit = (4 * ob + qs == q + b + 3) & (4 * oc + rs == r + c + 3)
+    return hit.astype(F32).astype(BF16)
 
 
 def sources():
@@ -60,7 +59,8 @@
     return (brick < meta[COUNT]).astype(F32)
 
 
-def gather_columns(meta, ext, gathered, shift, columns):
+def gather_columns(meta, ext, gathered, columns):
+    shift = shift_matrix(False)
     for b in range(NB):
         for plane, oa, source in sources():
             for d in range(9):
@@ -70,7 +70,7 @@
                 ]
     for b in range(NB):
         moved = jnp.dot(
-            shift[...], gathered[:, 6 * b * C : 6 * (b + 1) * C], preferred_element_type=F32
+            shift, gathered[:, 6 * b * C : 6 * (b + 1) * C], preferred_element_type=F32
         ).astype(BF16)
         for a in range(3):
             for p in range(4):
@@ -85,7 +85,8 @@
     return jnp.dot(columns[...], weight[...], preferred_element_type=F32)
 
 
-def convolve_back(meta, dz, weight, shift_back, spread, moved, acc):
+def convolve_back(meta, dz, weight, spread, moved, acc):
+    shift_back = shift_matrix(True)
     for a in range(3):
         spread[a] = lax.dot_general(
             dz,
@@ -108,7 +109,7 @@
                 )
     for b in range(NB):
         home = jnp.dot(
-            shift_back[...], moved[:, 6 * b * C : 6 * (b + 1) * C], preferred_element_type=F32
+            shift_back, moved[:, 6 * b * C : 6 * (b + 1) * C], preferred_element_type=F32
         )
         for plane, oa, source in sources():
             for d in range(9):
@@ -163,23 +164,9 @@
         out[...] = field[entry]
 
 
-def send_kernel(face_far, corner_far, field, x_up, x_low, y_faces, face, corner, sems):
-    lists = [
-        pltpu.make_async_copy(face_far, face, sems.at[8]),
-        pltpu.make_async_copy(corner_far, corner, sems.at[9]),
-    ]
-    for copy in lists:
-        copy.start()
-    for copy in lists:
-        copy.wait()
-    copies = []
-    for n, (entry, out) in enumerate(
-        sends_of(lambda k: face[0, k, 0], lambda k: corner[0, k, 0], x_up, x_low, y_faces)
-    ):
-        copies.append(pltpu.make_async_copy(field.at[entry], out, sems.at[n]))
-        copies[-1].start()
-    for copy in copies:
-        copy.wait()
+def send_kernel(lists, field, x_up, x_low, y_faces):
+    for entry, out in sends_of(lambda k: lists[k], lambda k: lists[4 + k], x_up, x_low, y_faces):
+        out[...] = field[entry]
 
 
 def join_kernel(faces, first, second, up, low):
@@ -192,7 +179,7 @@
 
 
 def first_kernel(
-    meta, voxel_feats, ux, lx, uy, ly, weight_far, shift,
+    meta, voxel_feats, ux, lx, uy, ly, weight_far,
     z_out, ext, sums, x_up, x_low, y_faces, weight, gathered, columns, sem,
 ):
     fetch = pltpu.make_async_copy(weight_far, weight, sem)
@@ -204,7 +191,7 @@
     for e, brick in enumerate(received_bricks(ux, lx, uy, ly)):
         keep = meta[VALID + e].astype(F32)
         ext[NB + e] = (brick[...].astype(F32) * keep).astype(BF16)
-    gather_columns(meta, ext, gathered, shift, columns)
+    gather_columns(meta, ext, gathered, columns)
     fetch.wait()
     z = convolve(columns, weight)
     z_out[...] = z.reshape(NB, 64, C)
@@ -219,7 +206,7 @@
 
 
 def second_kernel(
-    meta, got, z_one, ux, lx, uy, ly, norm, weight_far, shift,
+    meta, got, z_one, ux, lx, uy, ly, norm, weight_far,
     z_out, ext, sums, xh_out, recip_out, voxels_out, weight, gathered, columns, sem,
 ):
     fetch = pltpu.make_async_copy(weight_far, weight, sem)
@@ -240,7 +227,7 @@
         u = norm[0:1] * xh + norm[2:3]
         ext[e] = (u * sigmoid(u) * keep.astype(F32)).astype(BF16)
     ext[EXT - 1] = jnp.zeros((64, C), BF16)
-    gather_columns(meta, ext, gathered, shift, columns)
+    gather_columns(meta, ext, gathered, columns)
     fetch.wait()
     z = convolve(columns, weight)
     z_out[...] = z
@@ -283,7 +270,7 @@
 
 
 def fourth_kernel(
-    meta, got, voxels, dv, xh_two, recip, xh_one, norm, weight_far, shift_back,
+    meta, got, voxels, dv, xh_two, recip, xh_one, norm, weight_far,
     dz_out, own, y_low, y_up, x_faces, sums, grads, weight, spread, moved, acc, sem,
 ):
     fetch = pltpu.make_async_copy(weight_far, weight, sem)
@@ -296,7 +283,7 @@
     )
     dz_out[...] = dz
     fetch.wait()
-    convolve_back(meta, dz, weight, shift_back, spread, moved, acc)
+    convolve_back(meta, dz, weight, spread, moved, acc)
     send_gradients(acc, own, y_low, y_up, x_faces)
     first = jnp.zeros((64, C), F32)
     second = jnp.zeros((64, C), F32)
@@ -319,7 +306,7 @@
 
 
 def fifth_kernel(
-    meta, got, voxels, own_in, lx, ux, ly, uy, xh_one, recip, norm, weight_far, shift_back,
+    meta, got, voxels, own_in, lx, ux, ly, uy, xh_one, recip, norm, weight_far,
     dz_out, own, y_low, y_up, x_faces, grads, weight, field, spread, moved, acc, sem,
 ):
     fetch = pltpu.make_async_copy(weight_far, weight, sem)
@@ -335,12 +322,12 @@
     dz = norm_back(du, xh, norm[0:1], recip[0:1], total, cross, voxels[0:1], occupied)
     dz_out[...] = dz
     fetch.wait()
-    convolve_back(meta, dz, weight, shift_back, spread, moved, acc)
+    convolve_back(meta, dz, weight, spread, moved, acc)
     send_gradients(acc, own, y_low, y_up, x_faces)
 
 
-def taps_kernel(meta, ext, dz, shift, mine, other, gathered, columns, taps):
-    gather_columns(meta, ext, gathered, shift, columns)
+def taps_kernel(meta, ext, dz, mine, other, gathered, columns, taps):
+    gather_columns(meta, ext, gathered, columns)
     for k in range(TAPS):
         taps[k * C : (k + 1) * C, :] = lax.dot_general(
             columns[:, k * C : (k + 1) * C],
@@ -389,7 +376,7 @@
     grad_in[...] = total.astype(BF16)
 
 
-def local(kernel, outs, ins, scratch=(), far=()):
+def local(kernel, outs, ins, scratch=(), far=(), spare=SPARE):
     vmem = pl.BlockSpec(memory_space=pltpu.VMEM)
     smem = pl.BlockSpec(memory_space=pltpu.SMEM)
     hbm = pl.BlockSpec(memory_space=pltpu.HBM)
@@ -400,8 +387,7 @@
         in_specs=specs,
         out_specs=[vmem] * len(outs),
         scratch_shapes=[pltpu.VMEM(*s) if isinstance(s, tuple) else s for s in scratch],
-        compiler_params=pltpu.CompilerParams(vmem_limit_bytes=VMEM_BYTES),
-        name=kernel.__name__,
+        compiler_params=pltpu.CompilerParams(vmem_limit_bytes=VMEM_BYTES - spare),
     )(*ins)
 
 
@@ -413,7 +399,7 @@
         out_shape=jax.ShapeDtypeStruct((2, 2, HALF, C), F32),
         in_specs=[pl.BlockSpec(memory_space=pltpu.SMEM), block, block],
         out_specs=pl.BlockSpec((1, 1, HALF, C), lambda conv, half: (conv, half, 0, 0)),
-        compiler_params=pltpu.CompilerParams(vmem_limit_bytes=VMEM_BYTES),
+        compiler_params=pltpu.CompilerParams(vmem_limit_bytes=16 << 20),
         name="widen_kernel",
     )(meta, whole, partner)
 
@@ -436,25 +422,25 @@
     return local(join_kernel, outs, [faces, first, second])
 
 
+def pair(first, second, axis, by):
+    return shifted(first, axis, by), shifted(second, axis, -by)
+
+
 def outward(x_up, x_low, y_faces):
-    ux = shifted(x_up, GX, 1)
-    lx = shifted(x_low, GX, -1)
+    ux, lx = pair(x_up, x_low, GX, 1)
     up, low = join(y_faces, ux, lx)
-    uy = shifted(up, GY, 1)
-    ly = shifted(low, GY, -1)
+    uy, ly = pair(up, low, GY, 1)
     return ux, lx, uy, ly
 
 
 def homeward(y_low, y_up, x_faces):
-    ly = shifted(y_low, GY, -1)
-    uy = shifted(y_up, GY, 1)
+    ly, uy = pair(y_low, y_up, GY, -1)
     low, up = join(x_faces, ly, uy)
-    lx = shifted(low, GX, -1)
-    ux = shifted(up, GX, 1)
+    lx, ux = pair(low, up, GX, -1)
     return lx, ux, ly, uy
 
 
-def body(
+def program(
     voxel_feats,
     w_first,
     w_second,
@@ -466,6 +452,7 @@
     face_send,
     corner_send,
 ):
+    lists = jnp.concatenate([face_send.reshape(4), corner_send.reshape(4)])
     i = lax.axis_index(GX)
     j = lax.axis_index(GY)
     dx = np.array([d[0] for d in NEIGHBOURS], np.int32)
@@ -475,15 +462,12 @@
         [
             kernel_map.reshape(-1),
             brick_count,
-            face_send.reshape(-1),
-            corner_send.reshape(-1),
+            lists,
             inside.astype(jnp.int32),
             lax.axis_index(CORE).reshape(1),
         ]
     )
     norm = jnp.concatenate([norm_gain, norm_shift], axis=0)
-    shift = jnp.asarray(shift_matrix(), BF16)
-    shift_back = jnp.asarray(shift_matrix().T, BF16)
     flat_one = w_first.reshape(TAPS * C, C)
     flat_two = w_second.reshape(TAPS * C, C)
     brick = (64, C)
@@ -498,20 +482,15 @@
     gathered = ((144, 6 * NB * C), BF16)
     columns = ((ROWS, TAPS * C), BF16)
     forward = [weight, gathered, columns, sem(())]
-    lists = [pltpu.SMEM((1, 4, 1), jnp.int32)] * 2
 
     sends = local(
-        send_kernel,
-        [(three, BF16), (three, BF16), (two, BF16)],
-        [face_send, corner_send, voxel_feats],
-        lists + [sem((10,))],
-        far=(0, 1, 2),
+        send_kernel, [(three, BF16), (three, BF16), (two, BF16)], [lists, voxel_feats]
     )
     received = outward(*sends)
     z_one, ext_one, part, *sends = local(
         first_kernel,
         [((NB,) + brick, F32), ext, ((512, C), F32), (three, F32), (three, F32), (two, F32)],
-        [meta, voxel_feats, *received, flat_one, shift],
+        [meta, voxel_feats, *received, flat_one],
         forward,
         far=(6,),
     )
@@ -520,7 +499,7 @@
     z_two, ext_two, part, xh_one, recip_one, voxels = local(
         second_kernel,
         [(rows, F32), ext, sums, list_xh, row8, row8],
-        [meta, part, z_one, *received, norm, flat_two, shift],
+        [meta, part, z_one, *received, norm, flat_two],
         forward,
         far=(8,),
     )
@@ -535,7 +514,7 @@
     dz_two, own, y_low, y_up, x_faces, part, grads_two = local(
         fourth_kernel,
         [(rows, BF16), (rows, F32), (three, BF16), (three, BF16), (two, BF16), sums, ((2, C), F32)],
-        [meta, part, voxels, dv, xh_two, recip_two, xh_one, norm, flat_two, shift_back],
+        [meta, part, voxels, dv, xh_two, recip_two, xh_one, norm, flat_two],
         [weight] + back,
         far=(8,),
     )
@@ -543,18 +522,18 @@
     chunks = (32, CHUNK, C)
     halves = [(chunks, F32), (chunks, BF16)]
     products = [gathered, columns, ((TAPS * C, C), F32)]
-    mine, other = local(taps_kernel, halves, [meta, ext_two, dz_two, shift], products)
+    mine, other = local(taps_kernel, halves, [meta, ext_two, dz_two], products)
     (second,) = local(second_sum_kernel, [(chunks, BF16)], [mine, swap(other)])
     part = exchange(part, GX_GY)
     dz_one, own, y_low, y_up, x_faces, grads_one = local(
         fifth_kernel,
         [(rows, BF16), (rows, F32), (three, BF16), (three, BF16), (two, BF16), ((2, C), F32)],
-        [meta, part, voxels, own, *returned, xh_one, recip_one, norm, flat_one, shift_back],
+        [meta, part, voxels, own, *returned, xh_one, recip_one, norm, flat_one],
         [weight, ((NB,) + brick, F32)] + back,
         far=(11,),
     )
     returned = homeward(y_low, y_up, x_faces)
-    mine, other = local(taps_kernel, halves, [meta, ext_one, dz_one, shift], products)
+    mine, other = local(taps_kernel, halves, [meta, ext_one, dz_one], products)
     (grad_in,) = local(
         last_kernel, [(rows, BF16)], [meta, own, *returned, dv], [((NB,) + brick, F32)]
     )
@@ -588,4 +567,4 @@
         P(GX_GY, None, None),
     )
     out_specs = (P(GX_GY, None, None), P(GX_GY, None, None), P(), P())
-    return jax.shard_map(body, mesh=split, in_specs=in_specs, out_specs=out_specs, check_vma=False)
+    return jax.shard_map(program, mesh=split, in_specs=in_specs, out_specs=out_specs, check_vma=False)

time: 194 us -> 194 us (level)
    unnamed x46 -> x54, local copies, waits for them, and re-layouts: 13.4 us -> 13 us
where the time goes in v3:
time: 194 us; the launch traced here: 191 us
  blocking collectives  78.6 us (41%)
  starting transfers between devices  44.2 us (23%)
  waiting for transfers between devices  27.4 us (14%)
  Pallas kernels  20.6 us (11%)
  local copies, waits for them, and re-layouts  15 us (8%)
  other arithmetic  2.79 us (1%)
  between operations  2.24 us (1%)
    all_to_all x4, blocking collectives, exchange(): return lax.all_to_all(value, axes, 0, 0, tiled=True)  78.6 us
    ppermute x16, starting transfers between devices, shifted(): lax.ppermute(value, axis, [(i, (i + by) % length) for i in range(length)])  26.7 us
    ppermute x16, waiting for transfers between devices, shifted(): lax.ppermute(value, axis, [(i, (i + by) % length) for i in range(length)])  25.7 us
    pallas_call x16, Pallas kernels, local(): pl.pallas_call(kernel, out_shape=[jax.ShapeDtypeStruct(s, d) for s, d in...  17.7 us
    all_to_all x2, starting transfers between devices, exchange(): return lax.all_to_all(value, axes, 0, 0, tiled=True)  17.4 us
    unnamed x54, local copies, waits for them, and re-layouts  13 us
  transfers between devices with their start and end apart: 21, of which 11 were waited for; matrix products, arithmetic and copies ran while one was open for 2% of the time, Pallas kernels for 4%

profile of v3, /device:TPU:34, one launch (start us, length us, event | category | flops | bytes accessed | tf_op | source)
XLA Modules:
  0.0 190.8 jit_solution(13863821424469857075)
XLA Ops:
  4.5 2.6 %collective-permute-start.1 = (bf16[3,64,128]{2,1,0:T(8,128)(2,1)S(1)}, bf16[3,64,128]{2,1,0:T(8,128)(2,1)S(1)}, u32[]{:S(2)}, u32[]{:S(2)}) collective-permute-start(bf16[3,64,128]{2,1,0:T(8,128)(2,1)S(1)} %get-tuple-element.50), channel_id=1, source_target_pairs={{0,112},{16,0},{32,16},{48,32},{64,48},{80,64},{96,80},{112,96},{1... | collective-permute-start | bytes 147464 | tf_op jit(solution)/shard_map/ppermute | solution.py:409
  7.1 2.1 %collective-permute-done.first.ux = bf16[3,64,128]{2,1,0:T(8,128)(2,1)S(1)} collective-permute-done((bf16[3,64,128]{2,1,0:T(8,128)(2,1)S(1)}, bf16[3,64,128]{2,1,0:T(8,128)(2,1)S(1)}, u32[]{:S(2)}, u32[]{:S(2)}) %collective-permute-start) | collective-permute-done | bytes 49184 | tf_op jit(solution)/shard_map/ppermute | solution.py:409
  9.2 4.1 %collective-permute-start.3 = (bf16[3,64,128]{2,1,0:T(8,128)(2,1)S(1)}, bf16[3,64,128]{2,1,0:T(8,128)(2,1)S(1)}, u32[]{:S(2)}, u32[]{:S(2)}) collective-permute-start(bf16[3,64,128]{2,1,0:T(8,128)(2,1)S(1)} %get-tuple-element.53), channel_id=1, source_target_pairs={{0,15},{1,0},{2,1},{3,2},{4,3},{5,4},{6,5},{7,6},{8,7},{9,8},{10,9... | collective-permute-start | bytes 147464 | tf_op jit(solution)/shard_map/ppermute | solution.py:409
  18.2 2.6 %shard_map.149 = (f32[4,64,128]{2,1,0:T(8,128)S(1)}, bf16[13,64,128]{2,1,0:T(8,128)(2,1)S(1)}, f32[512,128]{1,0:T(8,128)}, f32[3,64,128]{2,1,0:T(8,128)S(1)}, f3...) custom-call(s32[126]{0:T(128)S(1)} %concatenate.13.meta, bf16[4,64,128]{2,1,0:T(8,128)(2,1)S(1)} %copy-done.5, ...), custom_call_target="tpu_custom_call" | custom-call | tf_op jit(solution)/shard_map/pallas_call | solution.py:384
  20.8 11.2 %all-to-all-start = ((f32[128,4,128]{2,1,0:T(4,128)}), f32[128,4,128]{2,1,0:T(4,128)S(1)}, u32[]{:S(2)}, u32[]{:S(2)}) async-start(f32[128,4,128]{2,1,0:T(4,128)} %bitcast.4), calls=%async_computation | async-start | bytes 524288 | tf_op jit(solution)/shard_map/all_to_all | solution.py:413
  33.7 2.6 %collective-permute-start.5 = (f32[3,64,128]{2,1,0:T(8,128)S(1)}, f32[3,64,128]{2,1,0:T(8,128)S(1)}, u32[]{:S(2)}, u32[]{:S(2)}) collective-permute-start(f32[3,64,128]{2,1,0:T(8,128)S(1)} %get-tuple-element.57), channel_id=1, source_target_pairs={{0,112},{16,0},{32,16},{48,32},{64,48},{80,64},{96,80},{112,96},{1... | collective-permute-start | bytes 294920 | tf_op jit(solution)/shard_map/ppermute | solution.py:409
  36.3 4.4 %collective-permute-done.4.first.ux = f32[3,64,128]{2,1,0:T(8,128)S(1)} collective-permute-done((f32[3,64,128]{2,1,0:T(8,128)S(1)}, f32[3,64,128]{2,1,0:T(8,128)S(1)}, u32[]{:S(2)}, u32[]{:S(2)}) %collective-permute-start.4) | collective-permute-done | bytes 98336 | tf_op jit(solution)/shard_map/ppermute | solution.py:409
  40.8 4.1 %collective-permute-start.7 = (f32[3,64,128]{2,1,0:T(8,128)S(1)}, f32[3,64,128]{2,1,0:T(8,128)S(1)}, u32[]{:S(2)}, u32[]{:S(2)}) collective-permute-start(f32[3,64,128]{2,1,0:T(8,128)S(1)} %get-tuple-element.60), channel_id=1, source_target_pairs={{0,15},{1,0},{2,1},{3,2},{4,3},{5,4},{6,5},{7,6},{8,7},{9,8},{10,9... | collective-permute-start | bytes 294920 | tf_op jit(solution)/shard_map/ppermute | solution.py:409
  48.4 2.1 %shard_map.151 = (f32[256,128]{1,0:T(8,128)S(1)}, bf16[13,64,128]{2,1,0:T(8,128)(2,1)S(1)}, f32[256,128]{1,0:T(8,128)S(1)}, f32[12,64,128]{2,1,0:T(8,128)S(1)}, ...) custom-call(s32[126]{0:T(128)S(1)} %concatenate.13.meta, f32[512,128]{1,0:T(8,128)S(1)} %bitcast.23, ...), custom_call_target="tpu_custom_call" | custom-call | tf_op jit(solution)/shard_map/pallas_call | solution.py:384
  50.5 18.1 %all_to_all.54 = f32[128,2,128]{2,1,0:T(2,128)S(1)} all-to-all(f32[128,2,128]{2,1,0:T(2,128)S(1)} %bitcast.28), channel_id=1, replica_groups=mesh['gx_0'=2,'gx_1'=4,'gy_0'=4,'gy_1'=2,'gy_2'=2] {'gx_0','gx_1','gy_0'..., dimensions={0} | all-to-all | bytes 262144 | tf_op jit(solution)/shard_map/all_to_all | solution.py:413
  69.9 14.2 %all_to_all.55 = f32[128,2,128]{2,1,0:T(2,128)S(1)} all-to-all(f32[128,2,128]{2,1,0:T(2,128)S(1)} %bitcast.29), channel_id=1, replica_groups=mesh['gx_0'=2,'gx_1'=4,'gy_0'=4,'gy_1'=2,'gy_2'=2] {'gx_0','gx_1','gy_0'..., dimensions={0} | all-to-all | bytes 262144 | tf_op jit(solution)/shard_map/all_to_all | solution.py:413
  85.4 3.1 %shard_map.153 = (bf16[256,128]{1,0:T(8,128)(2,1)S(1)}, f32[256,128]{1,0:T(8,128)S(1)}, bf16[3,64,128]{2,1,0:T(8,128)(2,1)S(1)}, bf16[3,64,128]{2,1,0:T(8,128)(2...) custom-call(s32[126]{0:T(128)S(1)} %copy-done.15, f32[256,128]{1,0:T(8,128)S(1)} %bitcast.26, ...), custom_call_target="tpu_custom_call" | custom-call | tf_op jit(solution)/shard_map/pallas_call | solution.py:384
  89.8 6.2 %all-to-all-start.3 = ((f32[128,2,128]{2,1,0:T(2,128)}), f32[128,2,128]{2,1,0:T(2,128)S(1)}, u32[]{:S(2)}, u32[]{:S(2)}) async-start(f32[128,2,128]{2,1,0:T(2,128)} %bitcast.14), calls=%async_computation.3 | async-start | bytes 262144 | tf_op jit(solution)/shard_map/all_to_all | solution.py:413
  99.5 4.2 %collective-permute-done.9.second.uy = bf16[3,64,128]{2,1,0:T(8,128)(2,1)S(1)} collective-permute-done((bf16[3,64,128]{2,1,0:T(8,128)(2,1)S(1)}, bf16[3,64,128]{2,1,0:T(8,128)(2,1)S(1)}, u32[]{:S(2)}, u32[]{:S(2)}) %collective-permute-start.9) | collective-permute-done | bytes 49184 | tf_op jit(solution)/shard_map/ppermute | solution.py:409
  103.7 3.7 %collective-permute-start.10 = (bf16[3,64,128]{2,1,0:T(8,128)(2,1)S(1)}, bf16[3,64,128]{2,1,0:T(8,128)(2,1)S(1)}, u32[]{:S(2)}, u32[]{:S(2)}) collective-permute-start(bf16[3,64,128]{2,1,0:T(8,128)(2,1)S(1)} %get-tuple-element.75), channel_id=1, source_target_pairs={{0,112},{16,0},{32,16},{48,32},{64,48},{80,64},{96,80},{112,96},{1... | collective-permute-start | bytes 147464 | tf_op jit(solution)/shard_map/ppermute | solution.py:409
  109.8 2.4 %shard_map.159 = (f32[32,56,128]{2,1,0:T(8,128)S(1)}, bf16[32,56,128]{2,1,0:T(8,128)(2,1)}) custom-call(s32[126]{0:T(128)S(1)} %copy-done.16, bf16[13,64,128]{2,1,0:T(8,128)(2,1)S(1)} %copy-done.8, bf16[256,128]{1,0:T(8,128)(2,1)S(1)} %copy-done.13), custom_call_target="tpu_custom_call" | custom-call | tf_op jit(solution)/shard_map/pallas_call | solution.py:384
  117.7 2.4 %shard_map.155 = (bf16[256,128]{1,0:T(8,128)(2,1)S(1)}, f32[256,128]{1,0:T(8,128)S(1)}, bf16[3,64,128]{2,1,0:T(8,128)(2,1)S(1)}, bf16[3,64,128]{2,1,0:T(8,128)(2...) custom-call(s32[126]{0:T(128)S(1)} %copy-done.17, f32[256,128]{1,0:T(8,128)S(1)} %bitcast.25, ...), custom_call_target="tpu_custom_call" | custom-call | tf_op jit(solution)/shard_map/pallas_call | solution.py:384
  123.7 25.4 %all_to_all.56.pieces = bf16[64,56,128]{2,1,0:T(8,128)(2,1)S(1)} all-to-all(bf16[64,56,128]{2,1,0:T(8,128)(2,1)S(1)} %shard_map.161), channel_id=1, replica_groups=mesh['gx_0'=2,'gx_1'=4,'gy_0'=4,'gy_1'=2,'gy_2'=2] {'gx_0','gx_1','gy_0'..., dimensions={0} | all-to-all | bytes 1835008 | tf_op jit(solution)/shard_map/all_to_all | solution.py:413
  149.3 20.9 %all_to_all.57.whole = bf16[64,56,128]{2,1,0:T(8,128)(2,1)S(1)} all-to-all(bf16[64,56,128]{2,1,0:T(8,128)(2,1)S(1)} %shard_map.162), channel_id=1, replica_groups=mesh['gx_0'=2,'gx_1'=4,'gy_0'=4,'gy_1'=2,'gy_2'=2] {'gx_0','gx_1','gy_0'..., dimensions={0} | all-to-all | bytes 1835008 | tf_op jit(solution)/shard_map/all_to_all | solution.py:413
  170.2 2.2 %collective-permute-start.12 = (bf16[3,64,128]{2,1,0:T(8,128)(2,1)S(1)}, bf16[3,64,128]{2,1,0:T(8,128)(2,1)S(1)}, u32[]{:S(2)}, u32[]{:S(2)}) collective-permute-start(bf16[3,64,128]{2,1,0:T(8,128)(2,1)S(1)} %get-tuple-element.80), channel_id=1, source_target_pairs={{0,15},{1,0},{2,1},{3,2},{4,3},{5,4},{6,5},{7,6},{8,7},{9,8},{10,9... | collective-permute-start | bytes 147464 | tf_op jit(solution)/shard_map/ppermute | solution.py:409
  174.1 4.2 %collective-permute-done.13.second.uy = bf16[3,64,128]{2,1,0:T(8,128)(2,1)S(1)} collective-permute-done((bf16[3,64,128]{2,1,0:T(8,128)(2,1)S(1)}, bf16[3,64,128]{2,1,0:T(8,128)(2,1)S(1)}, u32[]{:S(2)}, u32[]{:S(2)}) %collective-permute-start.13) | collective-permute-done | bytes 49184 | tf_op jit(solution)/shard_map/ppermute | solution.py:409
  178.3 2.2 %collective-permute-start.14 = (bf16[3,64,128]{2,1,0:T(8,128)(2,1)S(1)}, bf16[3,64,128]{2,1,0:T(8,128)(2,1)S(1)}, u32[]{:S(2)}, u32[]{:S(2)}) collective-permute-start(bf16[3,64,128]{2,1,0:T(8,128)(2,1)S(1)} %get-tuple-element.82), channel_id=1, source_target_pairs={{0,112},{16,0},{32,16},{48,32},{64,48},{80,64},{96,80},{112,96},{1... | collective-permute-start | bytes 147464 | tf_op jit(solution)/shard_map/ppermute | solution.py:409
  182.5 4.3 %collective-permute-done.15.ux = bf16[3,64,128]{2,1,0:T(8,128)(2,1)S(1)} collective-permute-done((bf16[3,64,128]{2,1,0:T(8,128)(2,1)S(1)}, bf16[3,64,128]{2,1,0:T(8,128)(2,1)S(1)}, u32[]{:S(2)}, u32[]{:S(2)}) %collective-permute-start.15) | collective-permute-done | bytes 49184 | tf_op jit(solution)/shard_map/ppermute | solution.py:409
  188.0 2.8 %widen_kernel.1 = f32[2,2,1728,128]{3,2,1,0:T(8,128)} custom-call(s32[126]{0:T(128)S(1)} %copy-done.17, bf16[64,56,128]{2,1,0:T(8,128)(2,1)S(1)} %all_to_all.57.whole, bf16[64,56,128]{2,1,0:T(8,128)(2,1)S(1)} %collective-permute-done.18.partner), custom_call_target="tpu_custom_call" | custom-call | tf_op jit(solution)/shard_map/widen_kernel/pallas_call | solution.py:396
  (100 shorter events, 36.5 us)
Async XLA Ops:
  0.6 83.5 %copy-start.1 = (bf16[27,128,128]{2,1,0:T(8,128)(2,1)S(1)}, bf16[27,128,128]{2,1,0:T(8,128)(2,1)}, u32[]{:S(2)}) copy-start(bf16[27,128,128]{2,1,0:T(8,128)(2,1)} %param.14) | copy-start | bytes 2654212
  2.9 6.3 %collective-permute-start = (bf16[3,64,128]{2,1,0:T(8,128)(2,1)S(1)}, bf16[3,64,128]{2,1,0:T(8,128)(2,1)S(1)}, u32[]{:S(2)}, u32[]{:S(2)}) collective-permute-start(bf16[3,64,128]{2,1,0:T(8,128)(2,1)S(1)} %get-tuple-element.49), channel_id=1, source_target_pairs={{0,16},{16,32},{32,48},{48,64},{64,80},{80,96},{96,112},{112,0},{1... | collective-permute-start | bytes 147464 | tf_op jit(solution)/shard_map/ppermute | solution.py:409
  4.5 4.6 %collective-permute-start.1 = (bf16[3,64,128]{2,1,0:T(8,128)(2,1)S(1)}, bf16[3,64,128]{2,1,0:T(8,128)(2,1)S(1)}, u32[]{:S(2)}, u32[]{:S(2)}) collective-permute-start(bf16[3,64,128]{2,1,0:T(8,128)(2,1)S(1)} %get-tuple-element.50), channel_id=1, source_target_pairs={{0,112},{16,0},{32,16},{48,32},{64,48},{80,64},{96,80},{112,96},{1... | collective-permute-start | bytes 147464 | tf_op jit(solution)/shard_map/ppermute | solution.py:409
  9.2 7.1 %collective-permute-start.2 = (bf16[3,64,128]{2,1,0:T(8,128)(2,1)S(1)}, bf16[3,64,128]{2,1,0:T(8,128)(2,1)S(1)}, u32[]{:S(2)}, u32[]{:S(2)}) collective-permute-start(bf16[3,64,128]{2,1,0:T(8,128)(2,1)S(1)} %get-tuple-element.52), channel_id=1, source_target_pairs={{0,1},{1,2},{2,3},{3,4},{4,5},{5,6},{6,7},{7,8},{8,9},{9,10},{10,1... | collective-permute-start | bytes 147464 | tf_op jit(solution)/shard_map/ppermute | solution.py:409
  9.2 7.0 %collective-permute-start.3 = (bf16[3,64,128]{2,1,0:T(8,128)(2,1)S(1)}, bf16[3,64,128]{2,1,0:T(8,128)(2,1)S(1)}, u32[]{:S(2)}, u32[]{:S(2)}) collective-permute-start(bf16[3,64,128]{2,1,0:T(8,128)(2,1)S(1)} %get-tuple-element.53), channel_id=1, source_target_pairs={{0,15},{1,0},{2,1},{3,2},{4,3},{5,4},{6,5},{7,6},{8,7},{9,8},{10,9... | collective-permute-start | bytes 147464 | tf_op jit(solution)/shard_map/ppermute | solution.py:409
  16.2 67.9 %copy-start.14 = (s32[126]{0:T(128)}, s32[126]{0:T(128)S(1)}, u32[]{:S(2)}) copy-start(s32[126]{0:T(128)S(1)} %concatenate.13.meta) | copy-start | bytes 1516
  18.2 96.0 %copy-start.3 = (bf16[27,128,128]{2,1,0:T(8,128)(2,1)S(1)}, bf16[27,128,128]{2,1,0:T(8,128)(2,1)}, u32[]{:S(2)}) copy-start(bf16[27,128,128]{2,1,0:T(8,128)(2,1)} %param.13) | copy-start | bytes 2654212
  20.8 26.4 %all-to-all-start = ((f32[128,4,128]{2,1,0:T(4,128)}), f32[128,4,128]{2,1,0:T(4,128)S(1)}, u32[]{:S(2)}, u32[]{:S(2)}) async-start(f32[128,4,128]{2,1,0:T(4,128)} %bitcast.4), calls=%async_computation | async-start | bytes 524288 | tf_op jit(solution)/shard_map/all_to_all | solution.py:413
  32.1 8.6 %collective-permute-start.4 = (f32[3,64,128]{2,1,0:T(8,128)S(1)}, f32[3,64,128]{2,1,0:T(8,128)S(1)}, u32[]{:S(2)}, u32[]{:S(2)}) collective-permute-start(f32[3,64,128]{2,1,0:T(8,128)S(1)} %get-tuple-element.56), channel_id=1, source_target_pairs={{0,16},{16,32},{32,48},{48,64},{64,80},{80,96},{96,112},{112,0},{1... | collective-permute-start | bytes 294920 | tf_op jit(solution)/shard_map/ppermute | solution.py:409
  33.7 7.0 %collective-permute-start.5 = (f32[3,64,128]{2,1,0:T(8,128)S(1)}, f32[3,64,128]{2,1,0:T(8,128)S(1)}, u32[]{:S(2)}, u32[]{:S(2)}) collective-permute-start(f32[3,64,128]{2,1,0:T(8,128)S(1)} %get-tuple-element.57), channel_id=1, source_target_pairs={{0,112},{16,0},{32,16},{48,32},{64,48},{80,64},{96,80},{112,96},{1... | collective-permute-start | bytes 294920 | tf_op jit(solution)/shard_map/ppermute | solution.py:409
  40.7 6.5 %collective-permute-start.6 = (f32[3,64,128]{2,1,0:T(8,128)S(1)}, f32[3,64,128]{2,1,0:T(8,128)S(1)}, u32[]{:S(2)}, u32[]{:S(2)}) collective-permute-start(f32[3,64,128]{2,1,0:T(8,128)S(1)} %get-tuple-element.59), channel_id=1, source_target_pairs={{0,1},{1,2},{2,3},{3,4},{4,5},{5,6},{6,7},{7,8},{8,9},{9,10},{10,1... | collective-permute-start | bytes 294920 | tf_op jit(solution)/shard_map/ppermute | solution.py:409
  40.8 6.4 %collective-permute-start.7 = (f32[3,64,128]{2,1,0:T(8,128)S(1)}, f32[3,64,128]{2,1,0:T(8,128)S(1)}, u32[]{:S(2)}, u32[]{:S(2)}) collective-permute-start(f32[3,64,128]{2,1,0:T(8,128)S(1)} %get-tuple-element.60), channel_id=1, source_target_pairs={{0,15},{1,0},{2,1},{3,2},{4,3},{5,4},{6,5},{7,6},{8,7},{9,8},{10,9... | collective-permute-start | bytes 294920 | tf_op jit(solution)/shard_map/ppermute | solution.py:409
  89.8 24.4 %all-to-all-start.3 = ((f32[128,2,128]{2,1,0:T(2,128)}), f32[128,2,128]{2,1,0:T(2,128)S(1)}, u32[]{:S(2)}, u32[]{:S(2)}) async-start(f32[128,2,128]{2,1,0:T(2,128)} %bitcast.14), calls=%async_computation.3 | async-start | bytes 262144 | tf_op jit(solution)/shard_map/all_to_all | solution.py:413
  96.0 3.5 %collective-permute-start.8 = (bf16[3,64,128]{2,1,0:T(8,128)(2,1)S(1)}, bf16[3,64,128]{2,1,0:T(8,128)(2,1)S(1)}, u32[]{:S(2)}, u32[]{:S(2)}) collective-permute-start(bf16[3,64,128]{2,1,0:T(8,128)(2,1)S(1)} %get-tuple-element.73), channel_id=1, source_target_pairs={{0,15},{1,0},{2,1},{3,2},{4,3},{5,4},{6,5},{7,6},{8,7},{9,8},{10,9... | collective-permute-start | bytes 147464 | tf_op jit(solution)/shard_map/ppermute | solution.py:409
  97.7 5.9 %collective-permute-start.9 = (bf16[3,64,128]{2,1,0:T(8,128)(2,1)S(1)}, bf16[3,64,128]{2,1,0:T(8,128)(2,1)S(1)}, u32[]{:S(2)}, u32[]{:S(2)}) collective-permute-start(bf16[3,64,128]{2,1,0:T(8,128)(2,1)S(1)} %get-tuple-element.74), channel_id=1, source_target_pairs={{0,1},{1,2},{2,3},{3,4},{4,5},{5,6},{6,7},{7,8},{8,9},{9,10},{10,1... | collective-permute-start | bytes 147464 | tf_op jit(solution)/shard_map/ppermute | solution.py:409
  103.7 8.6 %collective-permute-start.10 = (bf16[3,64,128]{2,1,0:T(8,128)(2,1)S(1)}, bf16[3,64,128]{2,1,0:T(8,128)(2,1)S(1)}, u32[]{:S(2)}, u32[]{:S(2)}) collective-permute-start(bf16[3,64,128]{2,1,0:T(8,128)(2,1)S(1)} %get-tuple-element.75), channel_id=1, source_target_pairs={{0,112},{16,0},{32,16},{48,32},{64,48},{80,64},{96,80},{112,96},{1... | collective-permute-start | bytes 147464 | tf_op jit(solution)/shard_map/ppermute | solution.py:409
  107.4 6.2 %collective-permute-start.11 = (bf16[3,64,128]{2,1,0:T(8,128)(2,1)S(1)}, bf16[3,64,128]{2,1,0:T(8,128)(2,1)S(1)}, u32[]{:S(2)}, u32[]{:S(2)}) collective-permute-start(bf16[3,64,128]{2,1,0:T(8,128)(2,1)S(1)} %get-tuple-element.76), channel_id=1, source_target_pairs={{0,16},{16,32},{32,48},{48,64},{64,80},{80,96},{96,112},{112,0},{1... | collective-permute-start | bytes 147464 | tf_op jit(solution)/shard_map/ppermute | solution.py:409
  112.2 9.6 %collective-permute-start.17 = (bf16[32,56,128]{2,1,0:T(8,128)(2,1)}, bf16[32,56,128]{2,1,0:T(8,128)(2,1)S(1)}, u32[]{:S(2)}, u32[]{:S(2)}) collective-permute-start(bf16[32,56,128]{2,1,0:T(8,128)(2,1)} %get-tuple-element.91), channel_id=1, source_target_pairs={{0,1},{1,0},{2,3},{3,2},{4,5},{5,4},{6,7},{7,6},{8,9},{9,8},{10,11... | collective-permute-start | bytes 1376264 | tf_op jit(solution)/shard_map/ppermute | solution.py:417
  121.7 1.9 collective-permute-start.16
  170.2 17.8 %collective-permute-start.18 = (bf16[64,56,128]{2,1,0:T(8,128)(2,1)S(1)}, bf16[64,56,128]{2,1,0:T(8,128)(2,1)S(1)}, u32[]{:S(2)}, u32[]{:S(2)}) collective-permute-start(bf16[64,56,128]{2,1,0:T(8,128)(2,1)S(1)} %all_to_all.57.whole), channel_id=1, source_target_pairs={{0,1},{1,0},{2,3},{3,2},{4,5},{5,4},{6,7},{7,6},{8,9},{9,8},{10,11... | collective-permute-start | bytes 2752520 | tf_op jit(solution)/shard_map/ppermute | solution.py:417
  170.2 3.9 %collective-permute-start.12 = (bf16[3,64,128]{2,1,0:T(8,128)(2,1)S(1)}, bf16[3,64,128]{2,1,0:T(8,128)(2,1)S(1)}, u32[]{:S(2)}, u32[]{:S(2)}) collective-permute-start(bf16[3,64,128]{2,1,0:T(8,128)(2,1)S(1)} %get-tuple-element.80), channel_id=1, source_target_pairs={{0,15},{1,0},{2,1},{3,2},{4,3},{5,4},{6,5},{7,6},{8,7},{9,8},{10,9... | collective-permute-start | bytes 147464 | tf_op jit(solution)/shard_map/ppermute | solution.py:409
  172.4 5.9 %collective-permute-start.13 = (bf16[3,64,128]{2,1,0:T(8,128)(2,1)S(1)}, bf16[3,64,128]{2,1,0:T(8,128)(2,1)S(1)}, u32[]{:S(2)}, u32[]{:S(2)}) collective-permute-start(bf16[3,64,128]{2,1,0:T(8,128)(2,1)S(1)} %get-tuple-element.81), channel_id=1, source_target_pairs={{0,1},{1,2},{2,3},{3,4},{4,5},{5,6},{6,7},{7,8},{8,9},{9,10},{10,1... | collective-permute-start | bytes 147464 | tf_op jit(solution)/shard_map/ppermute | solution.py:409
  178.3 4.2 %collective-permute-start.14 = (bf16[3,64,128]{2,1,0:T(8,128)(2,1)S(1)}, bf16[3,64,128]{2,1,0:T(8,128)(2,1)S(1)}, u32[]{:S(2)}, u32[]{:S(2)}) collective-permute-start(bf16[3,64,128]{2,1,0:T(8,128)(2,1)S(1)} %get-tuple-element.82), channel_id=1, source_target_pairs={{0,112},{16,0},{32,16},{48,32},{64,48},{80,64},{96,80},{112,96},{1... | collective-permute-start | bytes 147464 | tf_op jit(solution)/shard_map/ppermute | solution.py:409
  180.5 6.2 %collective-permute-start.15 = (bf16[3,64,128]{2,1,0:T(8,128)(2,1)S(1)}, bf16[3,64,128]{2,1,0:T(8,128)(2,1)S(1)}, u32[]{:S(2)}, u32[]{:S(2)}) collective-permute-start(bf16[3,64,128]{2,1,0:T(8,128)(2,1)S(1)} %get-tuple-element.83), channel_id=1, source_target_pairs={{0,16},{16,32},{32,48},{48,64},{64,80},{80,96},{96,112},{112,0},{1... | collective-permute-start | bytes 147464 | tf_op jit(solution)/shard_map/ppermute | solution.py:409
  (24 other events, 300.4 us)

commit v4 on v3

--- a/solution.py
+++ b/solution.py
@@ -24,8 +24,20 @@
 NEIGHBOURS = ((-1, 0), (1, 0), (0, -1), (0, 1), (-1, -1), (-1, 1), (1, -1), (1, 1))
 CHUNK = 56
 HALF = TAPS * C // 2
-VMEM_BYTES = 64 << 20
-SPARE = 48 << 20
+VMEM_BYTES = 16 << 20
+
+
+def row_of(k):
+    return slice(k, k + 1)
+
+
+VOXELS = row_of(0)
+RECIP = (row_of(1), row_of(2))
+NORM_ROWS = slice(4, 8)
+GAIN = (row_of(4), row_of(5))
+SHIFT = (row_of(6), row_of(7))
+CROSS = (row_of(8), row_of(9))
+TOTAL = (row_of(10), row_of(11))
 
 
 def shift_matrix(flipped):
@@ -164,7 +176,8 @@
         out[...] = field[entry]
 
 
-def send_kernel(lists, field, x_up, x_low, y_faces):
+def send_kernel(lists, field, x_up, x_low, y_faces, kept):
+    kept[...] = field[...]
     for entry, out in sends_of(lambda k: lists[k], lambda k: lists[4 + k], x_up, x_low, y_faces):
         out[...] = field[entry]
 
@@ -207,7 +220,7 @@
 
 def second_kernel(
     meta, got, z_one, ux, lx, uy, ly, norm, weight_far,
-    z_out, ext, sums, xh_out, recip_out, voxels_out, weight, gathered, columns, sem,
+    z_out, ext, sums, xh_out, consts, weight, gathered, columns, sem,
 ):
     fetch = pltpu.make_async_copy(weight_far, weight, sem)
     fetch.start()
@@ -217,8 +230,10 @@
     squares = rows_sum(jnp.where(row == 1, both, 0.0))
     voxels = rows_sum(jnp.where(row == 2, both, 0.0))
     center, recip = statistics(total, squares, voxels)
-    recip_out[...] = jnp.broadcast_to(recip, (8, C))
-    voxels_out[...] = jnp.broadcast_to(voxels, (8, C))
+    consts[...] = jnp.zeros_like(consts)
+    consts[VOXELS] = voxels
+    consts[RECIP[0]] = recip
+    consts[NORM_ROWS] = norm[...]
     for e in range(EXT - 1):
         keep = meta[COUNT] > e if e < NB else meta[VALID + e - NB] > 0
         field = z_one[e] if e < NB else received_bricks(ux, lx, uy, ly)[e - NB][...]
@@ -236,16 +251,17 @@
 
 
 def third_kernel(
-    meta, got, voxels, z_two, voxel_feats, grad_out, norm, out_feats, dv_out, xh_out, recip_out, sums
+    meta, got, constants, z_two, voxel_feats, grad_out, out_feats, dv_out, xh_out, consts, sums
 ):
     total, squares = read_sums(got)
-    center, recip = statistics(total, squares, voxels[0:1])
-    recip_out[...] = jnp.broadcast_to(recip, (8, C))
+    center, recip = statistics(total, squares, constants[VOXELS])
+    consts[...] = constants[...]
+    consts[RECIP[1]] = recip
     occupied = occupied_rows(meta)
     xh = (z_two[...] - center) * recip
     xh_out[...] = xh
     feats = voxel_feats[...].astype(F32) * occupied
-    pre = norm[1:2] * xh + norm[3:4] + feats
+    pre = constants[GAIN[1]] * xh + constants[SHIFT[1]] + feats
     s = sigmoid(pre)
     out_feats[...] = (pre * s * occupied).astype(BF16)
     dv = grad_out[...].astype(F32) * occupied * (s * (1.0 + pre * (1.0 - s)))
@@ -253,8 +269,10 @@
     write_sums(sums, rows_sum(dv), rows_sum(dv * xh))
 
 
-def norm_back(dv, xh, gain, recip, total, cross, voxels, occupied):
-    return (occupied * gain * recip * (dv - total / voxels - xh * cross / voxels)).astype(BF16)
+def norm_back(dv, xh, consts, number, total, cross, occupied):
+    voxels = consts[VOXELS]
+    scale = occupied * consts[GAIN[number]] * consts[RECIP[number]]
+    return (scale * (dv - total / voxels - xh * cross / voxels)).astype(BF16)
 
 
 def send_gradients(acc, own, y_low, y_up, x_faces):
@@ -270,17 +288,16 @@
 
 
 def fourth_kernel(
-    meta, got, voxels, dv, xh_two, recip, xh_one, norm, weight_far,
-    dz_out, own, y_low, y_up, x_faces, sums, grads, weight, spread, moved, acc, sem,
+    meta, got, dv, xh_two, constants, xh_one, weight_far,
+    dz_out, own, y_low, y_up, x_faces, sums, consts, weight, spread, moved, acc, sem,
 ):
     fetch = pltpu.make_async_copy(weight_far, weight, sem)
     fetch.start()
     total, cross = read_sums(got)
-    grads[0:1] = cross
-    grads[1:2] = total
-    dz = norm_back(
-        dv[...], xh_two[...], norm[1:2], recip[0:1], total, cross, voxels[0:1], occupied_rows(meta)
-    )
+    consts[...] = constants[...]
+    consts[CROSS[1]] = cross
+    consts[TOTAL[1]] = total
+    dz = norm_back(dv[...], xh_two[...], constants, 1, total, cross, occupied_rows(meta))
     dz_out[...] = dz
     fetch.wait()
     convolve_back(meta, dz, weight, spread, moved, acc)
@@ -290,7 +307,7 @@
     for e in range(EXT - 1):
         keep = meta[COUNT] > e if e < NB else meta[VALID + e - NB] > 0
         xh = xh_one[e]
-        du = acc[e] * slope(norm[0:1] * xh + norm[2:3]) * keep.astype(F32)
+        du = acc[e] * slope(constants[GAIN[0]] * xh + constants[SHIFT[0]]) * keep.astype(F32)
         first += du
         second += du * xh
     write_sums(sums, rows_sum(first), rows_sum(second))
@@ -306,20 +323,23 @@
 
 
 def fifth_kernel(
-    meta, got, voxels, own_in, lx, ux, ly, uy, xh_one, recip, norm, weight_far,
-    dz_out, own, y_low, y_up, x_faces, grads, weight, field, spread, moved, acc, sem,
+    meta, got, own_in, lx, ux, ly, uy, xh_one, constants, weight_far,
+    dz_out, own, y_low, y_up, x_faces, consts, weight, field, spread, moved, acc, sem,
 ):
     fetch = pltpu.make_async_copy(weight_far, weight, sem)
     fetch.start()
     total, cross = read_sums(got)
-    grads[0:1] = cross
-    grads[1:2] = total
+    consts[...] = constants[...]
+    consts[CROSS[0]] = cross
+    consts[TOTAL[0]] = total
     field[...] = own_in[...].reshape(NB, 64, C)
     add_returned(meta, field, lx, ux, ly, uy)
     occupied = occupied_rows(meta)
     xh = xh_one[0:NB].reshape(ROWS, C)
-    du = field[...].reshape(ROWS, C) * occupied * slope(norm[0:1] * xh + norm[2:3])
-    dz = norm_back(du, xh, norm[0:1], recip[0:1], total, cross, voxels[0:1], occupied)
+    du = field[...].reshape(ROWS, C) * occupied * slope(
+        constants[GAIN[0]] * xh + constants[SHIFT[0]]
+    )
+    dz = norm_back(du, xh, constants, 0, total, cross, occupied)
     dz_out[...] = dz
     fetch.wait()
     convolve_back(meta, dz, weight, spread, moved, acc)
@@ -356,52 +376,66 @@
     out[32:64] = second[...]
 
 
-def total_kernel(voxels, pieces, out):
-    total = jnp.sum(pieces[...].astype(F32), axis=0) / jnp.sqrt(voxels[0:1])
+def total_kernel(consts, pieces, out):
+    total = jnp.sum(pieces[...].astype(F32), axis=0) / jnp.sqrt(consts[VOXELS])
     out[...] = jnp.broadcast_to(total.astype(BF16)[None], (64, CHUNK, C))
 
 
-def widen_kernel(meta, whole, partner, out):
-    same = meta[CORE_AT] == pl.program_id(1)
-    for c in range(31):
-        full = min(CHUNK, HALF - CHUNK * c)
-        half = jnp.where(same, whole[c].astype(F32), partner[c].astype(F32))
-        out[0, 0, CHUNK * c : CHUNK * c + full, :] = half[0:full]
-
-
-def last_kernel(meta, own, lx, ux, ly, uy, dv, grad_in, field):
+def last_kernel(meta, own, lx, ux, ly, uy, dv, consts, grad_in, norm_grads, field):
     field[...] = own[...].reshape(NB, 64, C)
     add_returned(meta, field, lx, ux, ly, uy)
     total = (dv[...] + field[...].reshape(ROWS, C)) * occupied_rows(meta)
     grad_in[...] = total.astype(BF16)
-
-
-def local(kernel, outs, ins, scratch=(), far=(), spare=SPARE):
+    root = jnp.sqrt(consts[VOXELS])
+    for row, at in enumerate((CROSS[0], TOTAL[0], CROSS[1], TOTAL[1])):
+        norm_grads[row : row + 1] = consts[at] / root
+
+
+def widen_kernel(core, half, *refs):
+    out = refs[-1]
+    for c in range(31):
+        full = min(CHUNK, HALF - CHUNK * c)
+        out[0, 0, CHUNK * c : CHUNK * c + full, :] = half[c].astype(F32)[0:full]
+
+
+def local(kernel, outs, ins, scratch=(), far=()):
     vmem = pl.BlockSpec(memory_space=pltpu.VMEM)
     smem = pl.BlockSpec(memory_space=pltpu.SMEM)
     hbm = pl.BlockSpec(memory_space=pltpu.HBM)
     specs = [hbm if n in far else smem if a.ndim == 1 else vmem for n, a in enumerate(ins)]
+    ins = [
+        pltpu.with_memory_space_constraint(a, pltpu.HBM) if n in far else a
+        for n, a in enumerate(ins)
+    ]
     return pl.pallas_call(
         kernel,
         out_shape=[jax.ShapeDtypeStruct(s, d) for s, d in outs],
         in_specs=specs,
         out_specs=[vmem] * len(outs),
         scratch_shapes=[pltpu.VMEM(*s) if isinstance(s, tuple) else s for s in scratch],
-        compiler_params=pltpu.CompilerParams(vmem_limit_bytes=VMEM_BYTES - spare),
+        compiler_params=pltpu.CompilerParams(vmem_limit_bytes=VMEM_BYTES),
     )(*ins)
 
 
-def widen(meta, whole, partner):
-    block = pl.BlockSpec((32, CHUNK, C), lambda conv, half: (conv, 0, 0))
+def widen(core, half, partner, before):
+    def place(conv, core):
+        return conv, 1 - core[0] if partner else core[0], 0, 0
+
+    held = [] if before is None else [before]
     return pl.pallas_call(
         widen_kernel,
-        grid=(2, 2),
         out_shape=jax.ShapeDtypeStruct((2, 2, HALF, C), F32),
-        in_specs=[pl.BlockSpec(memory_space=pltpu.SMEM), block, block],
-        out_specs=pl.BlockSpec((1, 1, HALF, C), lambda conv, half: (conv, half, 0, 0)),
-        compiler_params=pltpu.CompilerParams(vmem_limit_bytes=16 << 20),
+        grid_spec=pltpu.PrefetchScalarGridSpec(
+            num_scalar_prefetch=1,
+            grid=(2,),
+            in_specs=[pl.BlockSpec((32, CHUNK, C), lambda conv, core: (conv, 0, 0))]
+            + [pl.BlockSpec(memory_space=pl.ANY)] * len(held),
+            out_specs=pl.BlockSpec((1, 1, HALF, C), place),
+        ),
+        input_output_aliases={2: 0} if held else {},
+        compiler_params=pltpu.CompilerParams(vmem_limit_bytes=VMEM_BYTES),
         name="widen_kernel",
-    )(meta, whole, partner)
+    )(core, half, *held)
 
 
 def shifted(value, axis, by):
@@ -476,47 +510,49 @@
     sums = ((2 * 128, C), F32)
     ext = ((EXT,) + brick, BF16)
     list_xh = ((EXT - 1,) + brick, F32)
-    row8 = ((8, C), F32)
+    table = ((16, C), F32)
     sem = pltpu.SemaphoreType.DMA
     weight = ((TAPS * C, C), BF16)
     gathered = ((144, 6 * NB * C), BF16)
     columns = ((ROWS, TAPS * C), BF16)
     forward = [weight, gathered, columns, sem(())]
 
-    sends = local(
-        send_kernel, [(three, BF16), (three, BF16), (two, BF16)], [lists, voxel_feats]
+    *sends, kept = local(
+        send_kernel,
+        [(three, BF16), (three, BF16), (two, BF16), ((NB,) + brick, BF16)],
+        [lists, voxel_feats],
     )
     received = outward(*sends)
     z_one, ext_one, part, *sends = local(
         first_kernel,
         [((NB,) + brick, F32), ext, ((512, C), F32), (three, F32), (three, F32), (two, F32)],
-        [meta, voxel_feats, *received, flat_one],
+        [meta, kept, *received, flat_one],
         forward,
         far=(6,),
     )
     received = outward(*sends)
     part = exchange(part, GX_GY)
-    z_two, ext_two, part, xh_one, recip_one, voxels = local(
+    z_two, ext_two, part, xh_one, consts = local(
         second_kernel,
-        [(rows, F32), ext, sums, list_xh, row8, row8],
+        [(rows, F32), ext, sums, list_xh, table],
         [meta, part, z_one, *received, norm, flat_two],
         forward,
         far=(8,),
     )
     part = exchange(part, GX_GY)
-    out_feats, dv, xh_two, recip_two, part = local(
+    out_feats, dv, xh_two, consts, part = local(
         third_kernel,
-        [(rows, BF16), (rows, F32), (rows, F32), row8, sums],
-        [meta, part, voxels, z_two, voxel_feats.reshape(rows), grad_out.reshape(rows), norm],
+        [(rows, BF16), (rows, F32), (rows, F32), table, sums],
+        [meta, part, consts, z_two, voxel_feats.reshape(rows), grad_out.reshape(rows)],
     )
     part = exchange(part, GX_GY)
     back = [((3, ROWS, 9 * C), F32), gathered, ((EXT,) + brick, F32), sem(())]
-    dz_two, own, y_low, y_up, x_faces, part, grads_two = local(
+    dz_two, own, y_low, y_up, x_faces, part, consts = local(
         fourth_kernel,
-        [(rows, BF16), (rows, F32), (three, BF16), (three, BF16), (two, BF16), sums, ((2, C), F32)],
-        [meta, part, voxels, dv, xh_two, recip_two, xh_one, norm, flat_two],
+        [(rows, BF16), (rows, F32), (three, BF16), (three, BF16), (two, BF16), sums, table],
+        [meta, part, dv, xh_two, consts, xh_one, flat_two],
         [weight] + back,
-        far=(8,),
+        far=(6,),
     )
     returned = homeward(y_low, y_up, x_faces)
     chunks = (32, CHUNK, C)
@@ -525,25 +561,29 @@
     mine, other = local(taps_kernel, halves, [meta, ext_two, dz_two], products)
     (second,) = local(second_sum_kernel, [(chunks, BF16)], [mine, swap(other)])
     part = exchange(part, GX_GY)
-    dz_one, own, y_low, y_up, x_faces, grads_one = local(
+    dz_one, own, y_low, y_up, x_faces, consts = local(
         fifth_kernel,
-        [(rows, BF16), (rows, F32), (three, BF16), (three, BF16), (two, BF16), ((2, C), F32)],
-        [meta, part, voxels, own, *returned, xh_one, recip_one, norm, flat_one],
+        [(rows, BF16), (rows, F32), (three, BF16), (three, BF16), (two, BF16), table],
+        [meta, part, own, *returned, xh_one, consts, flat_one],
         [weight, ((NB,) + brick, F32)] + back,
-        far=(11,),
+        far=(9,),
     )
     returned = homeward(y_low, y_up, x_faces)
     mine, other = local(taps_kernel, halves, [meta, ext_one, dz_one], products)
-    (grad_in,) = local(
-        last_kernel, [(rows, BF16)], [meta, own, *returned, dv], [((NB,) + brick, F32)]
+    grad_in, norm_grads = local(
+        last_kernel,
+        [(rows, BF16), ((4, C), F32)],
+        [meta, own, *returned, dv, consts],
+        [((NB,) + brick, F32)],
     )
     both = ((64, CHUNK, C), BF16)
     (part,) = local(first_sum_kernel, [both], [mine, swap(other), second])
-    (whole,) = local(total_kernel, [both], [voxels, exchange(part, CHIPS)])
+    (whole,) = local(total_kernel, [both], [consts, exchange(part, CHIPS)])
     whole = exchange(whole, CHIPS)
-    weight_grads = widen(meta, whole, swap(whole)).reshape(2, TAPS, C, C)
-    root = jnp.sqrt(voxels[0, 0])
-    norm_grads = jnp.concatenate([grads_one, grads_two], axis=0) / root
+    partner = swap(whole)
+    core = lax.axis_index(CORE).reshape(1)
+    weight_grads = widen(core, whole, False, None)
+    weight_grads = widen(core, partner, True, weight_grads).reshape(2, TAPS, C, C)
     return (
         out_feats.reshape(NB, 64, C),
         grad_in.reshape(NB, 64, C),

time: 194 us -> 185 us (0.954)
  local copies, waits for them, and re-layouts: 15 us -> 2.36 us
  waiting for transfers between devices: 27.4 us -> 32.3 us
  Pallas kernels: 20.6 us -> 22.8 us
    unnamed x54 -> x6, local copies, waits for them, and re-layouts: 13 us -> 0.85 us
    ppermute x16, waiting for transfers between devices: 25.7 us -> 30.6 us  [shifted(): lax.ppermute(value, axis, [(i, (i + by) % length) for i in range(length)])]
    pallas_call x16, Pallas kernels: 17.7 us -> 20.3 us  [local(): pl.pallas_call(kernel, out_shape=[jax.ShapeDtypeStruct(s, d) for s, d in...]
  transfers between devices with their start and end apart: 21 -> 21, of which waited for: 11 -> 11; matrix products, arithmetic and copies ran while one was open for 2% -> 2% of each run, Pallas kernels for 4% -> 5%
where the time goes in v4:
time: 185 us; the launch traced here: 183 us
  blocking collectives  77.5 us (42%)
  starting transfers between devices  44.3 us (24%)
  waiting for transfers between devices  32.3 us (17%)
  Pallas kernels  22.8 us (12%)
  local copies, waits for them, and re-layouts  2.36 us (1%)
  other arithmetic  2.13 us (1%)
    all_to_all x4, blocking collectives, exchange(): return lax.all_to_all(value, axes, 0, 0, tiled=True)  77.5 us
    ppermute x16, waiting for transfers between devices, shifted(): lax.ppermute(value, axis, [(i, (i + by) % length) for i in range(length)])  30.6 us
    ppermute x16, starting transfers between devices, shifted(): lax.ppermute(value, axis, [(i, (i + by) % length) for i in range(length)])  26.7 us
    pallas_call x16, Pallas kernels, local(): pl.pallas_call(kernel, out_shape=[jax.ShapeDtypeStruct(s, d) for s, d in...  20.3 us
    all_to_all x2, starting transfers between devices, exchange(): return lax.all_to_all(value, axes, 0, 0, tiled=True)  17.4 us
  transfers between devices with their start and end apart: 21, of which 11 were waited for; matrix products, arithmetic and copies ran while one was open for 2% of the time, Pallas kernels for 5%

profile of v4, /device:TPU:34, one launch (start us, length us, event | category | flops | bytes accessed | tf_op | source)
XLA Modules:
  0.0 182.8 jit_solution(11140831267700408981)
XLA Ops:
  4.4 2.6 %collective-permute-start.1 = (bf16[3,64,128]{2,1,0:T(8,128)(2,1)S(1)}, bf16[3,64,128]{2,1,0:T(8,128)(2,1)S(1)}, u32[]{:S(2)}, u32[]{:S(2)}) collective-permute-start(bf16[3,64,128]{2,1,0:T(8,128)(2,1)S(1)} %get-tuple-element.53), channel_id=1, source_target_pairs={{0,112},{16,0},{32,16},{48,32},{64,48},{80,64},{96,80},{112,96},{1... | collective-permute-start | bytes 147464 | tf_op jit(solution)/shard_map/ppermute | solution.py:443
  7.0 2.1 %collective-permute-done.first.ux = bf16[3,64,128]{2,1,0:T(8,128)(2,1)S(1)} collective-permute-done((bf16[3,64,128]{2,1,0:T(8,128)(2,1)S(1)}, bf16[3,64,128]{2,1,0:T(8,128)(2,1)S(1)}, u32[]{:S(2)}, u32[]{:S(2)}) %collective-permute-start) | collective-permute-done | bytes 49184 | tf_op jit(solution)/shard_map/ppermute | solution.py:443
  9.2 4.1 %collective-permute-start.3 = (bf16[3,64,128]{2,1,0:T(8,128)(2,1)S(1)}, bf16[3,64,128]{2,1,0:T(8,128)(2,1)S(1)}, u32[]{:S(2)}, u32[]{:S(2)}) collective-permute-start(bf16[3,64,128]{2,1,0:T(8,128)(2,1)S(1)} %get-tuple-element.56), channel_id=1, source_target_pairs={{0,15},{1,0},{2,1},{3,2},{4,3},{5,4},{6,5},{7,6},{8,7},{9,8},{10,9... | collective-permute-start | bytes 147464 | tf_op jit(solution)/shard_map/ppermute | solution.py:443
  16.1 3.4 %shard_map.149 = (f32[4,64,128]{2,1,0:T(8,128)S(1)}, bf16[13,64,128]{2,1,0:T(8,128)(2,1)S(1)}, f32[512,128]{1,0:T(8,128)}, f32[3,64,128]{2,1,0:T(8,128)S(1)}, f3...) custom-call(s32[126]{0:T(128)S(1)} %concatenate.10.meta, bf16[4,64,128]{2,1,0:T(8,128)(2,1)S(1)} %get-tuple-element.51.voxel_feats, ...), custom_call_target="tpu_custom_call" | custom-call | tf_op jit(solution)/shard_map/pallas_call | solution.py:410
  19.5 11.2 %all-to-all-start = ((f32[128,4,128]{2,1,0:T(4,128)}), f32[128,4,128]{2,1,0:T(4,128)S(1)}, u32[]{:S(2)}, u32[]{:S(2)}) async-start(f32[128,4,128]{2,1,0:T(4,128)} %bitcast.4), calls=%async_computation | async-start | bytes 524288 | tf_op jit(solution)/shard_map/all_to_all | solution.py:447
  32.3 2.6 %collective-permute-start.5 = (f32[3,64,128]{2,1,0:T(8,128)S(1)}, f32[3,64,128]{2,1,0:T(8,128)S(1)}, u32[]{:S(2)}, u32[]{:S(2)}) collective-permute-start(f32[3,64,128]{2,1,0:T(8,128)S(1)} %get-tuple-element.60), channel_id=1, source_target_pairs={{0,112},{16,0},{32,16},{48,32},{64,48},{80,64},{96,80},{112,96},{1... | collective-permute-start | bytes 294920 | tf_op jit(solution)/shard_map/ppermute | solution.py:443
  34.9 4.4 %collective-permute-done.4.first.ux = f32[3,64,128]{2,1,0:T(8,128)S(1)} collective-permute-done((f32[3,64,128]{2,1,0:T(8,128)S(1)}, f32[3,64,128]{2,1,0:T(8,128)S(1)}, u32[]{:S(2)}, u32[]{:S(2)}) %collective-permute-start.4) | collective-permute-done | bytes 98336 | tf_op jit(solution)/shard_map/ppermute | solution.py:443
  39.5 4.1 %collective-permute-start.7 = (f32[3,64,128]{2,1,0:T(8,128)S(1)}, f32[3,64,128]{2,1,0:T(8,128)S(1)}, u32[]{:S(2)}, u32[]{:S(2)}) collective-permute-start(f32[3,64,128]{2,1,0:T(8,128)S(1)} %get-tuple-element.63), channel_id=1, source_target_pairs={{0,15},{1,0},{2,1},{3,2},{4,3},{5,4},{6,5},{7,6},{8,7},{9,8},{10,9... | collective-permute-start | bytes 294920 | tf_op jit(solution)/shard_map/ppermute | solution.py:443
  45.9 2.8 %shard_map.151 = (f32[256,128]{1,0:T(8,128)S(1)}, bf16[13,64,128]{2,1,0:T(8,128)(2,1)S(1)}, f32[256,128]{1,0:T(8,128)S(1)}, f32[12,64,128]{2,1,0:T(8,128)S(1)}, f32[16,128]{1,0:T(8,128)S(1)}) custom-call(s32[126]{0:T(128)S(1)} %concatenate.10.meta, f32[512,128]{1,0:T(8,128)S(1)} %bitcast.18, f32[4,64,128]{2,1,0:T(8,128)S(1)} %get-tuple-element.58.z_one, ...), custom_call_target="tpu_custom_call" | custom-call | tf_op jit(solution)/shard_map/pallas_call | solution.py:410
  48.8 18.1 %all_to_all.54 = f32[128,2,128]{2,1,0:T(2,128)S(1)} all-to-all(f32[128,2,128]{2,1,0:T(2,128)S(1)} %bitcast.23), channel_id=1, replica_groups=mesh['gx_0'=2,'gx_1'=4,'gy_0'=4,'gy_1'=2,'gy_2'=2] {'gx_0','gx_1','gy_0'..., dimensions={0} | all-to-all | bytes 262144 | tf_op jit(solution)/shard_map/all_to_all | solution.py:447
  68.2 14.2 %all_to_all.55 = f32[128,2,128]{2,1,0:T(2,128)S(1)} all-to-all(f32[128,2,128]{2,1,0:T(2,128)S(1)} %bitcast.24), channel_id=1, replica_groups=mesh['gx_0'=2,'gx_1'=4,'gy_0'=4,'gy_1'=2,'gy_2'=2] {'gx_0','gx_1','gy_0'..., dimensions={0} | all-to-all | bytes 262144 | tf_op jit(solution)/shard_map/all_to_all | solution.py:447
  82.3 4.1 %shard_map.153 = (bf16[256,128]{1,0:T(8,128)(2,1)S(1)}, f32[256,128]{1,0:T(8,128)S(1)}, bf16[3,64,128]{2,1,0:T(8,128)(2,1)S(1)}, bf16[3,64,128]{2,1,0:T(8,128)(2...) custom-call(s32[126]{0:T(128)S(1)} %concatenate.10.meta, ...), custom_call_target="tpu_custom_call" | custom-call | tf_op jit(solution)/shard_map/pallas_call | solution.py:410
  86.4 6.2 %all-to-all-start.3 = ((f32[128,2,128]{2,1,0:T(2,128)}), f32[128,2,128]{2,1,0:T(2,128)S(1)}, u32[]{:S(2)}, u32[]{:S(2)}) async-start(f32[128,2,128]{2,1,0:T(2,128)} %bitcast.14), calls=%async_computation.3 | async-start | bytes 262144 | tf_op jit(solution)/shard_map/all_to_all | solution.py:447
  96.1 4.2 %collective-permute-done.9.second.uy = bf16[3,64,128]{2,1,0:T(8,128)(2,1)S(1)} collective-permute-done((bf16[3,64,128]{2,1,0:T(8,128)(2,1)S(1)}, bf16[3,64,128]{2,1,0:T(8,128)(2,1)S(1)}, u32[]{:S(2)}, u32[]{:S(2)}) %collective-permute-start.9) | collective-permute-done | bytes 49184 | tf_op jit(solution)/shard_map/ppermute | solution.py:443
  100.3 3.7 %collective-permute-start.10 = (bf16[3,64,128]{2,1,0:T(8,128)(2,1)S(1)}, bf16[3,64,128]{2,1,0:T(8,128)(2,1)S(1)}, u32[]{:S(2)}, u32[]{:S(2)}) collective-permute-start(bf16[3,64,128]{2,1,0:T(8,128)(2,1)S(1)} %get-tuple-element.78), channel_id=1, source_target_pairs={{0,112},{16,0},{32,16},{48,32},{64,48},{80,64},{96,80},{112,96},{1... | collective-permute-start | bytes 147464 | tf_op jit(solution)/shard_map/ppermute | solution.py:443
  105.8 4.4 %collective-permute-done.11.ux = bf16[3,64,128]{2,1,0:T(8,128)(2,1)S(1)} collective-permute-done((bf16[3,64,128]{2,1,0:T(8,128)(2,1)S(1)}, bf16[3,64,128]{2,1,0:T(8,128)(2,1)S(1)}, u32[]{:S(2)}, u32[]{:S(2)}) %collective-permute-start.11) | collective-permute-done | bytes 49184 | tf_op jit(solution)/shard_map/ppermute | solution.py:443
  110.2 3.2 %shard_map.155 = (bf16[256,128]{1,0:T(8,128)(2,1)S(1)}, f32[256,128]{1,0:T(8,128)S(1)}, bf16[3,64,128]{2,1,0:T(8,128)(2,1)S(1)}, bf16[3,64,128]{2,1,0:T(8,128)(2...) custom-call(s32[126]{0:T(128)S(1)} %concatenate.10.meta, f32[256,128]{1,0:T(8,128)S(1)} %bitcast.19, ...), custom_call_target="tpu_custom_call" | custom-call | tf_op jit(solution)/shard_map/pallas_call | solution.py:410
  117.1 24.2 %all_to_all.56.pieces = bf16[64,56,128]{2,1,0:T(8,128)(2,1)S(1)} all-to-all(bf16[64,56,128]{2,1,0:T(8,128)(2,1)S(1)} %shard_map.161), channel_id=1, replica_groups=mesh['gx_0'=2,'gx_1'=4,'gy_0'=4,'gy_1'=2,'gy_2'=2] {'gx_0','gx_1','gy_0'..., dimensions={0} | all-to-all | bytes 1835008 | tf_op jit(solution)/shard_map/all_to_all | solution.py:447
  141.5 21.0 %all_to_all.57.half = bf16[64,56,128]{2,1,0:T(8,128)(2,1)S(1)} all-to-all(bf16[64,56,128]{2,1,0:T(8,128)(2,1)S(1)} %shard_map.162), channel_id=1, replica_groups=mesh['gx_0'=2,'gx_1'=4,'gy_0'=4,'gy_1'=2,'gy_2'=2] {'gx_0','gx_1','gy_0'..., dimensions={0} | all-to-all | bytes 1835008 | tf_op jit(solution)/shard_map/all_to_all | solution.py:447
  162.5 2.2 %collective-permute-start.12 = (bf16[3,64,128]{2,1,0:T(8,128)(2,1)S(1)}, bf16[3,64,128]{2,1,0:T(8,128)(2,1)S(1)}, u32[]{:S(2)}, u32[]{:S(2)}) collective-permute-start(bf16[3,64,128]{2,1,0:T(8,128)(2,1)S(1)} %get-tuple-element.83), channel_id=1, source_target_pairs={{0,15},{1,0},{2,1},{3,2},{4,3},{5,4},{6,5},{7,6},{8,7},{9,8},{10,9... | collective-permute-start | bytes 147464 | tf_op jit(solution)/shard_map/ppermute | solution.py:443
  166.4 4.2 %collective-permute-done.13.second.uy = bf16[3,64,128]{2,1,0:T(8,128)(2,1)S(1)} collective-permute-done((bf16[3,64,128]{2,1,0:T(8,128)(2,1)S(1)}, bf16[3,64,128]{2,1,0:T(8,128)(2,1)S(1)}, u32[]{:S(2)}, u32[]{:S(2)}) %collective-permute-start.13) | collective-permute-done | bytes 49184 | tf_op jit(solution)/shard_map/ppermute | solution.py:443
  170.6 2.2 %collective-permute-start.14 = (bf16[3,64,128]{2,1,0:T(8,128)(2,1)S(1)}, bf16[3,64,128]{2,1,0:T(8,128)(2,1)S(1)}, u32[]{:S(2)}, u32[]{:S(2)}) collective-permute-start(bf16[3,64,128]{2,1,0:T(8,128)(2,1)S(1)} %get-tuple-element.85), channel_id=1, source_target_pairs={{0,112},{16,0},{32,16},{48,32},{64,48},{80,64},{96,80},{112,96},{1... | collective-permute-start | bytes 147464 | tf_op jit(solution)/shard_map/ppermute | solution.py:443
  172.8 1.9 %collective-permute-done.14.lx = bf16[3,64,128]{2,1,0:T(8,128)(2,1)S(1)} collective-permute-done((bf16[3,64,128]{2,1,0:T(8,128)(2,1)S(1)}, bf16[3,64,128]{2,1,0:T(8,128)(2,1)S(1)}, u32[]{:S(2)}, u32[]{:S(2)}) %collective-permute-start.14) | collective-permute-done | bytes 49184 | tf_op jit(solution)/shard_map/ppermute | solution.py:443
  174.8 4.3 %collective-permute-done.15.ux = bf16[3,64,128]{2,1,0:T(8,128)(2,1)S(1)} collective-permute-done((bf16[3,64,128]{2,1,0:T(8,128)(2,1)S(1)}, bf16[3,64,128]{2,1,0:T(8,128)(2,1)S(1)}, u32[]{:S(2)}, u32[]{:S(2)}) %collective-permute-start.15) | collective-permute-done | bytes 49184 | tf_op jit(solution)/shard_map/ppermute | solution.py:443
  (51 shorter events, 25.9 us)
Async XLA Ops:
  1.4 0.8 copy-start
  2.2 64.7 %copy-start.1 = (bf16[4,64,128]{2,1,0:T(8,128)(2,1)S(1)}, bf16[4,64,128]{2,1,0:T(8,128)(2,1)}, u32[]{:S(2)}) copy-start(bf16[4,64,128]{2,1,0:T(8,128)(2,1)} %field.1) | copy-start | bytes 196612
  2.2 64.7 %copy-start.2 = (bf16[4,64,128]{2,1,0:T(8,128)(2,1)S(1)}, bf16[4,64,128]{2,1,0:T(8,128)(2,1)}, u32[]{:S(2)}) copy-start(bf16[4,64,128]{2,1,0:T(8,128)(2,1)} %param.17) | copy-start | bytes 196612
  2.8 6.3 %collective-permute-start = (bf16[3,64,128]{2,1,0:T(8,128)(2,1)S(1)}, bf16[3,64,128]{2,1,0:T(8,128)(2,1)S(1)}, u32[]{:S(2)}, u32[]{:S(2)}) collective-permute-start(bf16[3,64,128]{2,1,0:T(8,128)(2,1)S(1)} %get-tuple-element.52), channel_id=1, source_target_pairs={{0,16},{16,32},{32,48},{48,64},{64,80},{80,96},{96,112},{112,0},{1... | collective-permute-start | bytes 147464 | tf_op jit(solution)/shard_map/ppermute | solution.py:443
  4.4 4.6 %collective-permute-start.1 = (bf16[3,64,128]{2,1,0:T(8,128)(2,1)S(1)}, bf16[3,64,128]{2,1,0:T(8,128)(2,1)S(1)}, u32[]{:S(2)}, u32[]{:S(2)}) collective-permute-start(bf16[3,64,128]{2,1,0:T(8,128)(2,1)S(1)} %get-tuple-element.53), channel_id=1, source_target_pairs={{0,112},{16,0},{32,16},{48,32},{64,48},{80,64},{96,80},{112,96},{1... | collective-permute-start | bytes 147464 | tf_op jit(solution)/shard_map/ppermute | solution.py:443
  9.1 7.1 %collective-permute-start.2 = (bf16[3,64,128]{2,1,0:T(8,128)(2,1)S(1)}, bf16[3,64,128]{2,1,0:T(8,128)(2,1)S(1)}, u32[]{:S(2)}, u32[]{:S(2)}) collective-permute-start(bf16[3,64,128]{2,1,0:T(8,128)(2,1)S(1)} %get-tuple-element.55), channel_id=1, source_target_pairs={{0,1},{1,2},{2,3},{3,4},{4,5},{5,6},{6,7},{7,8},{8,9},{9,10},{10,1... | collective-permute-start | bytes 147464 | tf_op jit(solution)/shard_map/ppermute | solution.py:443
  9.2 7.0 %collective-permute-start.3 = (bf16[3,64,128]{2,1,0:T(8,128)(2,1)S(1)}, bf16[3,64,128]{2,1,0:T(8,128)(2,1)S(1)}, u32[]{:S(2)}, u32[]{:S(2)}) collective-permute-start(bf16[3,64,128]{2,1,0:T(8,128)(2,1)S(1)} %get-tuple-element.56), channel_id=1, source_target_pairs={{0,15},{1,0},{2,1},{3,2},{4,3},{5,4},{6,5},{7,6},{8,7},{9,8},{10,9... | collective-permute-start | bytes 147464 | tf_op jit(solution)/shard_map/ppermute | solution.py:443
  19.5 26.4 %all-to-all-start = ((f32[128,4,128]{2,1,0:T(4,128)}), f32[128,4,128]{2,1,0:T(4,128)S(1)}, u32[]{:S(2)}, u32[]{:S(2)}) async-start(f32[128,4,128]{2,1,0:T(4,128)} %bitcast.4), calls=%async_computation | async-start | bytes 524288 | tf_op jit(solution)/shard_map/all_to_all | solution.py:447
  30.7 8.6 %collective-permute-start.4 = (f32[3,64,128]{2,1,0:T(8,128)S(1)}, f32[3,64,128]{2,1,0:T(8,128)S(1)}, u32[]{:S(2)}, u32[]{:S(2)}) collective-permute-start(f32[3,64,128]{2,1,0:T(8,128)S(1)} %get-tuple-element.59), channel_id=1, source_target_pairs={{0,16},{16,32},{32,48},{48,64},{64,80},{80,96},{96,112},{112,0},{1... | collective-permute-start | bytes 294920 | tf_op jit(solution)/shard_map/ppermute | solution.py:443
  32.3 7.0 %collective-permute-start.5 = (f32[3,64,128]{2,1,0:T(8,128)S(1)}, f32[3,64,128]{2,1,0:T(8,128)S(1)}, u32[]{:S(2)}, u32[]{:S(2)}) collective-permute-start(f32[3,64,128]{2,1,0:T(8,128)S(1)} %get-tuple-element.60), channel_id=1, source_target_pairs={{0,112},{16,0},{32,16},{48,32},{64,48},{80,64},{96,80},{112,96},{1... | collective-permute-start | bytes 294920 | tf_op jit(solution)/shard_map/ppermute | solution.py:443
  39.4 6.5 %collective-permute-start.6 = (f32[3,64,128]{2,1,0:T(8,128)S(1)}, f32[3,64,128]{2,1,0:T(8,128)S(1)}, u32[]{:S(2)}, u32[]{:S(2)}) collective-permute-start(f32[3,64,128]{2,1,0:T(8,128)S(1)} %get-tuple-element.62), channel_id=1, source_target_pairs={{0,1},{1,2},{2,3},{3,4},{4,5},{5,6},{6,7},{7,8},{8,9},{9,10},{10,1... | collective-permute-start | bytes 294920 | tf_op jit(solution)/shard_map/ppermute | solution.py:443
  39.5 6.4 %collective-permute-start.7 = (f32[3,64,128]{2,1,0:T(8,128)S(1)}, f32[3,64,128]{2,1,0:T(8,128)S(1)}, u32[]{:S(2)}, u32[]{:S(2)}) collective-permute-start(f32[3,64,128]{2,1,0:T(8,128)S(1)} %get-tuple-element.63), channel_id=1, source_target_pairs={{0,15},{1,0},{2,1},{3,2},{4,3},{5,4},{6,5},{7,6},{8,7},{9,8},{10,9... | collective-permute-start | bytes 294920 | tf_op jit(solution)/shard_map/ppermute | solution.py:443
  86.4 23.8 %all-to-all-start.3 = ((f32[128,2,128]{2,1,0:T(2,128)}), f32[128,2,128]{2,1,0:T(2,128)S(1)}, u32[]{:S(2)}, u32[]{:S(2)}) async-start(f32[128,2,128]{2,1,0:T(2,128)} %bitcast.14), calls=%async_computation.3 | async-start | bytes 262144 | tf_op jit(solution)/shard_map/all_to_all | solution.py:447
  92.6 3.5 %collective-permute-start.8 = (bf16[3,64,128]{2,1,0:T(8,128)(2,1)S(1)}, bf16[3,64,128]{2,1,0:T(8,128)(2,1)S(1)}, u32[]{:S(2)}, u32[]{:S(2)}) collective-permute-start(bf16[3,64,128]{2,1,0:T(8,128)(2,1)S(1)} %get-tuple-element.76), channel_id=1, source_target_pairs={{0,15},{1,0},{2,1},{3,2},{4,3},{5,4},{6,5},{7,6},{8,7},{9,8},{10,9... | collective-permute-start | bytes 147464 | tf_op jit(solution)/shard_map/ppermute | solution.py:443
  94.4 5.9 %collective-permute-start.9 = (bf16[3,64,128]{2,1,0:T(8,128)(2,1)S(1)}, bf16[3,64,128]{2,1,0:T(8,128)(2,1)S(1)}, u32[]{:S(2)}, u32[]{:S(2)}) collective-permute-start(bf16[3,64,128]{2,1,0:T(8,128)(2,1)S(1)} %get-tuple-element.77), channel_id=1, source_target_pairs={{0,1},{1,2},{2,3},{3,4},{4,5},{5,6},{6,7},{7,8},{8,9},{9,10},{10,1... | collective-permute-start | bytes 147464 | tf_op jit(solution)/shard_map/ppermute | solution.py:443
  100.3 5.5 %collective-permute-start.10 = (bf16[3,64,128]{2,1,0:T(8,128)(2,1)S(1)}, bf16[3,64,128]{2,1,0:T(8,128)(2,1)S(1)}, u32[]{:S(2)}, u32[]{:S(2)}) collective-permute-start(bf16[3,64,128]{2,1,0:T(8,128)(2,1)S(1)} %get-tuple-element.78), channel_id=1, source_target_pairs={{0,112},{16,0},{32,16},{48,32},{64,48},{80,64},{96,80},{112,96},{1... | collective-permute-start | bytes 147464 | tf_op jit(solution)/shard_map/ppermute | solution.py:443
  104.0 6.2 %collective-permute-start.11 = (bf16[3,64,128]{2,1,0:T(8,128)(2,1)S(1)}, bf16[3,64,128]{2,1,0:T(8,128)(2,1)S(1)}, u32[]{:S(2)}, u32[]{:S(2)}) collective-permute-start(bf16[3,64,128]{2,1,0:T(8,128)(2,1)S(1)} %get-tuple-element.79), channel_id=1, source_target_pairs={{0,16},{16,32},{32,48},{48,64},{64,80},{80,96},{96,112},{112,0},{1... | collective-permute-start | bytes 147464 | tf_op jit(solution)/shard_map/ppermute | solution.py:443
  105.7 9.5 %collective-permute-start.17 = (bf16[32,56,128]{2,1,0:T(8,128)(2,1)S(1)}, bf16[32,56,128]{2,1,0:T(8,128)(2,1)S(1)}, u32[]{:S(2)}, u32[]{:S(2)}) collective-permute-start(bf16[32,56,128]{2,1,0:T(8,128)(2,1)S(1)} %get-tuple-element.96), channel_id=1, source_target_pairs={{0,1},{1,0},{2,3},{3,2},{4,5},{5,4},{6,7},{7,6},{8,9},{9,8},{10,11... | collective-permute-start | bytes 1376264 | tf_op jit(solution)/shard_map/ppermute | solution.py:451
  115.1 1.9 %collective-permute-start.16 = (bf16[32,56,128]{2,1,0:T(8,128)(2,1)S(1)}, bf16[32,56,128]{2,1,0:T(8,128)(2,1)S(1)}, u32[]{:S(2)}, u32[]{:S(2)}) collective-permute-start(bf16[32,56,128]{2,1,0:T(8,128)(2,1)S(1)} %get-tuple-element.92), channel_id=1, source_target_pairs={{0,1},{1,0},{2,3},{3,2},{4,5},{5,4},{6,7},{7,6},{8,9},{9,8},{10,11... | collective-permute-start | bytes 1376264 | tf_op jit(solution)/shard_map/ppermute | solution.py:451
  162.5 19.1 %collective-permute-start.18 = (bf16[64,56,128]{2,1,0:T(8,128)(2,1)S(1)}, bf16[64,56,128]{2,1,0:T(8,128)(2,1)S(1)}, u32[]{:S(2)}, u32[]{:S(2)}) collective-permute-start(bf16[64,56,128]{2,1,0:T(8,128)(2,1)S(1)} %all_to_all.57.half), channel_id=1, source_target_pairs={{0,1},{1,0},{2,3},{3,2},{4,5},{5,4},{6,7},{7,6},{8,9},{9,8},{10,11... | collective-permute-start | bytes 2752520 | tf_op jit(solution)/shard_map/ppermute | solution.py:451
  162.5 3.9 %collective-permute-start.12 = (bf16[3,64,128]{2,1,0:T(8,128)(2,1)S(1)}, bf16[3,64,128]{2,1,0:T(8,128)(2,1)S(1)}, u32[]{:S(2)}, u32[]{:S(2)}) collective-permute-start(bf16[3,64,128]{2,1,0:T(8,128)(2,1)S(1)} %get-tuple-element.83), channel_id=1, source_target_pairs={{0,15},{1,0},{2,1},{3,2},{4,3},{5,4},{6,5},{7,6},{8,7},{9,8},{10,9... | collective-permute-start | bytes 147464 | tf_op jit(solution)/shard_map/ppermute | solution.py:443
  164.7 5.9 %collective-permute-start.13 = (bf16[3,64,128]{2,1,0:T(8,128)(2,1)S(1)}, bf16[3,64,128]{2,1,0:T(8,128)(2,1)S(1)}, u32[]{:S(2)}, u32[]{:S(2)}) collective-permute-start(bf16[3,64,128]{2,1,0:T(8,128)(2,1)S(1)} %get-tuple-element.84), channel_id=1, source_target_pairs={{0,1},{1,2},{2,3},{3,4},{4,5},{5,6},{6,7},{7,8},{8,9},{9,10},{10,1... | collective-permute-start | bytes 147464 | tf_op jit(solution)/shard_map/ppermute | solution.py:443
  170.6 4.2 %collective-permute-start.14 = (bf16[3,64,128]{2,1,0:T(8,128)(2,1)S(1)}, bf16[3,64,128]{2,1,0:T(8,128)(2,1)S(1)}, u32[]{:S(2)}, u32[]{:S(2)}) collective-permute-start(bf16[3,64,128]{2,1,0:T(8,128)(2,1)S(1)} %get-tuple-element.85), channel_id=1, source_target_pairs={{0,112},{16,0},{32,16},{48,32},{64,48},{80,64},{96,80},{112,96},{1... | collective-permute-start | bytes 147464 | tf_op jit(solution)/shard_map/ppermute | solution.py:443
  172.8 6.2 %collective-permute-start.15 = (bf16[3,64,128]{2,1,0:T(8,128)(2,1)S(1)}, bf16[3,64,128]{2,1,0:T(8,128)(2,1)S(1)}, u32[]{:S(2)}, u32[]{:S(2)}) collective-permute-start(bf16[3,64,128]{2,1,0:T(8,128)(2,1)S(1)} %get-tuple-element.86), channel_id=1, source_target_pairs={{0,16},{16,32},{32,48},{48,64},{64,80},{80,96},{96,112},{112,0},{1... | collective-permute-start | bytes 147464 | tf_op jit(solution)/shard_map/ppermute | solution.py:443

commit v5 on v4

--- a/solution.py
+++ b/solution.py
@@ -1,3 +1,5 @@
+import functools
+
 import jax
 import jax.numpy as jnp
 import numpy as np
@@ -157,29 +159,41 @@
 
 def received_bricks(ux, lx, uy, ly):
     return (
-        ux.at[0], lx.at[0], uy.at[0], ly.at[0], uy.at[1], ly.at[1], uy.at[2], ly.at[2]
-    )
-
-
-def sends_of(face, corner, x_up, x_low, y_faces):
+        ux.at[0], lx.at[0], uy.at[0], ly.at[0], ux.at[1], ux.at[2], lx.at[1], lx.at[2]
+    )
+
+
+def sends_of(face, corner, y_up, y_low, x_faces):
     return (
-        (face(0), x_up.at[0]), (corner(0), x_up.at[1]), (corner(1), x_up.at[2]),
-        (face(1), x_low.at[0]), (corner(2), x_low.at[1]), (corner(3), x_low.at[2]),
-        (face(2), y_faces.at[0]), (face(3), y_faces.at[1]),
-    )
-
-
-def select_sends(meta, field, x_up, x_low, y_faces):
+        (face(2), y_up.at[0]), (corner(0), y_up.at[1]), (corner(2), y_up.at[2]),
+        (face(3), y_low.at[0]), (corner(1), y_low.at[1]), (corner(3), y_low.at[2]),
+        (face(0), x_faces.at[0]), (face(1), x_faces.at[1]),
+    )
+
+
+def select_sends(meta, field, y_up, y_low, x_faces):
     for entry, out in sends_of(
-        lambda k: meta[FACE + k], lambda k: meta[CORNER + k], x_up, x_low, y_faces
+        lambda k: meta[FACE + k], lambda k: meta[CORNER + k], y_up, y_low, x_faces
     ):
         out[...] = field[entry]
 
 
-def send_kernel(lists, field, x_up, x_low, y_faces, kept):
+def send_kernel(lists, field, y_up, y_low, x_faces, kept):
     kept[...] = field[...]
-    for entry, out in sends_of(lambda k: lists[k], lambda k: lists[4 + k], x_up, x_low, y_faces):
+    for entry, out in sends_of(lambda k: lists[k], lambda k: lists[4 + k], y_up, y_low, x_faces):
         out[...] = field[entry]
+
+
+def fetch_one_kernel(far, out, sem):
+    copy = pltpu.make_async_copy(far, out, sem)
+    copy.start()
+    copy.wait()
+
+
+def fetch_two_kernel(far, out, sem):
+    copy = pltpu.make_async_copy(far, out, sem)
+    copy.start()
+    copy.wait()
 
 
 def join_kernel(faces, first, second, up, low):
@@ -192,11 +206,9 @@
 
 
 def first_kernel(
-    meta, voxel_feats, ux, lx, uy, ly, weight_far,
-    z_out, ext, sums, x_up, x_low, y_faces, weight, gathered, columns, sem,
+    meta, voxel_feats, ux, lx, uy, ly, weight,
+    z_out, ext, sums, y_up, y_low, x_faces, gathered, columns,
 ):
-    fetch = pltpu.make_async_copy(weight_far, weight, sem)
-    fetch.start()
     ext[NB + 8] = jnp.zeros((64, C), BF16)
     for b in range(NB):
         keep = (meta[COUNT] > b).astype(F32)
@@ -205,10 +217,9 @@
         keep = meta[VALID + e].astype(F32)
         ext[NB + e] = (brick[...].astype(F32) * keep).astype(BF16)
     gather_columns(meta, ext, gathered, columns)
-    fetch.wait()
     z = convolve(columns, weight)
     z_out[...] = z.reshape(NB, 64, C)
-    select_sends(meta, z_out, x_up, x_low, y_faces)
+    select_sends(meta, z_out, y_up, y_low, x_faces)
     masked = z * occupied_rows(meta)
     row = lax.broadcasted_iota(jnp.int32, (8, C), 0) % 4
     count = (64 * meta[COUNT]).astype(F32)
@@ -219,11 +230,9 @@
 
 
 def second_kernel(
-    meta, got, z_one, ux, lx, uy, ly, norm, weight_far,
-    z_out, ext, sums, xh_out, consts, weight, gathered, columns, sem,
+    meta, got, z_one, ux, lx, uy, ly, norm, weight,
+    z_out, ext, sums, xh_out, consts, gathered, columns,
 ):
-    fetch = pltpu.make_async_copy(weight_far, weight, sem)
-    fetch.start()
     row = lax.broadcasted_iota(jnp.int32, (8, C), 0) % 4
     both = jnp.sum(got[...].reshape(64, 8, C), axis=0)
     total = rows_sum(jnp.where(row == 0, both, 0.0))
@@ -243,7 +252,6 @@
         ext[e] = (u * sigmoid(u) * keep.astype(F32)).astype(BF16)
     ext[EXT - 1] = jnp.zeros((64, C), BF16)
     gather_columns(meta, ext, gathered, columns)
-    fetch.wait()
     z = convolve(columns, weight)
     z_out[...] = z
     masked = z * occupied_rows(meta)
@@ -288,18 +296,15 @@
 
 
 def fourth_kernel(
-    meta, got, dv, xh_two, constants, xh_one, weight_far,
-    dz_out, own, y_low, y_up, x_faces, sums, consts, weight, spread, moved, acc, sem,
+    meta, got, dv, xh_two, constants, xh_one, weight,
+    dz_out, own, y_low, y_up, x_faces, sums, consts, spread, moved, acc,
 ):
-    fetch = pltpu.make_async_copy(weight_far, weight, sem)
-    fetch.start()
     total, cross = read_sums(got)
     consts[...] = constants[...]
     consts[CROSS[1]] = cross
     consts[TOTAL[1]] = total
     dz = norm_back(dv[...], xh_two[...], constants, 1, total, cross, occupied_rows(meta))
     dz_out[...] = dz
-    fetch.wait()
     convolve_back(meta, dz, weight, spread, moved, acc)
     send_gradients(acc, own, y_low, y_up, x_faces)
     first = jnp.zeros((64, C), F32)
@@ -324,7 +329,7 @@
 
 def fifth_kernel(
     meta, got, own_in, lx, ux, ly, uy, xh_one, constants, weight_far,
-    dz_out, own, y_low, y_up, x_faces, consts, weight, field, spread, moved, acc, sem,
+    dz_out, own, y_low, y_up, x_faces, consts, weight, sem, field, spread, moved, acc,
 ):
     fetch = pltpu.make_async_copy(weight_far, weight, sem)
     fetch.start()
@@ -391,11 +396,27 @@
         norm_grads[row : row + 1] = consts[at] / root
 
 
-def widen_kernel(core, half, *refs):
-    out = refs[-1]
-    for c in range(31):
-        full = min(CHUNK, HALF - CHUNK * c)
-        out[0, 0, CHUNK * c : CHUNK * c + full, :] = half[c].astype(F32)[0:full]
+def widen_kernel(core, half, *refs, partner):
+    out, wide, sems = refs[-3:]
+    at = 1 - core[0] if partner else core[0]
+    copies = []
+    for conv in range(2):
+        for piece in range(4):
+            for c in range(8 * piece, min(8 * piece + 8, 31)):
+                full = min(CHUNK, HALF - CHUNK * c)
+                wide[conv, CHUNK * c : CHUNK * c + full, :] = half[32 * conv + c].astype(F32)[
+                    0:full
+                ]
+            first = 8 * CHUNK * piece
+            rows = pl.ds(first, min(8 * CHUNK, HALF - first))
+            copies.append(
+                pltpu.make_async_copy(
+                    wide.at[conv, rows], out.at[conv, at, rows], sems.at[4 * conv + piece]
+                )
+            )
+            copies[-1].start()
+    for copy in copies:
+        copy.wait()
 
 
 def local(kernel, outs, ins, scratch=(), far=()):
@@ -418,20 +439,15 @@
 
 
 def widen(core, half, partner, before):
-    def place(conv, core):
-        return conv, 1 - core[0] if partner else core[0], 0, 0
-
     held = [] if before is None else [before]
+    far = pl.BlockSpec(memory_space=pltpu.HBM)
     return pl.pallas_call(
-        widen_kernel,
+        functools.partial(widen_kernel, partner=partner),
         out_shape=jax.ShapeDtypeStruct((2, 2, HALF, C), F32),
-        grid_spec=pltpu.PrefetchScalarGridSpec(
-            num_scalar_prefetch=1,
-            grid=(2,),
-            in_specs=[pl.BlockSpec((32, CHUNK, C), lambda conv, core: (conv, 0, 0))]
-            + [pl.BlockSpec(memory_space=pl.ANY)] * len(held),
-            out_specs=pl.BlockSpec((1, 1, HALF, C), place),
-        ),
+        in_specs=[pl.BlockSpec(memory_space=pltpu.SMEM), pl.BlockSpec(memory_space=pltpu.VMEM)]
+        + [far] * len(held),
+        out_specs=far,
+        scratch_shapes=[pltpu.VMEM((2, HALF, C), F32), pltpu.SemaphoreType.DMA((8,))],
         input_output_aliases={2: 0} if held else {},
         compiler_params=pltpu.CompilerParams(vmem_limit_bytes=VMEM_BYTES),
         name="widen_kernel",
@@ -460,10 +476,10 @@
     return shifted(first, axis, by), shifted(second, axis, -by)
 
 
-def outward(x_up, x_low, y_faces):
-    ux, lx = pair(x_up, x_low, GX, 1)
-    up, low = join(y_faces, ux, lx)
-    uy, ly = pair(up, low, GY, 1)
+def outward(y_up, y_low, x_faces):
+    uy, ly = pair(y_up, y_low, GY, 1)
+    up, low = join(x_faces, uy, ly)
+    ux, lx = pair(up, low, GX, 1)
     return ux, lx, uy, ly
 
 
@@ -515,29 +531,29 @@
     weight = ((TAPS * C, C), BF16)
     gathered = ((144, 6 * NB * C), BF16)
     columns = ((ROWS, TAPS * C), BF16)
-    forward = [weight, gathered, columns, sem(())]
+    forward = [gathered, columns]
 
     *sends, kept = local(
         send_kernel,
         [(three, BF16), (three, BF16), (two, BF16), ((NB,) + brick, BF16)],
         [lists, voxel_feats],
     )
+    (near_one,) = local(fetch_one_kernel, [weight], [flat_one], [sem(())], far=(0,))
+    (near_two,) = local(fetch_two_kernel, [weight], [flat_two], [sem(())], far=(0,))
     received = outward(*sends)
     z_one, ext_one, part, *sends = local(
         first_kernel,
         [((NB,) + brick, F32), ext, ((512, C), F32), (three, F32), (three, F32), (two, F32)],
-        [meta, kept, *received, flat_one],
+        [meta, kept, *received, near_one],
         forward,
-        far=(6,),
     )
     received = outward(*sends)
     part = exchange(part, GX_GY)
     z_two, ext_two, part, xh_one, consts = local(
         second_kernel,
         [(rows, F32), ext, sums, list_xh, table],
-        [meta, part, z_one, *received, norm, flat_two],
+        [meta, part, z_one, *received, norm, near_two],
         forward,
-        far=(8,),
     )
     part = exchange(part, GX_GY)
     out_feats, dv, xh_two, consts, part = local(
@@ -546,13 +562,12 @@
         [meta, part, consts, z_two, voxel_feats.reshape(rows), grad_out.reshape(rows)],
     )
     part = exchange(part, GX_GY)
-    back = [((3, ROWS, 9 * C), F32), gathered, ((EXT,) + brick, F32), sem(())]
+    back = [((3, ROWS, 9 * C), F32), gathered, ((EXT,) + brick, F32)]
     dz_two, own, y_low, y_up, x_faces, part, consts = local(
         fourth_kernel,
         [(rows, BF16), (rows, F32), (three, BF16), (three, BF16), (two, BF16), sums, table],
-        [meta, part, dv, xh_two, consts, xh_one, flat_two],
-        [weight] + back,
-        far=(6,),
+        [meta, part, dv, xh_two, consts, xh_one, near_two],
+        back,
     )
     returned = homeward(y_low, y_up, x_faces)
     chunks = (32, CHUNK, C)
@@ -565,7 +580,7 @@
         fifth_kernel,
         [(rows, BF16), (rows, F32), (three, BF16), (three, BF16), (two, BF16), table],
         [meta, part, own, *returned, xh_one, consts, flat_one],
-        [weight, ((NB,) + brick, F32)] + back,
+        [weight, sem(()), ((NB,) + brick, F32)] + back,
         far=(9,),
     )
     returned = homeward(y_low, y_up, x_faces)

time: 185 us -> 181 us (0.978)
    pallas_call x16 -> x18, Pallas kernels: 20.3 us -> 19.4 us  [local(): pl.pallas_call(kernel, out_shape=[jax.ShapeDtypeStruct(s, d) for s, d in...]
  transfers between devices with their start and end apart: 21 -> 21, of which waited for: 11 -> 11; matrix products, arithmetic and copies ran while one was open for 2% -> 1% of each run, Pallas kernels for 5% -> 6%
where the time goes in v5:
time: 181 us; the launch traced here: 178 us
  blocking collectives  77.4 us (43%)
  starting transfers between devices  42.5 us (23%)
  waiting for transfers between devices  30.7 us (17%)
  Pallas kernels  22 us (12%)
  local copies, waits for them, and re-layouts  2.37 us (1%)
    all_to_all x4, blocking collectives, exchange(): return lax.all_to_all(value, axes, 0, 0, tiled=True)  77.4 us
    ppermute x16, waiting for transfers between devices, shifted(): lax.ppermute(value, axis, [(i, (i + by) % length) for i in range(length)])  29 us
    ppermute x16, starting transfers between devices, shifted(): lax.ppermute(value, axis, [(i, (i + by) % length) for i in range(length)])  26.7 us
    pallas_call x18, Pallas kernels, local(): pl.pallas_call(kernel, out_shape=[jax.ShapeDtypeStruct(s, d) for s, d in...  19.4 us
    all_to_all x2, starting transfers between devices, exchange(): return lax.all_to_all(value, axes, 0, 0, tiled=True)  15.7 us
  transfers between devices with their start and end apart: 21, of which 11 were waited for; matrix products, arithmetic and copies ran while one was open for 1% of the time, Pallas kernels for 6%

profile of v5, /device:TPU:34, one launch (start us, length us, event | category | flops | bytes accessed | tf_op | source)
XLA Modules:
  0.0 178.1 jit_solution(11174795780593832506)
XLA Ops:
  2.9 4.1 %collective-permute-start.1 = (bf16[3,64,128]{2,1,0:T(8,128)(2,1)S(1)}, bf16[3,64,128]{2,1,0:T(8,128)(2,1)S(1)}, u32[]{:S(2)}, u32[]{:S(2)}) collective-permute-start(bf16[3,64,128]{2,1,0:T(8,128)(2,1)S(1)} %get-tuple-element.54), channel_id=1, source_target_pairs={{0,15},{1,0},{2,1},{3,2},{4,3},{5,4},{6,5},{7,6},{8,7},{9,8},{10,9... | collective-permute-start | bytes 147464 | tf_op jit(solution)/shard_map/ppermute | solution.py:459
  7.0 1.8 collective-permute-done.first.uy
  10.5 2.6 %collective-permute-start.3 = (bf16[3,64,128]{2,1,0:T(8,128)(2,1)S(1)}, bf16[3,64,128]{2,1,0:T(8,128)(2,1)S(1)}, u32[]{:S(2)}, u32[]{:S(2)}) collective-permute-start(bf16[3,64,128]{2,1,0:T(8,128)(2,1)S(1)} %get-tuple-element.56), channel_id=1, source_target_pairs={{0,112},{16,0},{32,16},{48,32},{64,48},{80,64},{96,80},{112,96},{1... | collective-permute-start | bytes 147464 | tf_op jit(solution)/shard_map/ppermute | solution.py:459
  17.1 2.3 %shard_map.150 = (f32[4,64,128]{2,1,0:T(8,128)S(1)}, bf16[13,64,128]{2,1,0:T(8,128)(2,1)S(1)}, f32[512,128]{1,0:T(8,128)}, f32[3,64,128]{2,1,0:T(8,128)S(1)}, f3...) custom-call(s32[126]{0:T(128)S(1)} %concatenate.10.meta, bf16[4,64,128]{2,1,0:T(8,128)(2,1)S(1)} %get-tuple-element.51.voxel_feats, ...), custom_call_target="tpu_custom_call" | custom-call | tf_op jit(solution)/shard_map/pallas_call | solution.py:431
  19.4 9.5 %all-to-all-start = ((f32[128,4,128]{2,1,0:T(4,128)}), f32[128,4,128]{2,1,0:T(4,128)S(1)}, u32[]{:S(2)}, u32[]{:S(2)}) async-start(f32[128,4,128]{2,1,0:T(4,128)} %bitcast.4), calls=%async_computation | async-start | bytes 524288 | tf_op jit(solution)/shard_map/all_to_all | solution.py:463
  29.1 4.0 %collective-permute-start.5 = (f32[3,64,128]{2,1,0:T(8,128)S(1)}, f32[3,64,128]{2,1,0:T(8,128)S(1)}, u32[]{:S(2)}, u32[]{:S(2)}) collective-permute-start(f32[3,64,128]{2,1,0:T(8,128)S(1)} %get-tuple-element.61), channel_id=1, source_target_pairs={{0,15},{1,0},{2,1},{3,2},{4,3},{5,4},{6,5},{7,6},{8,7},{9,8},{10,9... | collective-permute-start | bytes 294920 | tf_op jit(solution)/shard_map/ppermute | solution.py:459
  37.1 2.8 %collective-permute-start.7 = (f32[3,64,128]{2,1,0:T(8,128)S(1)}, f32[3,64,128]{2,1,0:T(8,128)S(1)}, u32[]{:S(2)}, u32[]{:S(2)}) collective-permute-start(f32[3,64,128]{2,1,0:T(8,128)S(1)} %get-tuple-element.63), channel_id=1, source_target_pairs={{0,112},{16,0},{32,16},{48,32},{64,48},{80,64},{96,80},{112,96},{1... | collective-permute-start | bytes 294920 | tf_op jit(solution)/shard_map/ppermute | solution.py:459
  39.9 3.3 %collective-permute-done.6.ux = f32[3,64,128]{2,1,0:T(8,128)S(1)} collective-permute-done((f32[3,64,128]{2,1,0:T(8,128)S(1)}, f32[3,64,128]{2,1,0:T(8,128)S(1)}, u32[]{:S(2)}, u32[]{:S(2)}) %collective-permute-start.6) | collective-permute-done | bytes 98336 | tf_op jit(solution)/shard_map/ppermute | solution.py:459
  43.2 1.8 %shard_map.153 = (f32[256,128]{1,0:T(8,128)S(1)}, bf16[13,64,128]{2,1,0:T(8,128)(2,1)S(1)}, f32[256,128]{1,0:T(8,128)S(1)}, f32[12,64,128]{2,1,0:T(8,128)S(1)}, f32[16,128]{1,0:T(8,128)S(1)}) custom-call(s32[126]{0:T(128)S(1)} %concatenate.10.meta, f32[512,128]{1,0:T(8,128)S(1)} %bitcast.18, f32[4,64,128]{2,1,0:T(8,128)S(1)} %get-tuple-element.58.z_one, ...), custom_call_target="tpu_custom_call" | custom-call | tf_op jit(solution)/shard_map/pallas_call | solution.py:431
  45.1 18.0 %all_to_all.54 = f32[128,2,128]{2,1,0:T(2,128)S(1)} all-to-all(f32[128,2,128]{2,1,0:T(2,128)S(1)} %bitcast.23), channel_id=1, replica_groups=mesh['gx_0'=2,'gx_1'=4,'gy_0'=4,'gy_1'=2,'gy_2'=2] {'gx_0','gx_1','gy_0'..., dimensions={0} | all-to-all | bytes 262144 | tf_op jit(solution)/shard_map/all_to_all | solution.py:463
  64.4 14.2 %all_to_all.55 = f32[128,2,128]{2,1,0:T(2,128)S(1)} all-to-all(f32[128,2,128]{2,1,0:T(2,128)S(1)} %bitcast.24), channel_id=1, replica_groups=mesh['gx_0'=2,'gx_1'=4,'gy_0'=4,'gy_1'=2,'gy_2'=2] {'gx_0','gx_1','gy_0'..., dimensions={0} | all-to-all | bytes 262144 | tf_op jit(solution)/shard_map/all_to_all | solution.py:463
  78.5 2.9 %shard_map.155 = (bf16[256,128]{1,0:T(8,128)(2,1)S(1)}, f32[256,128]{1,0:T(8,128)S(1)}, bf16[3,64,128]{2,1,0:T(8,128)(2,1)S(1)}, bf16[3,64,128]{2,1,0:T(8,128)(2...) custom-call(s32[126]{0:T(128)S(1)} %concatenate.10.meta, ...), custom_call_target="tpu_custom_call" | custom-call | tf_op jit(solution)/shard_map/pallas_call | solution.py:431
  81.5 6.2 %all-to-all-start.3 = ((f32[128,2,128]{2,1,0:T(2,128)}), f32[128,2,128]{2,1,0:T(2,128)S(1)}, u32[]{:S(2)}, u32[]{:S(2)}) async-start(f32[128,2,128]{2,1,0:T(2,128)} %bitcast.14), calls=%async_computation.3 | async-start | bytes 262144 | tf_op jit(solution)/shard_map/all_to_all | solution.py:463
  91.2 4.2 %collective-permute-done.9.second.uy = bf16[3,64,128]{2,1,0:T(8,128)(2,1)S(1)} collective-permute-done((bf16[3,64,128]{2,1,0:T(8,128)(2,1)S(1)}, bf16[3,64,128]{2,1,0:T(8,128)(2,1)S(1)}, u32[]{:S(2)}, u32[]{:S(2)}) %collective-permute-start.9) | collective-permute-done | bytes 49184 | tf_op jit(solution)/shard_map/ppermute | solution.py:459
  95.3 3.7 %collective-permute-start.10 = (bf16[3,64,128]{2,1,0:T(8,128)(2,1)S(1)}, bf16[3,64,128]{2,1,0:T(8,128)(2,1)S(1)}, u32[]{:S(2)}, u32[]{:S(2)}) collective-permute-start(bf16[3,64,128]{2,1,0:T(8,128)(2,1)S(1)} %get-tuple-element.78), channel_id=1, source_target_pairs={{0,112},{16,0},{32,16},{48,32},{64,48},{80,64},{96,80},{112,96},{1... | collective-permute-start | bytes 147464 | tf_op jit(solution)/shard_map/ppermute | solution.py:459
  100.8 4.4 %collective-permute-done.11.ux = bf16[3,64,128]{2,1,0:T(8,128)(2,1)S(1)} collective-permute-done((bf16[3,64,128]{2,1,0:T(8,128)(2,1)S(1)}, bf16[3,64,128]{2,1,0:T(8,128)(2,1)S(1)}, u32[]{:S(2)}, u32[]{:S(2)}) %collective-permute-start.11) | collective-permute-done | bytes 49184 | tf_op jit(solution)/shard_map/ppermute | solution.py:459
  105.3 3.2 %shard_map.157 = (bf16[256,128]{1,0:T(8,128)(2,1)S(1)}, f32[256,128]{1,0:T(8,128)S(1)}, bf16[3,64,128]{2,1,0:T(8,128)(2,1)S(1)}, bf16[3,64,128]{2,1,0:T(8,128)(2...) custom-call(s32[126]{0:T(128)S(1)} %concatenate.10.meta, f32[256,128]{1,0:T(8,128)S(1)} %bitcast.19, ...), custom_call_target="tpu_custom_call" | custom-call | tf_op jit(solution)/shard_map/pallas_call | solution.py:431
  112.1 24.2 %all_to_all.56.pieces = bf16[64,56,128]{2,1,0:T(8,128)(2,1)S(1)} all-to-all(bf16[64,56,128]{2,1,0:T(8,128)(2,1)S(1)} %shard_map.163), channel_id=1, replica_groups=mesh['gx_0'=2,'gx_1'=4,'gy_0'=4,'gy_1'=2,'gy_2'=2] {'gx_0','gx_1','gy_0'..., dimensions={0} | all-to-all | bytes 1835008 | tf_op jit(solution)/shard_map/all_to_all | solution.py:463
  136.6 21.0 %all_to_all.57.half = bf16[64,56,128]{2,1,0:T(8,128)(2,1)S(1)} all-to-all(bf16[64,56,128]{2,1,0:T(8,128)(2,1)S(1)} %shard_map.164), channel_id=1, replica_groups=mesh['gx_0'=2,'gx_1'=4,'gy_0'=4,'gy_1'=2,'gy_2'=2] {'gx_0','gx_1','gy_0'..., dimensions={0} | all-to-all | bytes 1835008 | tf_op jit(solution)/shard_map/all_to_all | solution.py:463
  157.5 2.2 %collective-permute-start.12 = (bf16[3,64,128]{2,1,0:T(8,128)(2,1)S(1)}, bf16[3,64,128]{2,1,0:T(8,128)(2,1)S(1)}, u32[]{:S(2)}, u32[]{:S(2)}) collective-permute-start(bf16[3,64,128]{2,1,0:T(8,128)(2,1)S(1)} %get-tuple-element.83), channel_id=1, source_target_pairs={{0,15},{1,0},{2,1},{3,2},{4,3},{5,4},{6,5},{7,6},{8,7},{9,8},{10,9... | collective-permute-start | bytes 147464 | tf_op jit(solution)/shard_map/ppermute | solution.py:459
  161.5 4.2 %collective-permute-done.13.second.uy = bf16[3,64,128]{2,1,0:T(8,128)(2,1)S(1)} collective-permute-done((bf16[3,64,128]{2,1,0:T(8,128)(2,1)S(1)}, bf16[3,64,128]{2,1,0:T(8,128)(2,1)S(1)}, u32[]{:S(2)}, u32[]{:S(2)}) %collective-permute-start.13) | collective-permute-done | bytes 49184 | tf_op jit(solution)/shard_map/ppermute | solution.py:459
  165.6 2.2 %collective-permute-start.14 = (bf16[3,64,128]{2,1,0:T(8,128)(2,1)S(1)}, bf16[3,64,128]{2,1,0:T(8,128)(2,1)S(1)}, u32[]{:S(2)}, u32[]{:S(2)}) collective-permute-start(bf16[3,64,128]{2,1,0:T(8,128)(2,1)S(1)} %get-tuple-element.85), channel_id=1, source_target_pairs={{0,112},{16,0},{32,16},{48,32},{64,48},{80,64},{96,80},{112,96},{1... | collective-permute-start | bytes 147464 | tf_op jit(solution)/shard_map/ppermute | solution.py:459
  167.9 1.9 %collective-permute-done.14.lx = bf16[3,64,128]{2,1,0:T(8,128)(2,1)S(1)} collective-permute-done((bf16[3,64,128]{2,1,0:T(8,128)(2,1)S(1)}, bf16[3,64,128]{2,1,0:T(8,128)(2,1)S(1)}, u32[]{:S(2)}, u32[]{:S(2)}) %collective-permute-start.14) | collective-permute-done | bytes 49184 | tf_op jit(solution)/shard_map/ppermute | solution.py:459
  169.8 4.3 %collective-permute-done.15.ux = bf16[3,64,128]{2,1,0:T(8,128)(2,1)S(1)} collective-permute-done((bf16[3,64,128]{2,1,0:T(8,128)(2,1)S(1)}, bf16[3,64,128]{2,1,0:T(8,128)(2,1)S(1)}, u32[]{:S(2)}, u32[]{:S(2)}) %collective-permute-start.15) | collective-permute-done | bytes 49184 | tf_op jit(solution)/shard_map/ppermute | solution.py:459
  (57 shorter events, 27.4 us)
Async XLA Ops:
  0.6 39.3 %copy-start.3 = (f32[2,128]{1,0:T(2,128)S(1)}, f32[2,128]{1,0:T(2,128)}, u32[]{:S(2)}) copy-start(f32[2,128]{1,0:T(2,128)} %param.16) | copy-start | bytes 3076
  2.8 6.0 %collective-permute-start = (bf16[3,64,128]{2,1,0:T(8,128)(2,1)S(1)}, bf16[3,64,128]{2,1,0:T(8,128)(2,1)S(1)}, u32[]{:S(2)}, u32[]{:S(2)}) collective-permute-start(bf16[3,64,128]{2,1,0:T(8,128)(2,1)S(1)} %get-tuple-element.53), channel_id=1, source_target_pairs={{0,1},{1,2},{2,3},{3,4},{4,5},{5,6},{6,7},{7,8},{8,9},{9,10},{10,1... | collective-permute-start | bytes 147464 | tf_op jit(solution)/shard_map/ppermute | solution.py:459
  2.9 5.9 %collective-permute-start.1 = (bf16[3,64,128]{2,1,0:T(8,128)(2,1)S(1)}, bf16[3,64,128]{2,1,0:T(8,128)(2,1)S(1)}, u32[]{:S(2)}, u32[]{:S(2)}) collective-permute-start(bf16[3,64,128]{2,1,0:T(8,128)(2,1)S(1)} %get-tuple-element.54), channel_id=1, source_target_pairs={{0,15},{1,0},{2,1},{3,2},{4,3},{5,4},{6,5},{7,6},{8,7},{9,8},{10,9... | collective-permute-start | bytes 147464 | tf_op jit(solution)/shard_map/ppermute | solution.py:459
  8.8 8.3 %collective-permute-start.2 = (bf16[3,64,128]{2,1,0:T(8,128)(2,1)S(1)}, bf16[3,64,128]{2,1,0:T(8,128)(2,1)S(1)}, u32[]{:S(2)}, u32[]{:S(2)}) collective-permute-start(bf16[3,64,128]{2,1,0:T(8,128)(2,1)S(1)} %get-tuple-element.55), channel_id=1, source_target_pairs={{0,16},{16,32},{32,48},{48,64},{64,80},{80,96},{96,112},{112,0},{1... | collective-permute-start | bytes 147464 | tf_op jit(solution)/shard_map/ppermute | solution.py:459
  10.5 6.6 %collective-permute-start.3 = (bf16[3,64,128]{2,1,0:T(8,128)(2,1)S(1)}, bf16[3,64,128]{2,1,0:T(8,128)(2,1)S(1)}, u32[]{:S(2)}, u32[]{:S(2)}) collective-permute-start(bf16[3,64,128]{2,1,0:T(8,128)(2,1)S(1)} %get-tuple-element.56), channel_id=1, source_target_pairs={{0,112},{16,0},{32,16},{48,32},{64,48},{80,64},{96,80},{112,96},{1... | collective-permute-start | bytes 147464 | tf_op jit(solution)/shard_map/ppermute | solution.py:459
  15.1 48.0 %copy-start.1 = (bf16[4,64,128]{2,1,0:T(8,128)(2,1)S(1)}, bf16[4,64,128]{2,1,0:T(8,128)(2,1)}, u32[]{:S(2)}) copy-start(bf16[4,64,128]{2,1,0:T(8,128)(2,1)} %field.1) | copy-start | bytes 196612
  15.1 48.0 %copy-start.2 = (bf16[4,64,128]{2,1,0:T(8,128)(2,1)S(1)}, bf16[4,64,128]{2,1,0:T(8,128)(2,1)}, u32[]{:S(2)}) copy-start(bf16[4,64,128]{2,1,0:T(8,128)(2,1)} %param.17) | copy-start | bytes 196612
  19.4 23.8 %all-to-all-start = ((f32[128,4,128]{2,1,0:T(4,128)}), f32[128,4,128]{2,1,0:T(4,128)S(1)}, u32[]{:S(2)}, u32[]{:S(2)}) async-start(f32[128,4,128]{2,1,0:T(4,128)} %bitcast.4), calls=%async_computation | async-start | bytes 524288 | tf_op jit(solution)/shard_map/all_to_all | solution.py:463
  28.9 6.8 %collective-permute-start.4 = (f32[3,64,128]{2,1,0:T(8,128)S(1)}, f32[3,64,128]{2,1,0:T(8,128)S(1)}, u32[]{:S(2)}, u32[]{:S(2)}) collective-permute-start(f32[3,64,128]{2,1,0:T(8,128)S(1)} %get-tuple-element.60), channel_id=1, source_target_pairs={{0,1},{1,2},{2,3},{3,4},{4,5},{5,6},{6,7},{7,8},{8,9},{9,10},{10,1... | collective-permute-start | bytes 294920 | tf_op jit(solution)/shard_map/ppermute | solution.py:459
  29.1 6.6 %collective-permute-start.5 = (f32[3,64,128]{2,1,0:T(8,128)S(1)}, f32[3,64,128]{2,1,0:T(8,128)S(1)}, u32[]{:S(2)}, u32[]{:S(2)}) collective-permute-start(f32[3,64,128]{2,1,0:T(8,128)S(1)} %get-tuple-element.61), channel_id=1, source_target_pairs={{0,15},{1,0},{2,1},{3,2},{4,3},{5,4},{6,5},{7,6},{8,7},{9,8},{10,9... | collective-permute-start | bytes 294920 | tf_op jit(solution)/shard_map/ppermute | solution.py:459
  35.7 7.5 %collective-permute-start.6 = (f32[3,64,128]{2,1,0:T(8,128)S(1)}, f32[3,64,128]{2,1,0:T(8,128)S(1)}, u32[]{:S(2)}, u32[]{:S(2)}) collective-permute-start(f32[3,64,128]{2,1,0:T(8,128)S(1)} %get-tuple-element.62), channel_id=1, source_target_pairs={{0,16},{16,32},{32,48},{48,64},{64,80},{80,96},{96,112},{112,0},{1... | collective-permute-start | bytes 294920 | tf_op jit(solution)/shard_map/ppermute | solution.py:459
  37.1 6.1 %collective-permute-start.7 = (f32[3,64,128]{2,1,0:T(8,128)S(1)}, f32[3,64,128]{2,1,0:T(8,128)S(1)}, u32[]{:S(2)}, u32[]{:S(2)}) collective-permute-start(f32[3,64,128]{2,1,0:T(8,128)S(1)} %get-tuple-element.63), channel_id=1, source_target_pairs={{0,112},{16,0},{32,16},{48,32},{64,48},{80,64},{96,80},{112,96},{1... | collective-permute-start | bytes 294920 | tf_op jit(solution)/shard_map/ppermute | solution.py:459
  81.5 23.8 %all-to-all-start.3 = ((f32[128,2,128]{2,1,0:T(2,128)}), f32[128,2,128]{2,1,0:T(2,128)S(1)}, u32[]{:S(2)}, u32[]{:S(2)}) async-start(f32[128,2,128]{2,1,0:T(2,128)} %bitcast.14), calls=%async_computation.3 | async-start | bytes 262144 | tf_op jit(solution)/shard_map/all_to_all | solution.py:463
  87.7 3.5 %collective-permute-start.8 = (bf16[3,64,128]{2,1,0:T(8,128)(2,1)S(1)}, bf16[3,64,128]{2,1,0:T(8,128)(2,1)S(1)}, u32[]{:S(2)}, u32[]{:S(2)}) collective-permute-start(bf16[3,64,128]{2,1,0:T(8,128)(2,1)S(1)} %get-tuple-element.76), channel_id=1, source_target_pairs={{0,15},{1,0},{2,1},{3,2},{4,3},{5,4},{6,5},{7,6},{8,7},{9,8},{10,9... | collective-permute-start | bytes 147464 | tf_op jit(solution)/shard_map/ppermute | solution.py:459
  89.4 5.9 %collective-permute-start.9 = (bf16[3,64,128]{2,1,0:T(8,128)(2,1)S(1)}, bf16[3,64,128]{2,1,0:T(8,128)(2,1)S(1)}, u32[]{:S(2)}, u32[]{:S(2)}) collective-permute-start(bf16[3,64,128]{2,1,0:T(8,128)(2,1)S(1)} %get-tuple-element.77), channel_id=1, source_target_pairs={{0,1},{1,2},{2,3},{3,4},{4,5},{5,6},{6,7},{7,8},{8,9},{9,10},{10,1... | collective-permute-start | bytes 147464 | tf_op jit(solution)/shard_map/ppermute | solution.py:459
  95.3 5.5 %collective-permute-start.10 = (bf16[3,64,128]{2,1,0:T(8,128)(2,1)S(1)}, bf16[3,64,128]{2,1,0:T(8,128)(2,1)S(1)}, u32[]{:S(2)}, u32[]{:S(2)}) collective-permute-start(bf16[3,64,128]{2,1,0:T(8,128)(2,1)S(1)} %get-tuple-element.78), channel_id=1, source_target_pairs={{0,112},{16,0},{32,16},{48,32},{64,48},{80,64},{96,80},{112,96},{1... | collective-permute-start | bytes 147464 | tf_op jit(solution)/shard_map/ppermute | solution.py:459
  99.1 6.2 %collective-permute-start.11 = (bf16[3,64,128]{2,1,0:T(8,128)(2,1)S(1)}, bf16[3,64,128]{2,1,0:T(8,128)(2,1)S(1)}, u32[]{:S(2)}, u32[]{:S(2)}) collective-permute-start(bf16[3,64,128]{2,1,0:T(8,128)(2,1)S(1)} %get-tuple-element.79), channel_id=1, source_target_pairs={{0,16},{16,32},{32,48},{48,64},{64,80},{80,96},{96,112},{112,0},{1... | collective-permute-start | bytes 147464 | tf_op jit(solution)/shard_map/ppermute | solution.py:459
  100.7 9.5 %collective-permute-start.17 = (bf16[32,56,128]{2,1,0:T(8,128)(2,1)S(1)}, bf16[32,56,128]{2,1,0:T(8,128)(2,1)S(1)}, u32[]{:S(2)}, u32[]{:S(2)}) collective-permute-start(bf16[32,56,128]{2,1,0:T(8,128)(2,1)S(1)} %get-tuple-element.96), channel_id=1, source_target_pairs={{0,1},{1,0},{2,3},{3,2},{4,5},{5,4},{6,7},{7,6},{8,9},{9,8},{10,11... | collective-permute-start | bytes 1376264 | tf_op jit(solution)/shard_map/ppermute | solution.py:467
  110.1 1.9 %collective-permute-start.16 = (bf16[32,56,128]{2,1,0:T(8,128)(2,1)S(1)}, bf16[32,56,128]{2,1,0:T(8,128)(2,1)S(1)}, u32[]{:S(2)}, u32[]{:S(2)}) collective-permute-start(bf16[32,56,128]{2,1,0:T(8,128)(2,1)S(1)} %get-tuple-element.92), channel_id=1, source_target_pairs={{0,1},{1,0},{2,3},{3,2},{4,5},{5,4},{6,7},{7,6},{8,9},{9,8},{10,11... | collective-permute-start | bytes 1376264 | tf_op jit(solution)/shard_map/ppermute | solution.py:467
  157.5 19.1 %collective-permute-start.18 = (bf16[64,56,128]{2,1,0:T(8,128)(2,1)S(1)}, bf16[64,56,128]{2,1,0:T(8,128)(2,1)S(1)}, u32[]{:S(2)}, u32[]{:S(2)}) collective-permute-start(bf16[64,56,128]{2,1,0:T(8,128)(2,1)S(1)} %all_to_all.57.half), channel_id=1, source_target_pairs={{0,1},{1,0},{2,3},{3,2},{4,5},{5,4},{6,7},{7,6},{8,9},{9,8},{10,11... | collective-permute-start | bytes 2752520 | tf_op jit(solution)/shard_map/ppermute | solution.py:467
  157.5 3.9 %collective-permute-start.12 = (bf16[3,64,128]{2,1,0:T(8,128)(2,1)S(1)}, bf16[3,64,128]{2,1,0:T(8,128)(2,1)S(1)}, u32[]{:S(2)}, u32[]{:S(2)}) collective-permute-start(bf16[3,64,128]{2,1,0:T(8,128)(2,1)S(1)} %get-tuple-element.83), channel_id=1, source_target_pairs={{0,15},{1,0},{2,1},{3,2},{4,3},{5,4},{6,5},{7,6},{8,7},{9,8},{10,9... | collective-permute-start | bytes 147464 | tf_op jit(solution)/shard_map/ppermute | solution.py:459
  159.7 5.9 %collective-permute-start.13 = (bf16[3,64,128]{2,1,0:T(8,128)(2,1)S(1)}, bf16[3,64,128]{2,1,0:T(8,128)(2,1)S(1)}, u32[]{:S(2)}, u32[]{:S(2)}) collective-permute-start(bf16[3,64,128]{2,1,0:T(8,128)(2,1)S(1)} %get-tuple-element.84), channel_id=1, source_target_pairs={{0,1},{1,2},{2,3},{3,4},{4,5},{5,6},{6,7},{7,8},{8,9},{9,10},{10,1... | collective-permute-start | bytes 147464 | tf_op jit(solution)/shard_map/ppermute | solution.py:459
  165.6 4.2 %collective-permute-start.14 = (bf16[3,64,128]{2,1,0:T(8,128)(2,1)S(1)}, bf16[3,64,128]{2,1,0:T(8,128)(2,1)S(1)}, u32[]{:S(2)}, u32[]{:S(2)}) collective-permute-start(bf16[3,64,128]{2,1,0:T(8,128)(2,1)S(1)} %get-tuple-element.85), channel_id=1, source_target_pairs={{0,112},{16,0},{32,16},{48,32},{64,48},{80,64},{96,80},{112,96},{1... | collective-permute-start | bytes 147464 | tf_op jit(solution)/shard_map/ppermute | solution.py:459
  167.9 6.2 %collective-permute-start.15 = (bf16[3,64,128]{2,1,0:T(8,128)(2,1)S(1)}, bf16[3,64,128]{2,1,0:T(8,128)(2,1)S(1)}, u32[]{:S(2)}, u32[]{:S(2)}) collective-permute-start(bf16[3,64,128]{2,1,0:T(8,128)(2,1)S(1)} %get-tuple-element.86), channel_id=1, source_target_pairs={{0,16},{16,32},{32,48},{48,64},{64,80},{80,96},{96,112},{112,0},{1... | collective-permute-start | bytes 147464 | tf_op jit(solution)/shard_map/ppermute | solution.py:459
  (2 other events, 40.1 us)

commit v6 on v5

--- a/solution.py
+++ b/solution.py
@@ -73,7 +73,7 @@
     return (brick < meta[COUNT]).astype(F32)
 
 
-def gather_columns(meta, ext, gathered, columns):
+def shifted_planes(meta, ext, gathered, planes):
     shift = shift_matrix(False)
     for b in range(NB):
         for plane, oa, source in sources():
@@ -83,20 +83,29 @@
                     entry, 16 * source : 16 * source + 16, :
                 ]
     for b in range(NB):
-        moved = jnp.dot(
-            shift, gathered[:, 6 * b * C : 6 * (b + 1) * C], preferred_element_type=F32
-        ).astype(BF16)
-        for a in range(3):
-            for p in range(4):
-                for d in range(9):
-                    k = 9 * a + d
-                    columns[64 * b + 16 * p : 64 * b + 16 * p + 16, k * C : (k + 1) * C] = moved[
-                        16 * d : 16 * d + 16, (p + a) * C : (p + a + 1) * C
-                    ]
-
-
-def convolve(columns, weight):
-    return jnp.dot(columns[...], weight[...], preferred_element_type=F32)
+        at = slice(6 * b * C, 6 * (b + 1) * C)
+        planes[:, at] = jnp.dot(shift, gathered[:, at], preferred_element_type=F32).astype(BF16)
+
+
+def patches(planes, k):
+    a, d = divmod(k, 9)
+    tiles = [
+        planes[16 * d : 16 * d + 16, (6 * b + p + a) * C : (6 * b + p + a + 1) * C]
+        for b in range(NB)
+        for p in range(4)
+    ]
+    return jnp.concatenate(tiles, axis=0)
+
+
+def convolve(planes, weight):
+    total = jnp.zeros((ROWS, C), F32)
+    for k in range(0, TAPS, 2):
+        taps = range(k, min(k + 2, TAPS))
+        columns = jnp.concatenate([patches(planes, tap) for tap in taps], axis=1)
+        total += jnp.dot(
+            columns, weight[k * C : (k + len(taps)) * C, :], preferred_element_type=F32
+        )
+    return total
 
 
 def convolve_back(meta, dz, weight, spread, moved, acc):
@@ -178,10 +187,18 @@
         out[...] = field[entry]
 
 
-def send_kernel(lists, field, y_up, y_low, x_faces, kept):
-    kept[...] = field[...]
-    for entry, out in sends_of(lambda k: lists[k], lambda k: lists[4 + k], y_up, y_low, x_faces):
-        out[...] = field[entry]
+def send_kernel(face_far, corner_far, field, y_up, y_low, x_faces, kept, face, corner, sems):
+    copies = [
+        pltpu.make_async_copy(field, kept, sems.at[0]),
+        pltpu.make_async_copy(face_far, face, sems.at[1]),
+        pltpu.make_async_copy(corner_far, corner, sems.at[2]),
+    ]
+    for copy in copies:
+        copy.start()
+    for copy in copies:
+        copy.wait()
+    for entry, out in sends_of(lambda k: face[k], lambda k: corner[k], y_up, y_low, x_faces):
+        out[...] = kept[entry]
 
 
 def fetch_one_kernel(far, out, sem):
@@ -207,7 +224,7 @@
 
 def first_kernel(
     meta, voxel_feats, ux, lx, uy, ly, weight,
-    z_out, ext, sums, y_up, y_low, x_faces, gathered, columns,
+    z_out, ext, sums, y_up, y_low, x_faces, gathered, planes,
 ):
     ext[NB + 8] = jnp.zeros((64, C), BF16)
     for b in range(NB):
@@ -216,8 +233,8 @@
     for e, brick in enumerate(received_bricks(ux, lx, uy, ly)):
         keep = meta[VALID + e].astype(F32)
         ext[NB + e] = (brick[...].astype(F32) * keep).astype(BF16)
-    gather_columns(meta, ext, gathered, columns)
-    z = convolve(columns, weight)
+    shifted_planes(meta, ext, gathered, planes)
+    z = convolve(planes, weight)
     z_out[...] = z.reshape(NB, 64, C)
     select_sends(meta, z_out, y_up, y_low, x_faces)
     masked = z * occupied_rows(meta)
@@ -231,7 +248,7 @@
 
 def second_kernel(
     meta, got, z_one, ux, lx, uy, ly, norm, weight,
-    z_out, ext, sums, xh_out, consts, gathered, columns,
+    z_out, ext, sums, xh_out, consts, gathered, planes,
 ):
     row = lax.broadcasted_iota(jnp.int32, (8, C), 0) % 4
     both = jnp.sum(got[...].reshape(64, 8, C), axis=0)
@@ -251,8 +268,8 @@
         u = norm[0:1] * xh + norm[2:3]
         ext[e] = (u * sigmoid(u) * keep.astype(F32)).astype(BF16)
     ext[EXT - 1] = jnp.zeros((64, C), BF16)
-    gather_columns(meta, ext, gathered, columns)
-    z = convolve(columns, weight)
+    shifted_planes(meta, ext, gathered, planes)
+    z = convolve(planes, weight)
     z_out[...] = z
     masked = z * occupied_rows(meta)
     write_sums(sums, rows_sum(masked), rows_sum(z * masked))
@@ -351,11 +368,11 @@
     send_gradients(acc, own, y_low, y_up, x_faces)
 
 
-def taps_kernel(meta, ext, dz, mine, other, gathered, columns, taps):
-    gather_columns(meta, ext, gathered, columns)
+def taps_kernel(meta, ext, dz, mine, other, gathered, planes, taps):
+    shifted_planes(meta, ext, gathered, planes)
     for k in range(TAPS):
         taps[k * C : (k + 1) * C, :] = lax.dot_general(
-            columns[:, k * C : (k + 1) * C],
+            patches(planes, k),
             dz[...],
             (((0,), (0,)), ((), ())),
             preferred_element_type=F32,
@@ -502,7 +519,8 @@
     face_send,
     corner_send,
 ):
-    lists = jnp.concatenate([face_send.reshape(4), corner_send.reshape(4)])
+    face = face_send.reshape(4)
+    corner = corner_send.reshape(4)
     i = lax.axis_index(GX)
     j = lax.axis_index(GY)
     dx = np.array([d[0] for d in NEIGHBOURS], np.int32)
@@ -512,7 +530,8 @@
         [
             kernel_map.reshape(-1),
             brick_count,
-            lists,
+            face,
+            corner,
             inside.astype(jnp.int32),
             lax.axis_index(CORE).reshape(1),
         ]
@@ -530,13 +549,14 @@
     sem = pltpu.SemaphoreType.DMA
     weight = ((TAPS * C, C), BF16)
     gathered = ((144, 6 * NB * C), BF16)
-    columns = ((ROWS, TAPS * C), BF16)
-    forward = [gathered, columns]
+    forward = [gathered, gathered]
 
     *sends, kept = local(
         send_kernel,
         [(three, BF16), (three, BF16), (two, BF16), ((NB,) + brick, BF16)],
-        [lists, voxel_feats],
+        [face, corner, voxel_feats],
+        [pltpu.SMEM((4,), jnp.int32), pltpu.SMEM((4,), jnp.int32), sem((3,))],
+        far=(0, 1, 2),
     )
     (near_one,) = local(fetch_one_kernel, [weight], [flat_one], [sem(())], far=(0,))
     (near_two,) = local(fetch_two_kernel, [weight], [flat_two], [sem(())], far=(0,))
@@ -572,7 +592,7 @@
     returned = homeward(y_low, y_up, x_faces)
     chunks = (32, CHUNK, C)
     halves = [(chunks, F32), (chunks, BF16)]
-    products = [gathered, columns, ((TAPS * C, C), F32)]
+    products = [gathered, gathered, ((TAPS * C, C), F32)]
     mine, other = local(taps_kernel, halves, [meta, ext_two, dz_two], products)
     (second,) = local(second_sum_kernel, [(chunks, BF16)], [mine, swap(other)])
     part = exchange(part, GX_GY)

time: 181 us -> 179 us (0.989)
  no operation moved by 1% of the time
where the time goes in v6:
time: 179 us; the launch traced here: 177 us
  blocking collectives  77.4 us (43%)
  starting transfers between devices  42.5 us (24%)
  waiting for transfers between devices  30.7 us (17%)
  Pallas kernels  22.3 us (12%)
    all_to_all x4, blocking collectives, exchange(): return lax.all_to_all(value, axes, 0, 0, tiled=True)  77.4 us
    ppermute x16, waiting for transfers between devices, shifted(): lax.ppermute(value, axis, [(i, (i + by) % length) for i in range(length)])  29 us
    ppermute x16, starting transfers between devices, shifted(): lax.ppermute(value, axis, [(i, (i + by) % length) for i in range(length)])  26.7 us
    pallas_call x18, Pallas kernels, local(): pl.pallas_call(kernel, out_shape=[jax.ShapeDtypeStruct(s, d) for s, d in...  19.7 us
    all_to_all x2, starting transfers between devices, exchange(): return lax.all_to_all(value, axes, 0, 0, tiled=True)  15.7 us
  transfers between devices with their start and end apart: 21, of which 11 were waited for; matrix products, arithmetic and copies ran while one was open for 1% of the time, Pallas kernels for 6%

profile of v6, /device:TPU:34, one launch (start us, length us, event | category | flops | bytes accessed | tf_op | source)
XLA Modules:
  0.0 176.8 jit_solution(15396381025787610501)
XLA Ops:
  1.6 4.1 %collective-permute-start.1 = (bf16[3,64,128]{2,1,0:T(8,128)(2,1)S(1)}, bf16[3,64,128]{2,1,0:T(8,128)(2,1)S(1)}, u32[]{:S(2)}, u32[]{:S(2)}) collective-permute-start(bf16[3,64,128]{2,1,0:T(8,128)(2,1)S(1)} %get-tuple-element.54), channel_id=1, source_target_pairs={{0,15},{1,0},{2,1},{3,2},{4,3},{5,4},{6,5},{7,6},{8,7},{9,8},{10,9... | collective-permute-start | bytes 147464 | tf_op jit(solution)/shard_map/ppermute | solution.py:476
  5.8 1.8 %collective-permute-done.first.uy = bf16[3,64,128]{2,1,0:T(8,128)(2,1)S(1)} collective-permute-done((bf16[3,64,128]{2,1,0:T(8,128)(2,1)S(1)}, bf16[3,64,128]{2,1,0:T(8,128)(2,1)S(1)}, u32[]{:S(2)}, u32[]{:S(2)}) %collective-permute-start) | collective-permute-done | bytes 49184 | tf_op jit(solution)/shard_map/ppermute | solution.py:476
  9.2 2.6 %collective-permute-start.3 = (bf16[3,64,128]{2,1,0:T(8,128)(2,1)S(1)}, bf16[3,64,128]{2,1,0:T(8,128)(2,1)S(1)}, u32[]{:S(2)}, u32[]{:S(2)}) collective-permute-start(bf16[3,64,128]{2,1,0:T(8,128)(2,1)S(1)} %get-tuple-element.56), channel_id=1, source_target_pairs={{0,112},{16,0},{32,16},{48,32},{64,48},{80,64},{96,80},{112,96},{1... | collective-permute-start | bytes 147464 | tf_op jit(solution)/shard_map/ppermute | solution.py:476
  15.9 2.3 %shard_map.150 = (f32[4,64,128]{2,1,0:T(8,128)S(1)}, bf16[13,64,128]{2,1,0:T(8,128)(2,1)S(1)}, f32[512,128]{1,0:T(8,128)}, f32[3,64,128]{2,1,0:T(8,128)S(1)}, f3...) custom-call(s32[126]{0:T(128)S(1)} %concatenate.6.meta, bf16[4,64,128]{2,1,0:T(8,128)(2,1)S(1)} %get-tuple-element.51.voxel_feats, ...), custom_call_target="tpu_custom_call" | custom-call | tf_op jit(solution)/shard_map/pallas_call | solution.py:448
  18.2 9.5 %all-to-all-start = ((f32[128,4,128]{2,1,0:T(4,128)}), f32[128,4,128]{2,1,0:T(4,128)S(1)}, u32[]{:S(2)}, u32[]{:S(2)}) async-start(f32[128,4,128]{2,1,0:T(4,128)} %bitcast.4), calls=%async_computation | async-start | bytes 524288 | tf_op jit(solution)/shard_map/all_to_all | solution.py:480
  27.8 4.0 %collective-permute-start.5 = (f32[3,64,128]{2,1,0:T(8,128)S(1)}, f32[3,64,128]{2,1,0:T(8,128)S(1)}, u32[]{:S(2)}, u32[]{:S(2)}) collective-permute-start(f32[3,64,128]{2,1,0:T(8,128)S(1)} %get-tuple-element.61), channel_id=1, source_target_pairs={{0,15},{1,0},{2,1},{3,2},{4,3},{5,4},{6,5},{7,6},{8,7},{9,8},{10,9... | collective-permute-start | bytes 294920 | tf_op jit(solution)/shard_map/ppermute | solution.py:476
  35.9 2.8 %collective-permute-start.7 = (f32[3,64,128]{2,1,0:T(8,128)S(1)}, f32[3,64,128]{2,1,0:T(8,128)S(1)}, u32[]{:S(2)}, u32[]{:S(2)}) collective-permute-start(f32[3,64,128]{2,1,0:T(8,128)S(1)} %get-tuple-element.63), channel_id=1, source_target_pairs={{0,112},{16,0},{32,16},{48,32},{64,48},{80,64},{96,80},{112,96},{1... | collective-permute-start | bytes 294920 | tf_op jit(solution)/shard_map/ppermute | solution.py:476
  38.7 3.3 %collective-permute-done.6.ux = f32[3,64,128]{2,1,0:T(8,128)S(1)} collective-permute-done((f32[3,64,128]{2,1,0:T(8,128)S(1)}, f32[3,64,128]{2,1,0:T(8,128)S(1)}, u32[]{:S(2)}, u32[]{:S(2)}) %collective-permute-start.6) | collective-permute-done | bytes 98336 | tf_op jit(solution)/shard_map/ppermute | solution.py:476
  42.0 1.8 %shard_map.153 = (f32[256,128]{1,0:T(8,128)S(1)}, bf16[13,64,128]{2,1,0:T(8,128)(2,1)S(1)}, f32[256,128]{1,0:T(8,128)S(1)}, f32[12,64,128]{2,1,0:T(8,128)S(1)}, f32[16,128]{1,0:T(8,128)S(1)}) custom-call(s32[126]{0:T(128)S(1)} %concatenate.6.meta, f32[512,128]{1,0:T(8,128)S(1)} %bitcast.18, f32[4,64,128]{2,1,0:T(8,128)S(1)} %get-tuple-element.58.z_one, ...), custom_call_target="tpu_custom_call" | custom-call | tf_op jit(solution)/shard_map/pallas_call | solution.py:448
  43.8 18.0 %all_to_all.54 = f32[128,2,128]{2,1,0:T(2,128)S(1)} all-to-all(f32[128,2,128]{2,1,0:T(2,128)S(1)} %bitcast.23), channel_id=1, replica_groups=mesh['gx_0'=2,'gx_1'=4,'gy_0'=4,'gy_1'=2,'gy_2'=2] {'gx_0','gx_1','gy_0'..., dimensions={0} | all-to-all | bytes 262144 | tf_op jit(solution)/shard_map/all_to_all | solution.py:480
  63.1 14.2 %all_to_all.55 = f32[128,2,128]{2,1,0:T(2,128)S(1)} all-to-all(f32[128,2,128]{2,1,0:T(2,128)S(1)} %bitcast.24), channel_id=1, replica_groups=mesh['gx_0'=2,'gx_1'=4,'gy_0'=4,'gy_1'=2,'gy_2'=2] {'gx_0','gx_1','gy_0'..., dimensions={0} | all-to-all | bytes 262144 | tf_op jit(solution)/shard_map/all_to_all | solution.py:480
  77.3 2.9 %shard_map.155 = (bf16[256,128]{1,0:T(8,128)(2,1)S(1)}, f32[256,128]{1,0:T(8,128)S(1)}, bf16[3,64,128]{2,1,0:T(8,128)(2,1)S(1)}, bf16[3,64,128]{2,1,0:T(8,128)(2...) custom-call(s32[126]{0:T(128)S(1)} %concatenate.6.meta, ...), custom_call_target="tpu_custom_call" | custom-call | tf_op jit(solution)/shard_map/pallas_call | solution.py:448
  80.2 6.2 %all-to-all-start.3 = ((f32[128,2,128]{2,1,0:T(2,128)}), f32[128,2,128]{2,1,0:T(2,128)S(1)}, u32[]{:S(2)}, u32[]{:S(2)}) async-start(f32[128,2,128]{2,1,0:T(2,128)} %bitcast.14), calls=%async_computation.3 | async-start | bytes 262144 | tf_op jit(solution)/shard_map/all_to_all | solution.py:480
  89.9 4.2 %collective-permute-done.9.second.uy = bf16[3,64,128]{2,1,0:T(8,128)(2,1)S(1)} collective-permute-done((bf16[3,64,128]{2,1,0:T(8,128)(2,1)S(1)}, bf16[3,64,128]{2,1,0:T(8,128)(2,1)S(1)}, u32[]{:S(2)}, u32[]{:S(2)}) %collective-permute-start.9) | collective-permute-done | bytes 49184 | tf_op jit(solution)/shard_map/ppermute | solution.py:476
  94.1 3.7 %collective-permute-start.10 = (bf16[3,64,128]{2,1,0:T(8,128)(2,1)S(1)}, bf16[3,64,128]{2,1,0:T(8,128)(2,1)S(1)}, u32[]{:S(2)}, u32[]{:S(2)}) collective-permute-start(bf16[3,64,128]{2,1,0:T(8,128)(2,1)S(1)} %get-tuple-element.78), channel_id=1, source_target_pairs={{0,112},{16,0},{32,16},{48,32},{64,48},{80,64},{96,80},{112,96},{1... | collective-permute-start | bytes 147464 | tf_op jit(solution)/shard_map/ppermute | solution.py:476
  99.5 4.4 %collective-permute-done.11.ux = bf16[3,64,128]{2,1,0:T(8,128)(2,1)S(1)} collective-permute-done((bf16[3,64,128]{2,1,0:T(8,128)(2,1)S(1)}, bf16[3,64,128]{2,1,0:T(8,128)(2,1)S(1)}, u32[]{:S(2)}, u32[]{:S(2)}) %collective-permute-start.11) | collective-permute-done | bytes 49184 | tf_op jit(solution)/shard_map/ppermute | solution.py:476
  104.0 3.2 %shard_map.157 = (bf16[256,128]{1,0:T(8,128)(2,1)S(1)}, f32[256,128]{1,0:T(8,128)S(1)}, bf16[3,64,128]{2,1,0:T(8,128)(2,1)S(1)}, bf16[3,64,128]{2,1,0:T(8,128)(2...) custom-call(s32[126]{0:T(128)S(1)} %concatenate.6.meta, f32[256,128]{1,0:T(8,128)S(1)} %bitcast.19, ...), custom_call_target="tpu_custom_call" | custom-call | tf_op jit(solution)/shard_map/pallas_call | solution.py:448
  110.8 24.2 %all_to_all.56.pieces = bf16[64,56,128]{2,1,0:T(8,128)(2,1)S(1)} all-to-all(bf16[64,56,128]{2,1,0:T(8,128)(2,1)S(1)} %shard_map.163), channel_id=1, replica_groups=mesh['gx_0'=2,'gx_1'=4,'gy_0'=4,'gy_1'=2,'gy_2'=2] {'gx_0','gx_1','gy_0'..., dimensions={0} | all-to-all | bytes 1835008 | tf_op jit(solution)/shard_map/all_to_all | solution.py:480
  135.3 21.0 %all_to_all.57.half = bf16[64,56,128]{2,1,0:T(8,128)(2,1)S(1)} all-to-all(bf16[64,56,128]{2,1,0:T(8,128)(2,1)S(1)} %shard_map.164), channel_id=1, replica_groups=mesh['gx_0'=2,'gx_1'=4,'gy_0'=4,'gy_1'=2,'gy_2'=2] {'gx_0','gx_1','gy_0'..., dimensions={0} | all-to-all | bytes 1835008 | tf_op jit(solution)/shard_map/all_to_all | solution.py:480
  156.3 2.2 %collective-permute-start.12 = (bf16[3,64,128]{2,1,0:T(8,128)(2,1)S(1)}, bf16[3,64,128]{2,1,0:T(8,128)(2,1)S(1)}, u32[]{:S(2)}, u32[]{:S(2)}) collective-permute-start(bf16[3,64,128]{2,1,0:T(8,128)(2,1)S(1)} %get-tuple-element.83), channel_id=1, source_target_pairs={{0,15},{1,0},{2,1},{3,2},{4,3},{5,4},{6,5},{7,6},{8,7},{9,8},{10,9... | collective-permute-start | bytes 147464 | tf_op jit(solution)/shard_map/ppermute | solution.py:476
  160.2 4.2 %collective-permute-done.13.second.uy = bf16[3,64,128]{2,1,0:T(8,128)(2,1)S(1)} collective-permute-done((bf16[3,64,128]{2,1,0:T(8,128)(2,1)S(1)}, bf16[3,64,128]{2,1,0:T(8,128)(2,1)S(1)}, u32[]{:S(2)}, u32[]{:S(2)}) %collective-permute-start.13) | collective-permute-done | bytes 49184 | tf_op jit(solution)/shard_map/ppermute | solution.py:476
  164.4 2.2 %collective-permute-start.14 = (bf16[3,64,128]{2,1,0:T(8,128)(2,1)S(1)}, bf16[3,64,128]{2,1,0:T(8,128)(2,1)S(1)}, u32[]{:S(2)}, u32[]{:S(2)}) collective-permute-start(bf16[3,64,128]{2,1,0:T(8,128)(2,1)S(1)} %get-tuple-element.85), channel_id=1, source_target_pairs={{0,112},{16,0},{32,16},{48,32},{64,48},{80,64},{96,80},{112,96},{1... | collective-permute-start | bytes 147464 | tf_op jit(solution)/shard_map/ppermute | solution.py:476
  166.6 1.9 %collective-permute-done.14.lx = bf16[3,64,128]{2,1,0:T(8,128)(2,1)S(1)} collective-permute-done((bf16[3,64,128]{2,1,0:T(8,128)(2,1)S(1)}, bf16[3,64,128]{2,1,0:T(8,128)(2,1)S(1)}, u32[]{:S(2)}, u32[]{:S(2)}) %collective-permute-start.14) | collective-permute-done | bytes 49184 | tf_op jit(solution)/shard_map/ppermute | solution.py:476
  168.5 4.3 %collective-permute-done.15.ux = bf16[3,64,128]{2,1,0:T(8,128)(2,1)S(1)} collective-permute-done((bf16[3,64,128]{2,1,0:T(8,128)(2,1)S(1)}, bf16[3,64,128]{2,1,0:T(8,128)(2,1)S(1)}, u32[]{:S(2)}, u32[]{:S(2)}) %collective-permute-start.15) | collective-permute-done | bytes 49184 | tf_op jit(solution)/shard_map/ppermute | solution.py:476
  (54 shorter events, 26.2 us)
Async XLA Ops:
  0.6 38.0 %copy-start.2 = (f32[2,128]{1,0:T(2,128)S(1)}, f32[2,128]{1,0:T(2,128)}, u32[]{:S(2)}) copy-start(f32[2,128]{1,0:T(2,128)} %param.16) | copy-start | bytes 3076
  1.6 6.0 %collective-permute-start = (bf16[3,64,128]{2,1,0:T(8,128)(2,1)S(1)}, bf16[3,64,128]{2,1,0:T(8,128)(2,1)S(1)}, u32[]{:S(2)}, u32[]{:S(2)}) collective-permute-start(bf16[3,64,128]{2,1,0:T(8,128)(2,1)S(1)} %get-tuple-element.53), channel_id=1, source_target_pairs={{0,1},{1,2},{2,3},{3,4},{4,5},{5,6},{6,7},{7,8},{8,9},{9,10},{10,1... | collective-permute-start | bytes 147464 | tf_op jit(solution)/shard_map/ppermute | solution.py:476
  1.6 5.9 %collective-permute-start.1 = (bf16[3,64,128]{2,1,0:T(8,128)(2,1)S(1)}, bf16[3,64,128]{2,1,0:T(8,128)(2,1)S(1)}, u32[]{:S(2)}, u32[]{:S(2)}) collective-permute-start(bf16[3,64,128]{2,1,0:T(8,128)(2,1)S(1)} %get-tuple-element.54), channel_id=1, source_target_pairs={{0,15},{1,0},{2,1},{3,2},{4,3},{5,4},{6,5},{7,6},{8,7},{9,8},{10,9... | collective-permute-start | bytes 147464 | tf_op jit(solution)/shard_map/ppermute | solution.py:476
  7.6 8.3 %collective-permute-start.2 = (bf16[3,64,128]{2,1,0:T(8,128)(2,1)S(1)}, bf16[3,64,128]{2,1,0:T(8,128)(2,1)S(1)}, u32[]{:S(2)}, u32[]{:S(2)}) collective-permute-start(bf16[3,64,128]{2,1,0:T(8,128)(2,1)S(1)} %get-tuple-element.55), channel_id=1, source_target_pairs={{0,16},{16,32},{32,48},{48,64},{64,80},{80,96},{96,112},{112,0},{1... | collective-permute-start | bytes 147464 | tf_op jit(solution)/shard_map/ppermute | solution.py:476
  9.2 6.6 %collective-permute-start.3 = (bf16[3,64,128]{2,1,0:T(8,128)(2,1)S(1)}, bf16[3,64,128]{2,1,0:T(8,128)(2,1)S(1)}, u32[]{:S(2)}, u32[]{:S(2)}) collective-permute-start(bf16[3,64,128]{2,1,0:T(8,128)(2,1)S(1)} %get-tuple-element.56), channel_id=1, source_target_pairs={{0,112},{16,0},{32,16},{48,32},{64,48},{80,64},{96,80},{112,96},{1... | collective-permute-start | bytes 147464 | tf_op jit(solution)/shard_map/ppermute | solution.py:476
  13.9 48.0 %copy-start = (bf16[4,64,128]{2,1,0:T(8,128)(2,1)S(1)}, bf16[4,64,128]{2,1,0:T(8,128)(2,1)}, u32[]{:S(2)}) copy-start(bf16[4,64,128]{2,1,0:T(8,128)(2,1)} %field.1) | copy-start | bytes 196612
  13.9 48.0 %copy-start.1 = (bf16[4,64,128]{2,1,0:T(8,128)(2,1)S(1)}, bf16[4,64,128]{2,1,0:T(8,128)(2,1)}, u32[]{:S(2)}) copy-start(bf16[4,64,128]{2,1,0:T(8,128)(2,1)} %param.17) | copy-start | bytes 196612
  18.2 23.8 %all-to-all-start = ((f32[128,4,128]{2,1,0:T(4,128)}), f32[128,4,128]{2,1,0:T(4,128)S(1)}, u32[]{:S(2)}, u32[]{:S(2)}) async-start(f32[128,4,128]{2,1,0:T(4,128)} %bitcast.4), calls=%async_computation | async-start | bytes 524288 | tf_op jit(solution)/shard_map/all_to_all | solution.py:480
  27.6 6.8 %collective-permute-start.4 = (f32[3,64,128]{2,1,0:T(8,128)S(1)}, f32[3,64,128]{2,1,0:T(8,128)S(1)}, u32[]{:S(2)}, u32[]{:S(2)}) collective-permute-start(f32[3,64,128]{2,1,0:T(8,128)S(1)} %get-tuple-element.60), channel_id=1, source_target_pairs={{0,1},{1,2},{2,3},{3,4},{4,5},{5,6},{6,7},{7,8},{8,9},{9,10},{10,1... | collective-permute-start | bytes 294920 | tf_op jit(solution)/shard_map/ppermute | solution.py:476
  27.8 6.6 %collective-permute-start.5 = (f32[3,64,128]{2,1,0:T(8,128)S(1)}, f32[3,64,128]{2,1,0:T(8,128)S(1)}, u32[]{:S(2)}, u32[]{:S(2)}) collective-permute-start(f32[3,64,128]{2,1,0:T(8,128)S(1)} %get-tuple-element.61), channel_id=1, source_target_pairs={{0,15},{1,0},{2,1},{3,2},{4,3},{5,4},{6,5},{7,6},{8,7},{9,8},{10,9... | collective-permute-start | bytes 294920 | tf_op jit(solution)/shard_map/ppermute | solution.py:476
  34.5 7.5 %collective-permute-start.6 = (f32[3,64,128]{2,1,0:T(8,128)S(1)}, f32[3,64,128]{2,1,0:T(8,128)S(1)}, u32[]{:S(2)}, u32[]{:S(2)}) collective-permute-start(f32[3,64,128]{2,1,0:T(8,128)S(1)} %get-tuple-element.62), channel_id=1, source_target_pairs={{0,16},{16,32},{32,48},{48,64},{64,80},{80,96},{96,112},{112,0},{1... | collective-permute-start | bytes 294920 | tf_op jit(solution)/shard_map/ppermute | solution.py:476
  35.9 6.1 %collective-permute-start.7 = (f32[3,64,128]{2,1,0:T(8,128)S(1)}, f32[3,64,128]{2,1,0:T(8,128)S(1)}, u32[]{:S(2)}, u32[]{:S(2)}) collective-permute-start(f32[3,64,128]{2,1,0:T(8,128)S(1)} %get-tuple-element.63), channel_id=1, source_target_pairs={{0,112},{16,0},{32,16},{48,32},{64,48},{80,64},{96,80},{112,96},{1... | collective-permute-start | bytes 294920 | tf_op jit(solution)/shard_map/ppermute | solution.py:476
  80.2 23.8 %all-to-all-start.3 = ((f32[128,2,128]{2,1,0:T(2,128)}), f32[128,2,128]{2,1,0:T(2,128)S(1)}, u32[]{:S(2)}, u32[]{:S(2)}) async-start(f32[128,2,128]{2,1,0:T(2,128)} %bitcast.14), calls=%async_computation.3 | async-start | bytes 262144 | tf_op jit(solution)/shard_map/all_to_all | solution.py:480
  86.4 3.5 %collective-permute-start.8 = (bf16[3,64,128]{2,1,0:T(8,128)(2,1)S(1)}, bf16[3,64,128]{2,1,0:T(8,128)(2,1)S(1)}, u32[]{:S(2)}, u32[]{:S(2)}) collective-permute-start(bf16[3,64,128]{2,1,0:T(8,128)(2,1)S(1)} %get-tuple-element.76), channel_id=1, source_target_pairs={{0,15},{1,0},{2,1},{3,2},{4,3},{5,4},{6,5},{7,6},{8,7},{9,8},{10,9... | collective-permute-start | bytes 147464 | tf_op jit(solution)/shard_map/ppermute | solution.py:476
  88.1 5.9 %collective-permute-start.9 = (bf16[3,64,128]{2,1,0:T(8,128)(2,1)S(1)}, bf16[3,64,128]{2,1,0:T(8,128)(2,1)S(1)}, u32[]{:S(2)}, u32[]{:S(2)}) collective-permute-start(bf16[3,64,128]{2,1,0:T(8,128)(2,1)S(1)} %get-tuple-element.77), channel_id=1, source_target_pairs={{0,1},{1,2},{2,3},{3,4},{4,5},{5,6},{6,7},{7,8},{8,9},{9,10},{10,1... | collective-permute-start | bytes 147464 | tf_op jit(solution)/shard_map/ppermute | solution.py:476
  94.1 5.5 %collective-permute-start.10 = (bf16[3,64,128]{2,1,0:T(8,128)(2,1)S(1)}, bf16[3,64,128]{2,1,0:T(8,128)(2,1)S(1)}, u32[]{:S(2)}, u32[]{:S(2)}) collective-permute-start(bf16[3,64,128]{2,1,0:T(8,128)(2,1)S(1)} %get-tuple-element.78), channel_id=1, source_target_pairs={{0,112},{16,0},{32,16},{48,32},{64,48},{80,64},{96,80},{112,96},{1... | collective-permute-start | bytes 147464 | tf_op jit(solution)/shard_map/ppermute | solution.py:476
  97.8 6.2 %collective-permute-start.11 = (bf16[3,64,128]{2,1,0:T(8,128)(2,1)S(1)}, bf16[3,64,128]{2,1,0:T(8,128)(2,1)S(1)}, u32[]{:S(2)}, u32[]{:S(2)}) collective-permute-start(bf16[3,64,128]{2,1,0:T(8,128)(2,1)S(1)} %get-tuple-element.79), channel_id=1, source_target_pairs={{0,16},{16,32},{32,48},{48,64},{64,80},{80,96},{96,112},{112,0},{1... | collective-permute-start | bytes 147464 | tf_op jit(solution)/shard_map/ppermute | solution.py:476
  99.4 9.5 %collective-permute-start.17 = (bf16[32,56,128]{2,1,0:T(8,128)(2,1)S(1)}, bf16[32,56,128]{2,1,0:T(8,128)(2,1)S(1)}, u32[]{:S(2)}, u32[]{:S(2)}) collective-permute-start(bf16[32,56,128]{2,1,0:T(8,128)(2,1)S(1)} %get-tuple-element.96), channel_id=1, source_target_pairs={{0,1},{1,0},{2,3},{3,2},{4,5},{5,4},{6,7},{7,6},{8,9},{9,8},{10,11... | collective-permute-start | bytes 1376264 | tf_op jit(solution)/shard_map/ppermute | solution.py:484
  108.8 1.9 %collective-permute-start.16 = (bf16[32,56,128]{2,1,0:T(8,128)(2,1)S(1)}, bf16[32,56,128]{2,1,0:T(8,128)(2,1)S(1)}, u32[]{:S(2)}, u32[]{:S(2)}) collective-permute-start(bf16[32,56,128]{2,1,0:T(8,128)(2,1)S(1)} %get-tuple-element.92), channel_id=1, source_target_pairs={{0,1},{1,0},{2,3},{3,2},{4,5},{5,4},{6,7},{7,6},{8,9},{9,8},{10,11... | collective-permute-start | bytes 1376264 | tf_op jit(solution)/shard_map/ppermute | solution.py:484
  156.2 19.1 %collective-permute-start.18 = (bf16[64,56,128]{2,1,0:T(8,128)(2,1)S(1)}, bf16[64,56,128]{2,1,0:T(8,128)(2,1)S(1)}, u32[]{:S(2)}, u32[]{:S(2)}) collective-permute-start(bf16[64,56,128]{2,1,0:T(8,128)(2,1)S(1)} %all_to_all.57.half), channel_id=1, source_target_pairs={{0,1},{1,0},{2,3},{3,2},{4,5},{5,4},{6,7},{7,6},{8,9},{9,8},{10,11... | collective-permute-start | bytes 2752520 | tf_op jit(solution)/shard_map/ppermute | solution.py:484
  156.3 3.9 %collective-permute-start.12 = (bf16[3,64,128]{2,1,0:T(8,128)(2,1)S(1)}, bf16[3,64,128]{2,1,0:T(8,128)(2,1)S(1)}, u32[]{:S(2)}, u32[]{:S(2)}) collective-permute-start(bf16[3,64,128]{2,1,0:T(8,128)(2,1)S(1)} %get-tuple-element.83), channel_id=1, source_target_pairs={{0,15},{1,0},{2,1},{3,2},{4,3},{5,4},{6,5},{7,6},{8,7},{9,8},{10,9... | collective-permute-start | bytes 147464 | tf_op jit(solution)/shard_map/ppermute | solution.py:476
  158.4 5.9 %collective-permute-start.13 = (bf16[3,64,128]{2,1,0:T(8,128)(2,1)S(1)}, bf16[3,64,128]{2,1,0:T(8,128)(2,1)S(1)}, u32[]{:S(2)}, u32[]{:S(2)}) collective-permute-start(bf16[3,64,128]{2,1,0:T(8,128)(2,1)S(1)} %get-tuple-element.84), channel_id=1, source_target_pairs={{0,1},{1,2},{2,3},{3,4},{4,5},{5,6},{6,7},{7,8},{8,9},{9,10},{10,1... | collective-permute-start | bytes 147464 | tf_op jit(solution)/shard_map/ppermute | solution.py:476
  164.4 4.2 %collective-permute-start.14 = (bf16[3,64,128]{2,1,0:T(8,128)(2,1)S(1)}, bf16[3,64,128]{2,1,0:T(8,128)(2,1)S(1)}, u32[]{:S(2)}, u32[]{:S(2)}) collective-permute-start(bf16[3,64,128]{2,1,0:T(8,128)(2,1)S(1)} %get-tuple-element.85), channel_id=1, source_target_pairs={{0,112},{16,0},{32,16},{48,32},{64,48},{80,64},{96,80},{112,96},{1... | collective-permute-start | bytes 147464 | tf_op jit(solution)/shard_map/ppermute | solution.py:476
  166.6 6.2 %collective-permute-start.15 = (bf16[3,64,128]{2,1,0:T(8,128)(2,1)S(1)}, bf16[3,64,128]{2,1,0:T(8,128)(2,1)S(1)}, u32[]{:S(2)}, u32[]{:S(2)}) collective-permute-start(bf16[3,64,128]{2,1,0:T(8,128)(2,1)S(1)} %get-tuple-element.86), channel_id=1, source_target_pairs={{0,16},{16,32},{32,48},{48,64},{64,80},{80,96},{96,112},{112,0},{1... | collective-permute-start | bytes 147464 | tf_op jit(solution)/shard_map/ppermute | solution.py:476
  (1 other events, 38.0 us)

commit v7 on v6

--- a/solution.py
+++ b/solution.py
@@ -13,7 +13,8 @@
 GY = ("gy_0", "gy_1", "gy_2")
 GX_GY = ("gx_0", "gx_1", "gy_0", "gy_1", "gy_2")
 CORE = ("gy_2",)
-CHIPS = ("gx_0", "gx_1", "gy_0", "gy_1")
+PLANE = ("gx_1", "gy_0")
+LINE = ("gx_0", "gy_1")
 C = 128
 NB = 4
 ROWS = NB * 64
@@ -398,9 +399,15 @@
     out[32:64] = second[...]
 
 
-def total_kernel(consts, pieces, out):
-    total = jnp.sum(pieces[...].astype(F32), axis=0) / jnp.sqrt(consts[VOXELS])
-    out[...] = jnp.broadcast_to(total.astype(BF16)[None], (64, CHUNK, C))
+def plane_sum_kernel(pieces, out):
+    out[...] = jnp.sum(pieces[...].astype(F32), axis=0).astype(BF16)
+
+
+def total_kernel(consts, own, next_one, opposite, last_one, out):
+    even = own[...].astype(F32) + opposite[...].astype(F32)
+    odd = next_one[...].astype(F32) + last_one[...].astype(F32)
+    total = (even + odd) / jnp.sqrt(consts[VOXELS])
+    out[...] = jnp.broadcast_to(total.astype(BF16)[None], out.shape)
 
 
 def last_kernel(meta, own, lx, ux, ly, uy, dv, consts, grad_in, norm_grads, field):
@@ -613,8 +620,12 @@
     )
     both = ((64, CHUNK, C), BF16)
     (part,) = local(first_sum_kernel, [both], [mine, swap(other), second])
-    (whole,) = local(total_kernel, [both], [consts, exchange(part, CHIPS)])
-    whole = exchange(whole, CHIPS)
+    chunk = (4 * CHUNK, C)
+    part = exchange(part.reshape((16,) + chunk), PLANE)
+    (part,) = local(plane_sum_kernel, [(chunk, BF16)], [part])
+    others = [shifted(part, LINE, by) for by in (1, 2, 3)]
+    (whole,) = local(total_kernel, [((16,) + chunk, BF16)], [consts, part, *others])
+    whole = exchange(whole, PLANE).reshape(64, CHUNK, C)
     partner = swap(whole)
     core = lax.axis_index(CORE).reshape(1)
     weight_grads = widen(core, whole, False, None)

time: 179 us -> 182 us (1.017)
  blocking collectives: 77.4 us -> 71 us
  starting transfers between devices: 42.5 us -> 48.8 us
  waiting for transfers between devices: 30.7 us -> 33.5 us
    all_to_all x4, blocking collectives: 77.4 us -> 71 us  [exchange(): return lax.all_to_all(value, axes, 0, 0, tiled=True)]
    ppermute x16 -> x19, starting transfers between devices: 26.7 us -> 33 us  [shifted(): lax.ppermute(value, axis, [(i, (i + by) % length) for i in range(length)])]
    ppermute x16 -> x19, waiting for transfers between devices: 29 us -> 31.7 us  [shifted(): lax.ppermute(value, axis, [(i, (i + by) % length) for i in range(length)])]
    pallas_call x18 -> x19, Pallas kernels: 19.7 us -> 19.7 us  [local(): pl.pallas_call(kernel, out_shape=[jax.ShapeDtypeStruct(s, d) for s, d in...]
  transfers between devices with their start and end apart: 21 -> 24, of which waited for: 11 -> 13; matrix products, arithmetic and copies ran while one was open for 1% -> 1% of each run, Pallas kernels for 6% -> 6%
where the time goes in v7:
time: 182 us; the launch traced here: 179 us
  blocking collectives  71 us (39%)
  starting transfers between devices  48.8 us (27%)
  waiting for transfers between devices  33.5 us (18%)
  Pallas kernels  22.3 us (12%)
    all_to_all x4, blocking collectives, exchange(): return lax.all_to_all(value, axes, 0, 0, tiled=True)  71 us
    ppermute x19, starting transfers between devices, shifted(): lax.ppermute(value, axis, [(i, (i + by) % length) for i in range(length)])  33 us
    ppermute x19, waiting for transfers between devices, shifted(): lax.ppermute(value, axis, [(i, (i + by) % length) for i in range(length)])  31.7 us
    pallas_call x19, Pallas kernels, local(): pl.pallas_call(kernel, out_shape=[jax.ShapeDtypeStruct(s, d) for s, d in...  19.7 us
    all_to_all x2, starting transfers between devices, exchange(): return lax.all_to_all(value, axes, 0, 0, tiled=True)  15.7 us
  transfers between devices with their start and end apart: 24, of which 13 were waited for; matrix products, arithmetic and copies ran while one was open for 1% of the time, Pallas kernels for 6%

profile of v7, /device:TPU:34, one launch (start us, length us, event | category | flops | bytes accessed | tf_op | source)
XLA Modules:
  0.0 179.4 jit_solution(16877340656495280089)
XLA Ops:
  1.6 4.1 %collective-permute-start.1 = (bf16[3,64,128]{2,1,0:T(8,128)(2,1)S(1)}, bf16[3,64,128]{2,1,0:T(8,128)(2,1)S(1)}, u32[]{:S(2)}, u32[]{:S(2)}) collective-permute-start(bf16[3,64,128]{2,1,0:T(8,128)(2,1)S(1)} %get-tuple-element.54), channel_id=1, source_target_pairs={{0,15},{1,0},{2,1},{3,2},{4,3},{5,4},{6,5},{7,6},{8,7},{9,8},{10,9... | collective-permute-start | bytes 147464 | tf_op jit(solution)/shard_map/ppermute | solution.py:483
  9.2 2.6 %collective-permute-start.3 = (bf16[3,64,128]{2,1,0:T(8,128)(2,1)S(1)}, bf16[3,64,128]{2,1,0:T(8,128)(2,1)S(1)}, u32[]{:S(2)}, u32[]{:S(2)}) collective-permute-start(bf16[3,64,128]{2,1,0:T(8,128)(2,1)S(1)} %get-tuple-element.56), channel_id=1, source_target_pairs={{0,112},{16,0},{32,16},{48,32},{64,48},{80,64},{96,80},{112,96},{1... | collective-permute-start | bytes 147464 | tf_op jit(solution)/shard_map/ppermute | solution.py:483
  15.9 2.3 %shard_map.150 = (f32[4,64,128]{2,1,0:T(8,128)S(1)}, bf16[13,64,128]{2,1,0:T(8,128)(2,1)S(1)}, f32[512,128]{1,0:T(8,128)}, f32[3,64,128]{2,1,0:T(8,128)S(1)}, f3...) custom-call(s32[126]{0:T(128)S(1)} %concatenate.6.meta, bf16[4,64,128]{2,1,0:T(8,128)(2,1)S(1)} %get-tuple-element.51.voxel_feats, ...), custom_call_target="tpu_custom_call" | custom-call | tf_op jit(solution)/shard_map/pallas_call | solution.py:455
  18.2 9.5 %all-to-all-start = ((f32[128,4,128]{2,1,0:T(4,128)}), f32[128,4,128]{2,1,0:T(4,128)S(1)}, u32[]{:S(2)}, u32[]{:S(2)}) async-start(f32[128,4,128]{2,1,0:T(4,128)} %bitcast.4), calls=%async_computation | async-start | bytes 524288 | tf_op jit(solution)/shard_map/all_to_all | solution.py:487
  27.8 4.0 %collective-permute-start.5 = (f32[3,64,128]{2,1,0:T(8,128)S(1)}, f32[3,64,128]{2,1,0:T(8,128)S(1)}, u32[]{:S(2)}, u32[]{:S(2)}) collective-permute-start(f32[3,64,128]{2,1,0:T(8,128)S(1)} %get-tuple-element.61), channel_id=1, source_target_pairs={{0,15},{1,0},{2,1},{3,2},{4,3},{5,4},{6,5},{7,6},{8,7},{9,8},{10,9... | collective-permute-start | bytes 294920 | tf_op jit(solution)/shard_map/ppermute | solution.py:483
  35.9 2.8 %collective-permute-start.7 = (f32[3,64,128]{2,1,0:T(8,128)S(1)}, f32[3,64,128]{2,1,0:T(8,128)S(1)}, u32[]{:S(2)}, u32[]{:S(2)}) collective-permute-start(f32[3,64,128]{2,1,0:T(8,128)S(1)} %get-tuple-element.63), channel_id=1, source_target_pairs={{0,112},{16,0},{32,16},{48,32},{64,48},{80,64},{96,80},{112,96},{1... | collective-permute-start | bytes 294920 | tf_op jit(solution)/shard_map/ppermute | solution.py:483
  38.7 3.3 %collective-permute-done.6.ux = f32[3,64,128]{2,1,0:T(8,128)S(1)} collective-permute-done((f32[3,64,128]{2,1,0:T(8,128)S(1)}, f32[3,64,128]{2,1,0:T(8,128)S(1)}, u32[]{:S(2)}, u32[]{:S(2)}) %collective-permute-start.6) | collective-permute-done | bytes 98336 | tf_op jit(solution)/shard_map/ppermute | solution.py:483
  42.0 1.8 shard_map.153
  43.8 18.0 %all_to_all.54 = f32[128,2,128]{2,1,0:T(2,128)S(1)} all-to-all(f32[128,2,128]{2,1,0:T(2,128)S(1)} %bitcast.28), channel_id=1, replica_groups=mesh['gx_0'=2,'gx_1'=4,'gy_0'=4,'gy_1'=2,'gy_2'=2] {'gx_0','gx_1','gy_0'..., dimensions={0} | all-to-all | bytes 262144 | tf_op jit(solution)/shard_map/all_to_all | solution.py:487
  63.1 14.2 %all_to_all.55 = f32[128,2,128]{2,1,0:T(2,128)S(1)} all-to-all(f32[128,2,128]{2,1,0:T(2,128)S(1)} %bitcast.29), channel_id=1, replica_groups=mesh['gx_0'=2,'gx_1'=4,'gy_0'=4,'gy_1'=2,'gy_2'=2] {'gx_0','gx_1','gy_0'..., dimensions={0} | all-to-all | bytes 262144 | tf_op jit(solution)/shard_map/all_to_all | solution.py:487
  77.3 2.9 %shard_map.155 = (bf16[256,128]{1,0:T(8,128)(2,1)S(1)}, f32[256,128]{1,0:T(8,128)S(1)}, bf16[3,64,128]{2,1,0:T(8,128)(2,1)S(1)}, bf16[3,64,128]{2,1,0:T(8,128)(2...) custom-call(s32[126]{0:T(128)S(1)} %concatenate.6.meta, ...), custom_call_target="tpu_custom_call" | custom-call | tf_op jit(solution)/shard_map/pallas_call | solution.py:455
  80.2 6.2 %all-to-all-start.3 = ((f32[128,2,128]{2,1,0:T(2,128)}), f32[128,2,128]{2,1,0:T(2,128)S(1)}, u32[]{:S(2)}, u32[]{:S(2)}) async-start(f32[128,2,128]{2,1,0:T(2,128)} %bitcast.14), calls=%async_computation.3 | async-start | bytes 262144 | tf_op jit(solution)/shard_map/all_to_all | solution.py:487
  89.9 4.2 %collective-permute-done.9.second.uy = bf16[3,64,128]{2,1,0:T(8,128)(2,1)S(1)} collective-permute-done((bf16[3,64,128]{2,1,0:T(8,128)(2,1)S(1)}, bf16[3,64,128]{2,1,0:T(8,128)(2,1)S(1)}, u32[]{:S(2)}, u32[]{:S(2)}) %collective-permute-start.9) | collective-permute-done | bytes 49184 | tf_op jit(solution)/shard_map/ppermute | solution.py:483
  94.1 3.7 %collective-permute-start.10 = (bf16[3,64,128]{2,1,0:T(8,128)(2,1)S(1)}, bf16[3,64,128]{2,1,0:T(8,128)(2,1)S(1)}, u32[]{:S(2)}, u32[]{:S(2)}) collective-permute-start(bf16[3,64,128]{2,1,0:T(8,128)(2,1)S(1)} %get-tuple-element.78), channel_id=1, source_target_pairs={{0,112},{16,0},{32,16},{48,32},{64,48},{80,64},{96,80},{112,96},{1... | collective-permute-start | bytes 147464 | tf_op jit(solution)/shard_map/ppermute | solution.py:483
  99.5 4.4 %collective-permute-done.11.ux = bf16[3,64,128]{2,1,0:T(8,128)(2,1)S(1)} collective-permute-done((bf16[3,64,128]{2,1,0:T(8,128)(2,1)S(1)}, bf16[3,64,128]{2,1,0:T(8,128)(2,1)S(1)}, u32[]{:S(2)}, u32[]{:S(2)}) %collective-permute-start.11) | collective-permute-done | bytes 49184 | tf_op jit(solution)/shard_map/ppermute | solution.py:483
  104.0 3.2 %shard_map.157 = (bf16[256,128]{1,0:T(8,128)(2,1)S(1)}, f32[256,128]{1,0:T(8,128)S(1)}, bf16[3,64,128]{2,1,0:T(8,128)(2,1)S(1)}, bf16[3,64,128]{2,1,0:T(8,128)(2...) custom-call(s32[126]{0:T(128)S(1)} %concatenate.6.meta, f32[256,128]{1,0:T(8,128)S(1)} %bitcast.24, ...), custom_call_target="tpu_custom_call" | custom-call | tf_op jit(solution)/shard_map/pallas_call | solution.py:455
  110.8 21.6 %all_to_all.56.pieces = bf16[16,224,128]{2,1,0:T(8,128)(2,1)S(1)} all-to-all(bf16[16,224,128]{2,1,0:T(8,128)(2,1)S(1)} %bitcast.22), channel_id=1, replica_groups=mesh['gx_0'=2,'gx_1'=4,'gy_0'=4,'gy_1'=2,'gy_2'=2] {'gx_1','gy_0'}, dimensions={0} | all-to-all | bytes 1835008 | tf_op jit(solution)/shard_map/all_to_all | solution.py:487
  133.4 2.8 %collective-permute-start.18 = (bf16[224,128]{1,0:T(8,128)(2,1)S(1)}, bf16[224,128]{1,0:T(8,128)(2,1)S(1)}, u32[]{:S(2)}, u32[]{:S(2)}) collective-permute-start(bf16[224,128]{1,0:T(8,128)(2,1)S(1)} %shard_map.164.own), channel_id=1, source_target_pairs={{0,2},{2,64},{64,66},{66,0},{1,3},{3,65},{65,67},{67,1},{4,6},{6,6... | collective-permute-start | bytes 172040 | tf_op jit(solution)/shard_map/ppermute | solution.py:483
  136.2 2.1 %collective-permute-done.20.last_one = bf16[224,128]{1,0:T(8,128)(2,1)S(1)} collective-permute-done((bf16[224,128]{1,0:T(8,128)(2,1)S(1)}, bf16[224,128]{1,0:T(8,128)(2,1)S(1)}, u32[]{:S(2)}, u32[]{:S(2)}) %collective-permute-start.20) | collective-permute-done | bytes 57376 | tf_op jit(solution)/shard_map/ppermute | solution.py:483
  139.0 17.2 %all_to_all.57 = bf16[16,224,128]{2,1,0:T(8,128)(2,1)S(1)} all-to-all(bf16[16,224,128]{2,1,0:T(8,128)(2,1)S(1)} %shard_map.165), channel_id=1, replica_groups=mesh['gx_0'=2,'gx_1'=4,'gy_0'=4,'gy_1'=2,'gy_2'=2] {'gx_1','gy_0'}, dimensions={0} | all-to-all | bytes 1835008 | tf_op jit(solution)/shard_map/all_to_all | solution.py:487
  156.2 3.9 %collective-permute-start.12 = (bf16[3,64,128]{2,1,0:T(8,128)(2,1)S(1)}, bf16[3,64,128]{2,1,0:T(8,128)(2,1)S(1)}, u32[]{:S(2)}, u32[]{:S(2)}) collective-permute-start(bf16[3,64,128]{2,1,0:T(8,128)(2,1)S(1)} %get-tuple-element.83), channel_id=1, source_target_pairs={{0,15},{1,0},{2,1},{3,2},{4,3},{5,4},{6,5},{7,6},{8,7},{9,8},{10,9... | collective-permute-start | bytes 147464 | tf_op jit(solution)/shard_map/ppermute | solution.py:483
  161.9 4.2 %collective-permute-done.13.second.uy = bf16[3,64,128]{2,1,0:T(8,128)(2,1)S(1)} collective-permute-done((bf16[3,64,128]{2,1,0:T(8,128)(2,1)S(1)}, bf16[3,64,128]{2,1,0:T(8,128)(2,1)S(1)}, u32[]{:S(2)}, u32[]{:S(2)}) %collective-permute-start.13) | collective-permute-done | bytes 49184 | tf_op jit(solution)/shard_map/ppermute | solution.py:483
  166.1 3.2 %collective-permute-start.14 = (bf16[3,64,128]{2,1,0:T(8,128)(2,1)S(1)}, bf16[3,64,128]{2,1,0:T(8,128)(2,1)S(1)}, u32[]{:S(2)}, u32[]{:S(2)}) collective-permute-start(bf16[3,64,128]{2,1,0:T(8,128)(2,1)S(1)} %get-tuple-element.85), channel_id=1, source_target_pairs={{0,112},{16,0},{32,16},{48,32},{64,48},{80,64},{96,80},{112,96},{1... | collective-permute-start | bytes 147464 | tf_op jit(solution)/shard_map/ppermute | solution.py:483
  171.0 4.4 %collective-permute-done.15.ux = bf16[3,64,128]{2,1,0:T(8,128)(2,1)S(1)} collective-permute-done((bf16[3,64,128]{2,1,0:T(8,128)(2,1)S(1)}, bf16[3,64,128]{2,1,0:T(8,128)(2,1)S(1)}, u32[]{:S(2)}, u32[]{:S(2)}) %collective-permute-start.15) | collective-permute-done | bytes 49184 | tf_op jit(solution)/shard_map/ppermute | solution.py:483
  (61 shorter events, 31.1 us)
Async XLA Ops:
  1.6 6.0 %collective-permute-start = (bf16[3,64,128]{2,1,0:T(8,128)(2,1)S(1)}, bf16[3,64,128]{2,1,0:T(8,128)(2,1)S(1)}, u32[]{:S(2)}, u32[]{:S(2)}) collective-permute-start(bf16[3,64,128]{2,1,0:T(8,128)(2,1)S(1)} %get-tuple-element.53), channel_id=1, source_target_pairs={{0,1},{1,2},{2,3},{3,4},{4,5},{5,6},{6,7},{7,8},{8,9},{9,10},{10,1... | collective-permute-start | bytes 147464 | tf_op jit(solution)/shard_map/ppermute | solution.py:483
  1.6 5.9 %collective-permute-start.1 = (bf16[3,64,128]{2,1,0:T(8,128)(2,1)S(1)}, bf16[3,64,128]{2,1,0:T(8,128)(2,1)S(1)}, u32[]{:S(2)}, u32[]{:S(2)}) collective-permute-start(bf16[3,64,128]{2,1,0:T(8,128)(2,1)S(1)} %get-tuple-element.54), channel_id=1, source_target_pairs={{0,15},{1,0},{2,1},{3,2},{4,3},{5,4},{6,5},{7,6},{8,7},{9,8},{10,9... | collective-permute-start | bytes 147464 | tf_op jit(solution)/shard_map/ppermute | solution.py:483
  7.6 8.3 %collective-permute-start.2 = (bf16[3,64,128]{2,1,0:T(8,128)(2,1)S(1)}, bf16[3,64,128]{2,1,0:T(8,128)(2,1)S(1)}, u32[]{:S(2)}, u32[]{:S(2)}) collective-permute-start(bf16[3,64,128]{2,1,0:T(8,128)(2,1)S(1)} %get-tuple-element.55), channel_id=1, source_target_pairs={{0,16},{16,32},{32,48},{48,64},{64,80},{80,96},{96,112},{112,0},{1... | collective-permute-start | bytes 147464 | tf_op jit(solution)/shard_map/ppermute | solution.py:483
  9.2 6.6 %collective-permute-start.3 = (bf16[3,64,128]{2,1,0:T(8,128)(2,1)S(1)}, bf16[3,64,128]{2,1,0:T(8,128)(2,1)S(1)}, u32[]{:S(2)}, u32[]{:S(2)}) collective-permute-start(bf16[3,64,128]{2,1,0:T(8,128)(2,1)S(1)} %get-tuple-element.56), channel_id=1, source_target_pairs={{0,112},{16,0},{32,16},{48,32},{64,48},{80,64},{96,80},{112,96},{1... | collective-permute-start | bytes 147464 | tf_op jit(solution)/shard_map/ppermute | solution.py:483
  18.2 23.8 %all-to-all-start = ((f32[128,4,128]{2,1,0:T(4,128)}), f32[128,4,128]{2,1,0:T(4,128)S(1)}, u32[]{:S(2)}, u32[]{:S(2)}) async-start(f32[128,4,128]{2,1,0:T(4,128)} %bitcast.4), calls=%async_computation | async-start | bytes 524288 | tf_op jit(solution)/shard_map/all_to_all | solution.py:487
  27.6 6.8 %collective-permute-start.4 = (f32[3,64,128]{2,1,0:T(8,128)S(1)}, f32[3,64,128]{2,1,0:T(8,128)S(1)}, u32[]{:S(2)}, u32[]{:S(2)}) collective-permute-start(f32[3,64,128]{2,1,0:T(8,128)S(1)} %get-tuple-element.60), channel_id=1, source_target_pairs={{0,1},{1,2},{2,3},{3,4},{4,5},{5,6},{6,7},{7,8},{8,9},{9,10},{10,1... | collective-permute-start | bytes 294920 | tf_op jit(solution)/shard_map/ppermute | solution.py:483
  27.8 6.6 %collective-permute-start.5 = (f32[3,64,128]{2,1,0:T(8,128)S(1)}, f32[3,64,128]{2,1,0:T(8,128)S(1)}, u32[]{:S(2)}, u32[]{:S(2)}) collective-permute-start(f32[3,64,128]{2,1,0:T(8,128)S(1)} %get-tuple-element.61), channel_id=1, source_target_pairs={{0,15},{1,0},{2,1},{3,2},{4,3},{5,4},{6,5},{7,6},{8,7},{9,8},{10,9... | collective-permute-start | bytes 294920 | tf_op jit(solution)/shard_map/ppermute | solution.py:483
  34.5 7.5 %collective-permute-start.6 = (f32[3,64,128]{2,1,0:T(8,128)S(1)}, f32[3,64,128]{2,1,0:T(8,128)S(1)}, u32[]{:S(2)}, u32[]{:S(2)}) collective-permute-start(f32[3,64,128]{2,1,0:T(8,128)S(1)} %get-tuple-element.62), channel_id=1, source_target_pairs={{0,16},{16,32},{32,48},{48,64},{64,80},{80,96},{96,112},{112,0},{1... | collective-permute-start | bytes 294920 | tf_op jit(solution)/shard_map/ppermute | solution.py:483
  35.9 6.1 %collective-permute-start.7 = (f32[3,64,128]{2,1,0:T(8,128)S(1)}, f32[3,64,128]{2,1,0:T(8,128)S(1)}, u32[]{:S(2)}, u32[]{:S(2)}) collective-permute-start(f32[3,64,128]{2,1,0:T(8,128)S(1)} %get-tuple-element.63), channel_id=1, source_target_pairs={{0,112},{16,0},{32,16},{48,32},{64,48},{80,64},{96,80},{112,96},{1... | collective-permute-start | bytes 294920 | tf_op jit(solution)/shard_map/ppermute | solution.py:483
  80.2 23.8 %all-to-all-start.3 = ((f32[128,2,128]{2,1,0:T(2,128)}), f32[128,2,128]{2,1,0:T(2,128)S(1)}, u32[]{:S(2)}, u32[]{:S(2)}) async-start(f32[128,2,128]{2,1,0:T(2,128)} %bitcast.14), calls=%async_computation.3 | async-start | bytes 262144 | tf_op jit(solution)/shard_map/all_to_all | solution.py:487
  86.4 3.5 %collective-permute-start.8 = (bf16[3,64,128]{2,1,0:T(8,128)(2,1)S(1)}, bf16[3,64,128]{2,1,0:T(8,128)(2,1)S(1)}, u32[]{:S(2)}, u32[]{:S(2)}) collective-permute-start(bf16[3,64,128]{2,1,0:T(8,128)(2,1)S(1)} %get-tuple-element.76), channel_id=1, source_target_pairs={{0,15},{1,0},{2,1},{3,2},{4,3},{5,4},{6,5},{7,6},{8,7},{9,8},{10,9... | collective-permute-start | bytes 147464 | tf_op jit(solution)/shard_map/ppermute | solution.py:483
  88.1 5.9 %collective-permute-start.9 = (bf16[3,64,128]{2,1,0:T(8,128)(2,1)S(1)}, bf16[3,64,128]{2,1,0:T(8,128)(2,1)S(1)}, u32[]{:S(2)}, u32[]{:S(2)}) collective-permute-start(bf16[3,64,128]{2,1,0:T(8,128)(2,1)S(1)} %get-tuple-element.77), channel_id=1, source_target_pairs={{0,1},{1,2},{2,3},{3,4},{4,5},{5,6},{6,7},{7,8},{8,9},{9,10},{10,1... | collective-permute-start | bytes 147464 | tf_op jit(solution)/shard_map/ppermute | solution.py:483
  94.1 5.5 %collective-permute-start.10 = (bf16[3,64,128]{2,1,0:T(8,128)(2,1)S(1)}, bf16[3,64,128]{2,1,0:T(8,128)(2,1)S(1)}, u32[]{:S(2)}, u32[]{:S(2)}) collective-permute-start(bf16[3,64,128]{2,1,0:T(8,128)(2,1)S(1)} %get-tuple-element.78), channel_id=1, source_target_pairs={{0,112},{16,0},{32,16},{48,32},{64,48},{80,64},{96,80},{112,96},{1... | collective-permute-start | bytes 147464 | tf_op jit(solution)/shard_map/ppermute | solution.py:483
  97.8 6.2 %collective-permute-start.11 = (bf16[3,64,128]{2,1,0:T(8,128)(2,1)S(1)}, bf16[3,64,128]{2,1,0:T(8,128)(2,1)S(1)}, u32[]{:S(2)}, u32[]{:S(2)}) collective-permute-start(bf16[3,64,128]{2,1,0:T(8,128)(2,1)S(1)} %get-tuple-element.79), channel_id=1, source_target_pairs={{0,16},{16,32},{32,48},{48,64},{64,80},{80,96},{96,112},{112,0},{1... | collective-permute-start | bytes 147464 | tf_op jit(solution)/shard_map/ppermute | solution.py:483
  99.4 9.5 %collective-permute-start.17 = (bf16[32,56,128]{2,1,0:T(8,128)(2,1)S(1)}, bf16[32,56,128]{2,1,0:T(8,128)(2,1)S(1)}, u32[]{:S(2)}, u32[]{:S(2)}) collective-permute-start(bf16[32,56,128]{2,1,0:T(8,128)(2,1)S(1)} %get-tuple-element.96), channel_id=1, source_target_pairs={{0,1},{1,0},{2,3},{3,2},{4,5},{5,4},{6,7},{7,6},{8,9},{9,8},{10,11... | collective-permute-start | bytes 1376264 | tf_op jit(solution)/shard_map/ppermute | solution.py:491
  108.8 1.9 %collective-permute-start.16 = (bf16[32,56,128]{2,1,0:T(8,128)(2,1)S(1)}, bf16[32,56,128]{2,1,0:T(8,128)(2,1)S(1)}, u32[]{:S(2)}, u32[]{:S(2)}) collective-permute-start(bf16[32,56,128]{2,1,0:T(8,128)(2,1)S(1)} %get-tuple-element.92), channel_id=1, source_target_pairs={{0,1},{1,0},{2,3},{3,2},{4,5},{5,4},{6,7},{7,6},{8,9},{9,8},{10,11... | collective-permute-start | bytes 1376264 | tf_op jit(solution)/shard_map/ppermute | solution.py:491
  132.6 5.8 %collective-permute-start.20 = (bf16[224,128]{1,0:T(8,128)(2,1)S(1)}, bf16[224,128]{1,0:T(8,128)(2,1)S(1)}, u32[]{:S(2)}, u32[]{:S(2)}) collective-permute-start(bf16[224,128]{1,0:T(8,128)(2,1)S(1)} %shard_map.164.own), channel_id=1, source_target_pairs={{0,66},{2,0},{64,2},{66,64},{1,67},{3,1},{65,3},{67,65},{4,70},{6,... | collective-permute-start | bytes 172040 | tf_op jit(solution)/shard_map/ppermute | solution.py:483
  132.7 5.7 %collective-permute-start.19 = (bf16[224,128]{1,0:T(8,128)(2,1)S(1)}, bf16[224,128]{1,0:T(8,128)(2,1)S(1)}, u32[]{:S(2)}, u32[]{:S(2)}) collective-permute-start(bf16[224,128]{1,0:T(8,128)(2,1)S(1)} %shard_map.164.own), channel_id=1, source_target_pairs={{0,64},{2,66},{64,0},{66,2},{1,65},{3,67},{65,1},{67,3},{4,68},{6,... | collective-permute-start | bytes 172040 | tf_op jit(solution)/shard_map/ppermute | solution.py:483
  133.4 5.6 %collective-permute-start.18 = (bf16[224,128]{1,0:T(8,128)(2,1)S(1)}, bf16[224,128]{1,0:T(8,128)(2,1)S(1)}, u32[]{:S(2)}, u32[]{:S(2)}) collective-permute-start(bf16[224,128]{1,0:T(8,128)(2,1)S(1)} %shard_map.164.own), channel_id=1, source_target_pairs={{0,2},{2,64},{64,66},{66,0},{1,3},{3,65},{65,67},{67,1},{4,6},{6,6... | collective-permute-start | bytes 172040 | tf_op jit(solution)/shard_map/ppermute | solution.py:483
  156.2 21.7 %collective-permute-start.21 = (bf16[64,56,128]{2,1,0:T(8,128)(2,1)S(1)}, bf16[64,56,128]{2,1,0:T(8,128)(2,1)S(1)}, u32[]{:S(2)}, u32[]{:S(2)}) collective-permute-start(bf16[64,56,128]{2,1,0:T(8,128)(2,1)S(1)} %bitcast.20), channel_id=1, source_target_pairs={{0,1},{1,0},{2,3},{3,2},{4,5},{5,4},{6,7},{7,6},{8,9},{9,8},{10,11... | collective-permute-start | bytes 2752520 | tf_op jit(solution)/shard_map/ppermute | solution.py:491
  156.2 5.7 %collective-permute-start.12 = (bf16[3,64,128]{2,1,0:T(8,128)(2,1)S(1)}, bf16[3,64,128]{2,1,0:T(8,128)(2,1)S(1)}, u32[]{:S(2)}, u32[]{:S(2)}) collective-permute-start(bf16[3,64,128]{2,1,0:T(8,128)(2,1)S(1)} %get-tuple-element.83), channel_id=1, source_target_pairs={{0,15},{1,0},{2,1},{3,2},{4,3},{5,4},{6,5},{7,6},{8,7},{9,8},{10,9... | collective-permute-start | bytes 147464 | tf_op jit(solution)/shard_map/ppermute | solution.py:483
  160.2 5.9 %collective-permute-start.13 = (bf16[3,64,128]{2,1,0:T(8,128)(2,1)S(1)}, bf16[3,64,128]{2,1,0:T(8,128)(2,1)S(1)}, u32[]{:S(2)}, u32[]{:S(2)}) collective-permute-start(bf16[3,64,128]{2,1,0:T(8,128)(2,1)S(1)} %get-tuple-element.84), channel_id=1, source_target_pairs={{0,1},{1,2},{2,3},{3,4},{4,5},{5,6},{6,7},{7,8},{8,9},{9,10},{10,1... | collective-permute-start | bytes 147464 | tf_op jit(solution)/shard_map/ppermute | solution.py:483
  166.1 4.9 %collective-permute-start.14 = (bf16[3,64,128]{2,1,0:T(8,128)(2,1)S(1)}, bf16[3,64,128]{2,1,0:T(8,128)(2,1)S(1)}, u32[]{:S(2)}, u32[]{:S(2)}) collective-permute-start(bf16[3,64,128]{2,1,0:T(8,128)(2,1)S(1)} %get-tuple-element.85), channel_id=1, source_target_pairs={{0,112},{16,0},{32,16},{48,32},{64,48},{80,64},{96,80},{112,96},{1... | collective-permute-start | bytes 147464 | tf_op jit(solution)/shard_map/ppermute | solution.py:483
  169.2 6.2 %collective-permute-start.15 = (bf16[3,64,128]{2,1,0:T(8,128)(2,1)S(1)}, bf16[3,64,128]{2,1,0:T(8,128)(2,1)S(1)}, u32[]{:S(2)}, u32[]{:S(2)}) collective-permute-start(bf16[3,64,128]{2,1,0:T(8,128)(2,1)S(1)} %get-tuple-element.86), channel_id=1, source_target_pairs={{0,16},{16,32},{32,48},{48,64},{64,80},{80,96},{96,112},{112,0},{1... | collective-permute-start | bytes 147464 | tf_op jit(solution)/shard_map/ppermute | solution.py:483
  (4 other events, 172.0 us)
